TPU v7x, 256 devices: a whole 4x4x8 slice. The times are simulated.
256 devices in a mesh: tm: 4 (over x), pix: 64 (over y, z, core).
Axes of the slice: x: 4, y: 4, z: 8, core: 2. Of those that a mesh axis runs over, the one named last changes fastest.
Arguments:
- latent: float32 [16, 256, 448], P(None, 'pix'), may hold values from -6 to 6
- step_size: float32 [8], P('tm'), may hold values from 0.05 to 0.2
- time_embed: float32 [8, 128], P('tm'), may hold values from -6 to 6
- conv_in: bfloat16 [3, 3, 128, 16], replicated, may hold values from -0.5 to 0.5
- conv_mid: bfloat16 [3, 3, 128, 128], replicated, may hold values from -0.1875 to 0.1875
- conv_out: bfloat16 [3, 3, 16, 128], replicated, may hold values from -0.1875 to 0.1875
Outputs:
- trajectory: float32 [8, 16, 256, 448], P('tm', None, 'pix')
All inputs are finite; a program needn't handle non-finite values.
Results may differ from a plain program's by a relative error of at most 0.00075.
Values may be sent and summed in bfloat16 or wider, within the bound.
No kernel may reach another device: no remote copies, remote signals or barrier semaphores. Data moves between devices by JAX's collectives and lax.ppermute only.
A program may use at most 64 MiB of HBM per device.

v0:
```python
import functools

import jax
import jax.numpy as jnp
from jax import lax
from jax.experimental import pallas as pl
from jax.experimental.pallas import tpu as pltpu
from jax.sharding import PartitionSpec as P

TIMES = 8
C = 16
F = 128
L = 128
ROWS = 4
STARTS = (-1, 105, 215, 321)
CUTS = (114, 224, 334)
BF = jnp.bfloat16
F32 = jnp.float32


def prepare_body(conv_mid, conv_out, w_mid, w_out):
    w_mid[...] = jnp.zeros_like(w_mid)
    w_out[...] = jnp.zeros_like(w_out)
    for a in range(3):
        for b in range(3):
            mid = conv_mid[a, b] * 0.5
            tail = conv_out[a, b]
            for q in range(2):
                w_mid[q * F:(q + 1) * F, ((a + q) * 3 + b) * F:((a + q) * 3 + b + 1) * F] = mid
                w_out[q * 48 + b * C:q * 48 + (b + 1) * C, (a + q) * F:(a + q + 1) * F] = tail


VM = pl.BlockSpec(memory_space=pltpu.VMEM)
SM = pl.BlockSpec(memory_space=pltpu.SMEM)


def prepare(conv_mid, conv_out):
    return pl.pallas_call(
        prepare_body,
        out_shape=(jax.ShapeDtypeStruct((3 * F, 12 * F), BF), jax.ShapeDtypeStruct((96, 4 * F), BF)),
        in_specs=[VM, VM],
        out_specs=(VM, VM),
        name="prepare",
    )(conv_mid, conv_out)


def silu2(v):
    return v + v * jnp.tanh(v)


def round_body(rounds, place, step, lat, prior, from_a, from_b, w_in, w_mid, w_out, *rest):
    pix, tm = place[0], place[1]
    core = pix % 2
    last = rounds == 2
    if last:
        out, *rest = rest
        low, hid, sec = rest[:2], rest[2:10], rest[10:16]
    else:
        nxt, to_a, to_b, *rest = rest
        low, hid, sec = rest[:2], rest[2:10], rest[10:16]
    groups = [(t0, min(4, TIMES - t0)) for t0 in (rounds, rounds + 4)]

    lane = lax.broadcasted_iota(jnp.int32, (C, L), 1)
    column = jnp.where(((tm == 0) & (lane == 0)) | ((tm == 3) & (lane == L - 1)), 0.0, 1.0)

    def state(t, row):
        return lat[row] if rounds == 0 else prior[t, row]

    def spread(x):
        x = x * column
        return jnp.concatenate([pltpu.roll(x, 1, 1) * column, x, pltpu.roll(x, L - 1, 1) * column], axis=0).astype(BF)

    def fill(g):
        t0, n = groups[g]
        for w in range(10):
            for i in range(n if rounds else 1):
                if 3 <= w < 7:
                    x = state(t0 + i, w - 3)
                else:
                    d = w if w < 3 else w - 7
                    at = (t0 + i - rounds, d) if rounds else (d,)
                    a, b = from_a[at].astype(F32), from_b[at].astype(F32)
                    x = jnp.where((core == 0) == (w < 3), b, a)
                x = spread(x)
                for lanes in ([i] if rounds else range(n)):
                    low[g][w * 48:(w + 1) * 48, lanes * L:(lanes + 1) * L] = x

    def weights(ref, top_inside, bottom_inside):
        top = 0 if top_inside is None else pl.multiple_of(jnp.where(top_inside, 0, 2 * F), F)
        bottom = F if bottom_inside is None else pl.multiple_of(jnp.where(bottom_inside, F, 2 * F), F)
        return jnp.concatenate([ref[pl.ds(top, F), :], ref[pl.ds(bottom, F), :]], axis=0)

    above, below = pix > 0, pix < 63

    def hidden_pair(g, p):
        t0, n = groups[g]
        width = n * L
        r = lax.broadcasted_iota(jnp.int32, (64, width), 0)
        c = lax.broadcasted_iota(jnp.int32, (64, width), 1)
        edge = ((tm == 0) & ((c & 127) == 0)) | ((tm == 3) & ((c & 127) == L - 1))
        pick = jnp.where(((r & 7) == t0 + (c >> 7)) & (r < 24) & jnp.logical_not(edge), 1.0, 0.0).astype(BF)
        rhs = jnp.concatenate([low[g][2 * p * 48:2 * p * 48 + 192, :width], pick], axis=0)
        inside = above if p == 0 else below if p == 3 else None
        v = silu2(jnp.dot(weights(w_in, inside, inside), rhs, preferred_element_type=F32))
        to = hid[g * 4 + p]
        for i in range(n):
            for q in range(2):
                x = v[q * F:(q + 1) * F, i * L:(i + 1) * L]
                at = q * 384
                to[at:at + F, i * L:(i + 1) * L] = pltpu.roll(x, 1, 1).astype(BF)
                to[at + F:at + 2 * F, i * L:(i + 1) * L] = x.astype(BF)
                to[at + 2 * F:at + 3 * F, i * L:(i + 1) * L] = pltpu.roll(x, L - 1, 1).astype(BF)

    def second_pair(g, p):
        width = groups[g][1] * L
        rhs = jnp.concatenate([hid[g * 4 + p][:, :width], hid[g * 4 + p + 1][:, :width]], axis=0)
        w = weights(w_mid, above if p == 0 else None, below if p == 2 else None)
        sec[g * 3 + p][:, :width] = silu2(jnp.dot(w, rhs, preferred_element_type=F32)).astype(BF)

    totals = [jnp.zeros((C, L), F32) if rounds == 0 else prior[0, row] for row in range(ROWS)]

    def out_pair(g, p):
        t0, n = groups[g]
        width = n * L
        rhs = jnp.concatenate([sec[g * 3 + p][:, :width], sec[g * 3 + p + 1][:, :width]], axis=0)
        y = jnp.dot(w_out[...], rhs, preferred_element_type=F32)
        for q in range(2):
            row = 2 * p + q
            for i in range(n):
                t = t0 + i
                part = y[q * 48:(q + 1) * 48, i * L:(i + 1) * L]
                conv = pltpu.roll(part[:C] * column, 1, 1) + part[C:2 * C] + pltpu.roll(part[2 * C:] * column, L - 1, 1)
                totals[row] = totals[row] + step[t] * (state(t, row) + conv)
                value = lat[row] + totals[row]
                if last:
                    out[(t // 2) ^ tm, t % 2, row] = value
                else:
                    nxt[t + 1, row] = value
                    if t == rounds:
                        nxt[0, row] = totals[row]

    fill(0)
    for p in range(4):
        hidden_pair(0, p)
    fill(1)
    second_pair(0, 0)
    hidden_pair(1, 0)
    second_pair(0, 1)
    hidden_pair(1, 1)
    second_pair(0, 2)
    hidden_pair(1, 2)
    out_pair(0, 0)
    hidden_pair(1, 3)
    out_pair(0, 1)
    for p in range(3):
        second_pair(1, p)
    for p in range(2):
        out_pair(1, p)

    for row in range(ROWS):
        if rounds == 1:
            nxt[1, row] = prior[1, row]
        if last:
            for t in range(2):
                out[(t // 2) ^ tm, t % 2, row] = prior[t + 1, row]
    if not last:
        for t in range(rounds + 1, TIMES):
            for d in range(3):
                to_a[t - rounds - 1, d] = nxt[t, d + 1 - core].astype(BF)
                to_b[t - rounds - 1, d] = nxt[t, d + core].astype(BF)


def run_round(rounds, place, step, lat, prior, from_a, from_b, w_in, w_mid, w_out):
    if rounds == 2:
        out_shape = jax.ShapeDtypeStruct((4, 2, ROWS, C, L), F32)
        out_specs = VM
    else:
        sent = jax.ShapeDtypeStruct((TIMES - 1 - rounds, 3, C, L), BF)
        out_shape = (jax.ShapeDtypeStruct((TIMES + 1, ROWS, C, L), F32), sent, sent)
        out_specs = (VM, VM, VM)
    return pl.pallas_call(
        functools.partial(round_body, rounds),
        out_shape=out_shape,
        in_specs=[SM, SM] + [VM] * 7,
        out_specs=out_specs,
        scratch_shapes=[pltpu.VMEM((480, 4 * L), BF)] * 2 + [pltpu.VMEM((768, 4 * L), BF)] * 8 + [pltpu.VMEM((2 * F, 4 * L), BF)] * 6,
        compiler_params=pltpu.CompilerParams(vmem_limit_bytes=40 << 20),
        name="round%d" % rounds,
    )(place, step, lat, prior, from_a, from_b, w_in, w_mid, w_out)


def join_body(place, p0, p1, p2, p3, out):
    tm = place[1]
    pieces = [p0[...], p1[...], p2[...], p3[...]]
    lane = lax.broadcasted_iota(jnp.int32, pieces[0].shape, 1)
    placed = []
    for t in range(4):
        k = t ^ tm
        x = jnp.where(k == 0, pieces[0], jnp.where(k == 1, pieces[1], jnp.where(k == 2, pieces[2], pieces[3])))
        placed.append(pltpu.roll(x, STARTS[t] % L, 1) if STARTS[t] % L else x)
    for g in range(3):
        out[:, g * L:(g + 1) * L] = jnp.where(lane < CUTS[g] - g * L, placed[g], placed[g + 1])
    out[:, 3 * L:] = placed[3][:, :448 - 3 * L]


def join(place, pieces):
    return pl.pallas_call(
        join_body,
        out_shape=jax.ShapeDtypeStruct((128, 448), F32),
        in_specs=[SM] + [VM] * 4,
        out_specs=VM,
        name="join",
    )(place, *pieces)


def across(x, k):
    return lax.ppermute(x, "tm", [(t, t ^ k) for t in range(4)])


def pair_up(x, pairs):
    return lax.ppermute(x, "pix", [(a, b) for a, b in pairs] + [(b, a) for a, b in pairs])


CORES = [(2 * k, 2 * k + 1) for k in range(32)]
CHIPS = [(2 * k + 1, 2 * k + 2) for k in range(31)]


def shards(latent, step_size, time_embed, conv_in, conv_mid, conv_out):
    tm, pix = lax.axis_index("tm"), lax.axis_index("pix")
    core = pix % 2
    start = jnp.where(tm == 0, STARTS[0], jnp.where(tm == 1, STARTS[1], jnp.where(tm == 2, STARTS[2], STARTS[3])))
    padded = jnp.pad(latent, ((0, 0), (0, 0), (1, 1)))
    lat = lax.dynamic_slice(padded, (0, 0, start + 1), (C, ROWS, L)).transpose(1, 0, 2)
    place = jnp.stack([pix, tm]).astype(jnp.int32)

    rounded = lat.astype(BF)
    to_a = jnp.where(core == 0, rounded[1:], rounded[:3])
    to_b = jnp.where(core == 0, rounded[:3], rounded[1:])
    from_b, from_a = pair_up(to_b, CHIPS), pair_up(to_a, CORES)

    small = jnp.concatenate([time_embed, jnp.broadcast_to(step_size[:, None], (2, F))])
    parts = jnp.stack([small] + [across(small, k) for k in (1, 2, 3)])
    every = jnp.concatenate([lax.dynamic_index_in_dim(parts, t ^ tm, 0, keepdims=False)[None] for t in range(4)])
    embed = every[:, :2].reshape(TIMES, F) * 0.5
    step = every[:, 2:, 0].reshape(TIMES)

    hi = lax.reduce_precision(embed, 8, 7)
    rest = embed - hi
    mid = lax.reduce_precision(rest, 8, 7)
    te = jnp.concatenate([hi, mid, rest - mid]).T.astype(BF)
    flat = (conv_in * 0.5).transpose(2, 0, 1, 3).reshape(F, 144)
    wide = jnp.concatenate([jnp.pad(flat, ((0, 0), (0, 48))), jnp.pad(flat, ((0, 0), (48, 0)))])
    w_in = jnp.concatenate([wide, jnp.pad(jnp.concatenate([te, te]), ((0, 0), (0, 40)))], axis=1)
    w_in = jnp.pad(w_in, ((0, F), (0, 0)))
    w_mid, w_out = prepare(conv_mid, conv_out)

    prior = lat
    for rounds in range(2):
        prior, to_a, to_b = run_round(rounds, place, step, lat, prior, from_a, from_b, w_in, w_mid, w_out)
        from_b, from_a = pair_up(to_b, CHIPS), pair_up(to_a, CORES)
    pieces = run_round(2, place, step, lat, prior, from_a, from_b, w_in, w_mid, w_out).reshape(4, 128, L)
    got = [pieces[0]] + [across(pieces[k], k) for k in (1, 2, 3)]
    return join(place, got).reshape(2, 4, C, 448).transpose(0, 2, 1, 3)


def solution(mesh):
    in_specs = (P(None, "pix", None), P("tm"), P("tm", None), P(), P(), P())
    out_specs = P("tm", None, "pix", None)
    return jax.shard_map(shards, mesh=mesh, in_specs=in_specs, out_specs=out_specs, check_vma=False)
```

profile of v0, /device:TPU:24, one launch (start us, length us, event | category | flops | bytes accessed | tf_op | source)
XLA Modules:
  0.0 61.9 jit_solution(5544868449270804803)
XLA Ops:
  0.0 0.7 %pad.42.clone = f32[4]{0:T(128)S(1)} pad(f32[2]{0:T(128)} %param.7, f32[]{:T(128)} %constant.73), padding=2_0 | pad | bytes 28 | tf_op jit(solution)/shard_map/concatenate | solution.py:241
  0.7 0.7 %fusion.11 = (f32[1,4,128]{2,1,0:T(4,128)S(1)}, f32[4,128]{1,0:T(4,128)S(1)}) fusion(f32[4]{0:T(128)S(1)} %pad.42.clone, f32[2,128]{1,0:T(2,128)} %param.8), kind=kLoop, calls=%fused_computation.36 | loop fusion | flops 512 | bytes 5136 | tf_op jit(solution)/shard_map/stack | solution.py:242
  1.5 3.0 %collective-permute-start.1 = (f32[4,128]{1,0:T(4,128)S(1)}, f32[4,128]{1,0:T(4,128)S(1)}, u32[]{:S(2)}, u32[]{:S(2)}) collective-permute-start(f32[4,128]{1,0:T(4,128)S(1)} %get-tuple-element.37), channel_id=1, source_target_pairs={{0,128},{64,192},{128,0},{192,64},{1,129},{65,193},{129,1},{193,65... | collective-permute-start | bytes 6152 | tf_op jit(solution)/shard_map/ppermute | solution.py:217
  4.5 0.6 collective-permute-start
  5.1 0.6 collective-permute-start.2
  5.6 0.9 %copy.17 = f32[16,4,448]{2,0,1:T(8,128)S(1)} copy(f32[16,4,448]{2,1,0:T(4,128)} %param.6) | data formatting | bytes 229376 | tf_op args[0]
  6.6 0.1 fusion.12
  6.7 6.8 %collective-permute-start.4 = (bf16[3,16,128]{2,1,0:T(8,128)(2,1)S(1)}, bf16[3,16,128]{2,1,0:T(8,128)(2,1)S(1)}, u32[]{:S(2)}, u32[]{:S(2)}) collective-permute-start(bf16[3,16,128]{2,1,0:T(8,128)(2,1)S(1)} %get-tuple-element.27), channel_id=1, source_target_pairs={{1,2},{3,4},{5,6},{7,8},{9,10},{11,12},{13,14},{15,16},{17,18},{19... | collective-permute-start | bytes 36872 | tf_op jit(solution)/shard_map/ppermute | solution.py:221
  13.5 0.1 collective-permute-start.3
  13.6 0.8 %broadcast_multiply_fusion = bf16[3,3,128,16]{2,3,1,0:T(8,128)(2,1)S(1)} fusion(bf16[3,3,128,16]{2,3,1,0:T(8,128)(2,1)} %param.9), kind=kLoop, calls=%fused_computation.16 | loop fusion | flops 18432 | bytes 73728 | tf_op jit(solution)/shard_map/mul | solution.py:251
  14.4 0.1 pad_add_fusion.place
  14.5 0.0 copy-start.2
  14.5 0.1 copy.18
  14.6 2.2 %prepare.1 = (bf16[384,1536]{1,0:T(8,128)(2,1)}, bf16[96,512]{1,0:T(8,128)(2,1)}) custom-call(bf16[3,3,128,128]{3,2,1,0:T(8,128)(2,1)} %conv_mid.1, bf16[3,3,16,128]{3,2,1,0:T(8,128)(2,1)} %conv_out.1), custom_call_target="tpu_custom_call" | custom-call | tf_op jit(solution)/shard_map/prepare/pallas_call | solution.py:38
  16.8 0.0 collective-permute-done.1
  16.8 0.0 collective-permute-done
  16.8 0.0 collective-permute-done.2
  16.9 0.1 copy.20
  17.1 0.1 fusion.7
  17.2 0.1 slice_reduce_fusion
  17.3 0.1 reshape_squeeze.3.step
  17.4 0.0 collective-permute-done.4.from_b
  17.4 0.0 collective-permute-done.3.from_a
  17.4 0.0 copy-start
  17.4 1.3 %copy-done = bf16[384,1536]{1,0:T(8,128)(2,1)S(1)} copy-done((bf16[384,1536]{1,0:T(8,128)(2,1)S(1)}, bf16[384,1536]{1,0:T(8,128)(2,1)}, u32[]{:S(2)}) %copy-start) | copy-done | bytes 1179672
  18.7 0.0 copy-start.1
  18.7 0.9 %copy-done.1 = bf16[96,512]{1,0:T(8,128)(2,1)S(1)} copy-done((bf16[96,512]{1,0:T(8,128)(2,1)S(1)}, bf16[96,512]{1,0:T(8,128)(2,1)}, u32[]{:S(2)}) %copy-start.1) | copy-done | bytes 98328
  19.5 4.5 %round0.1 = (f32[9,4,16,128]{3,2,1,0:T(8,128)S(1)}, bf16[7,3,16,128]{3,2,1,0:T(8,128)(2,1)S(1)}, bf16[7,3,16,128]{3,2,1,0:T(8,128)(2,1)S(1)}) custom-call(s32[2]{0:T(128)S(1)} %pad_add_fusion.place, f32[8]{0:T(128)S(1)} %reshape_squeeze.3.step, f32[4,16,128]{2,1,0:T(8,128)S(1)} %get-tuple-element.22.lat.prior, ...), custom_call_target="tpu_custom_call" | custom-call | tf_op jit(solution)/shard_map/round0/pallas_call | solution.py:181
  24.1 0.6 collective-permute-start.5
  24.7 2.8 %collective-permute-start.6 = (bf16[7,3,16,128]{3,2,1,0:T(8,128)(2,1)S(1)}, bf16[7,3,16,128]{3,2,1,0:T(8,128)(2,1)S(1)}, u32[]{:S(2)}, u32[]{:S(2)}) collective-permute-start(bf16[7,3,16,128]{3,2,1,0:T(8,128)(2,1)S(1)} %get-tuple-element.17), channel_id=1, source_target_pairs={{1,2},{3,4},{5,6},{7,8},{9,10},{11,12},{13,14},{15,16},{17,18},{19... | collective-permute-start | bytes 258056 | tf_op jit(solution)/shard_map/ppermute | solution.py:221
  27.5 0.0 collective-permute-done.5.from_a
  27.5 5.1 %collective-permute-done.6.from_b = bf16[7,3,16,128]{3,2,1,0:T(8,128)(2,1)S(1)} collective-permute-done((bf16[7,3,16,128]{3,2,1,0:T(8,128)(2,1)S(1)}, bf16[7,3,16,128]{3,2,1,0:T(8,128)(2,1)S(1)}, u32[]{:S(2)}, u32[]{:S(2)}) %collective-permute-start.6) | collective-permute-done | bytes 86048 | tf_op jit(solution)/shard_map/ppermute | solution.py:221
  32.6 4.5 %round1.1 = (f32[9,4,16,128]{3,2,1,0:T(8,128)S(1)}, bf16[6,3,16,128]{3,2,1,0:T(8,128)(2,1)S(1)}, bf16[6,3,16,128]{3,2,1,0:T(8,128)(2,1)S(1)}) custom-call(s32[2]{0:T(128)S(1)} %pad_add_fusion.place, f32[8]{0:T(128)S(1)} %reshape_squeeze.3.step, f32[4,16,128]{2,1,0:T(8,128)S(1)} %get-tuple-element.22.lat.prior, ...), custom_call_target="tpu_custom_call" | custom-call | tf_op jit(solution)/shard_map/round1/pallas_call | solution.py:181
  37.1 0.1 collective-permute-start.7
  37.2 3.0 %collective-permute-start.8 = (bf16[6,3,16,128]{3,2,1,0:T(8,128)(2,1)S(1)}, bf16[6,3,16,128]{3,2,1,0:T(8,128)(2,1)S(1)}, u32[]{:S(2)}, u32[]{:S(2)}) collective-permute-start(bf16[6,3,16,128]{3,2,1,0:T(8,128)(2,1)S(1)} %get-tuple-element.20), channel_id=1, source_target_pairs={{1,2},{3,4},{5,6},{7,8},{9,10},{11,12},{13,14},{15,16},{17,18},{19... | collective-permute-start | bytes 221192 | tf_op jit(solution)/shard_map/ppermute | solution.py:221
  40.1 0.0 collective-permute-done.7.from_a
  40.1 4.8 %collective-permute-done.8.from_b = bf16[6,3,16,128]{3,2,1,0:T(8,128)(2,1)S(1)} collective-permute-done((bf16[6,3,16,128]{3,2,1,0:T(8,128)(2,1)S(1)}, bf16[6,3,16,128]{3,2,1,0:T(8,128)(2,1)S(1)}, u32[]{:S(2)}, u32[]{:S(2)}) %collective-permute-start.8) | collective-permute-done | bytes 73760 | tf_op jit(solution)/shard_map/ppermute | solution.py:221
  44.9 0.0 copy-done.2
  44.9 3.8 %round2.1 = f32[4,2,4,16,128]{4,3,2,1,0:T(8,128)S(1)} custom-call(s32[2]{0:T(128)S(1)} %pad_add_fusion.place, f32[8]{0:T(128)S(1)} %reshape_squeeze.3.step, f32[4,16,128]{2,1,0:T(8,128)S(1)} %get-tuple-element.22.lat.prior, f32[9,4,16,128]{3,2,1,0:T(8,128)S(1)} %get-tuple-element.18.prior, bf16[6,3,16,128]{3,2,1,0:T(8,128)(2,1)S(1)} %collective-permute-done.7.from_a, ...), custom_call_target="tpu_custom_call" | custom-call | tf_op jit(solution)/shard_map/round2/pallas_call | solution.py:181
  48.8 0.7 %fusion.14 = (f32[1,2,4,16,128]{4,3,2,1,0:T(8,128)S(1)}, f32[1,2,4,16,128]{4,3,2,1,0:T(8,128)S(1)}, f32[1,2,4,16,128]{4,3,2,1,0:T(8,128)S(1)}, f32[1,2,4,16,128]{4,3,2,1,0:T(8,128)}) fusion(f32[4,2,4,16,128]{4,3,2,1,0:T(8,128)S(1)} %round2.1), kind=kLoop, calls=%fused_computation.38 | loop fusion | bytes 524288 | tf_op jit(solution)/shard_map/slice | solution.py:262
  49.4 2.7 %collective-permute-start.10 = (f32[128,128]{1,0:T(8,128)S(1)}, f32[128,128]{1,0:T(8,128)S(1)}, u32[]{:S(2)}, u32[]{:S(2)}) collective-permute-start(f32[128,128]{1,0:T(8,128)S(1)} %bitcast.29), channel_id=1, source_target_pairs={{0,128},{64,192},{128,0},{192,64},{1,129},{65,193},{129,1},{193,65... | collective-permute-start | bytes 196616 | tf_op jit(solution)/shard_map/ppermute | solution.py:217
  52.1 1.2 %collective-permute-start.11 = (f32[128,128]{1,0:T(8,128)S(1)}, f32[128,128]{1,0:T(8,128)S(1)}, u32[]{:S(2)}, u32[]{:S(2)}) collective-permute-start(f32[128,128]{1,0:T(8,128)S(1)} %bitcast.28), channel_id=1, source_target_pairs={{0,192},{64,128},{128,64},{192,0},{1,193},{65,129},{129,65},{193,1... | collective-permute-start | bytes 196616 | tf_op jit(solution)/shard_map/ppermute | solution.py:217
  53.2 0.0 collective-permute-start.9
  53.2 2.1 %collective-permute-done.10.p2 = f32[128,128]{1,0:T(8,128)S(1)} collective-permute-done((f32[128,128]{1,0:T(8,128)S(1)}, f32[128,128]{1,0:T(8,128)S(1)}, u32[]{:S(2)}, u32[]{:S(2)}) %collective-permute-start.10) | collective-permute-done | bytes 65568 | tf_op jit(solution)/shard_map/ppermute | solution.py:217
  55.3 0.0 copy-start.3
  55.3 2.3 %collective-permute-done.11.p3 = f32[128,128]{1,0:T(8,128)S(1)} collective-permute-done((f32[128,128]{1,0:T(8,128)S(1)}, f32[128,128]{1,0:T(8,128)S(1)}, u32[]{:S(2)}, u32[]{:S(2)}) %collective-permute-start.11) | collective-permute-done | bytes 65568 | tf_op jit(solution)/shard_map/ppermute | solution.py:217
  57.6 0.0 copy-start.4
  57.6 0.0 collective-permute-done.9.p1
  57.6 0.0 copy-start.5
  57.6 0.0 copy-done.3
  57.6 0.6 copy-done.4
  58.2 0.0 copy-done.5
  58.2 1.8 %join.1 = f32[128,448]{1,0:T(8,128)} custom-call(s32[2]{0:T(128)} %copy-done.2, f32[128,128]{1,0:T(8,128)} %bitcast.25, f32[128,128]{1,0:T(8,128)} %copy-done.5, f32[128,128]{1,0:T(8,128)} %copy-done.3, f32[128,128]{1,0:T(8,128)} %copy-done.4), custom_call_target="tpu_custom_call" | custom-call | tf_op jit(solution)/shard_map/join/pallas_call | solution.py:207
  60.0 1.8 %copy.23 = f32[2,4,16,448]{3,1,2,0:T(4,128)} copy(f32[2,4,16,448]{3,2,1,0:T(8,128)} %bitcast.24) | data formatting | bytes 458752 | tf_op jit(solution)/shard_map/reshape | solution.py:263
  (9 shorter events, 0.1 us)
Async XLA Ops:
  1.5 15.3 %collective-permute-start.1 = (f32[4,128]{1,0:T(4,128)S(1)}, f32[4,128]{1,0:T(4,128)S(1)}, u32[]{:S(2)}, u32[]{:S(2)}) collective-permute-start(f32[4,128]{1,0:T(4,128)S(1)} %get-tuple-element.37), channel_id=1, source_target_pairs={{0,128},{64,192},{128,0},{192,64},{1,129},{65,193},{129,1},{193,65... | collective-permute-start | bytes 6152 | tf_op jit(solution)/shard_map/ppermute | solution.py:217
  4.5 12.3 %collective-permute-start = (f32[4,128]{1,0:T(4,128)S(1)}, f32[4,128]{1,0:T(4,128)S(1)}, u32[]{:S(2)}, u32[]{:S(2)}) collective-permute-start(f32[4,128]{1,0:T(4,128)S(1)} %get-tuple-element.37), channel_id=1, source_target_pairs={{0,64},{64,0},{128,192},{192,128},{1,65},{65,1},{129,193},{193,129... | collective-permute-start | bytes 6152 | tf_op jit(solution)/shard_map/ppermute | solution.py:217
  5.1 11.7 %collective-permute-start.2 = (f32[4,128]{1,0:T(4,128)S(1)}, f32[4,128]{1,0:T(4,128)S(1)}, u32[]{:S(2)}, u32[]{:S(2)}) collective-permute-start(f32[4,128]{1,0:T(4,128)S(1)} %get-tuple-element.37), channel_id=1, source_target_pairs={{0,192},{64,128},{128,64},{192,0},{1,193},{65,129},{129,65},{193,1... | collective-permute-start | bytes 6152 | tf_op jit(solution)/shard_map/ppermute | solution.py:217
  6.7 10.7 %collective-permute-start.4 = (bf16[3,16,128]{2,1,0:T(8,128)(2,1)S(1)}, bf16[3,16,128]{2,1,0:T(8,128)(2,1)S(1)}, u32[]{:S(2)}, u32[]{:S(2)}) collective-permute-start(bf16[3,16,128]{2,1,0:T(8,128)(2,1)S(1)} %get-tuple-element.27), channel_id=1, source_target_pairs={{1,2},{3,4},{5,6},{7,8},{9,10},{11,12},{13,14},{15,16},{17,18},{19... | collective-permute-start | bytes 36872 | tf_op jit(solution)/shard_map/ppermute | solution.py:221
  13.5 3.8 %collective-permute-start.3 = (bf16[3,16,128]{2,1,0:T(8,128)(2,1)S(1)}, bf16[3,16,128]{2,1,0:T(8,128)(2,1)S(1)}, u32[]{:S(2)}, u32[]{:S(2)}) collective-permute-start(bf16[3,16,128]{2,1,0:T(8,128)(2,1)S(1)} %get-tuple-element.28), channel_id=1, source_target_pairs={{0,1},{2,3},{4,5},{6,7},{8,9},{10,11},{12,13},{14,15},{16,17},{18,... | collective-permute-start | bytes 36872 | tf_op jit(solution)/shard_map/ppermute | solution.py:221
  14.5 30.5 %copy-start.2 = (s32[2]{0:T(128)}, s32[2]{0:T(128)S(1)}, u32[]{:S(2)}) copy-start(s32[2]{0:T(128)S(1)} %pad_add_fusion.place) | copy-start | bytes 28
  17.4 1.3 %copy-start = (bf16[384,1536]{1,0:T(8,128)(2,1)S(1)}, bf16[384,1536]{1,0:T(8,128)(2,1)}, u32[]{:S(2)}) copy-start(bf16[384,1536]{1,0:T(8,128)(2,1)} %get-tuple-element.13.w_mid) | copy-start | bytes 3538948
  18.7 0.9 %copy-start.1 = (bf16[96,512]{1,0:T(8,128)(2,1)S(1)}, bf16[96,512]{1,0:T(8,128)(2,1)}, u32[]{:S(2)}) copy-start(bf16[96,512]{1,0:T(8,128)(2,1)} %get-tuple-element.14.w_out) | copy-start | bytes 294916
  24.1 3.4 %collective-permute-start.5 = (bf16[7,3,16,128]{3,2,1,0:T(8,128)(2,1)S(1)}, bf16[7,3,16,128]{3,2,1,0:T(8,128)(2,1)S(1)}, u32[]{:S(2)}, u32[]{:S(2)}) collective-permute-start(bf16[7,3,16,128]{3,2,1,0:T(8,128)(2,1)S(1)} %get-tuple-element.16), channel_id=1, source_target_pairs={{0,1},{2,3},{4,5},{6,7},{8,9},{10,11},{12,13},{14,15},{16,17},{18,... | collective-permute-start | bytes 258056 | tf_op jit(solution)/shard_map/ppermute | solution.py:221
  24.7 7.9 %collective-permute-start.6 = (bf16[7,3,16,128]{3,2,1,0:T(8,128)(2,1)S(1)}, bf16[7,3,16,128]{3,2,1,0:T(8,128)(2,1)S(1)}, u32[]{:S(2)}, u32[]{:S(2)}) collective-permute-start(bf16[7,3,16,128]{3,2,1,0:T(8,128)(2,1)S(1)} %get-tuple-element.17), channel_id=1, source_target_pairs={{1,2},{3,4},{5,6},{7,8},{9,10},{11,12},{13,14},{15,16},{17,18},{19... | collective-permute-start | bytes 258056 | tf_op jit(solution)/shard_map/ppermute | solution.py:221
  37.1 3.1 %collective-permute-start.7 = (bf16[6,3,16,128]{3,2,1,0:T(8,128)(2,1)S(1)}, bf16[6,3,16,128]{3,2,1,0:T(8,128)(2,1)S(1)}, u32[]{:S(2)}, u32[]{:S(2)}) collective-permute-start(bf16[6,3,16,128]{3,2,1,0:T(8,128)(2,1)S(1)} %get-tuple-element.19), channel_id=1, source_target_pairs={{0,1},{2,3},{4,5},{6,7},{8,9},{10,11},{12,13},{14,15},{16,17},{18,... | collective-permute-start | bytes 221192 | tf_op jit(solution)/shard_map/ppermute | solution.py:221
  37.2 7.8 %collective-permute-start.8 = (bf16[6,3,16,128]{3,2,1,0:T(8,128)(2,1)S(1)}, bf16[6,3,16,128]{3,2,1,0:T(8,128)(2,1)S(1)}, u32[]{:S(2)}, u32[]{:S(2)}) collective-permute-start(bf16[6,3,16,128]{3,2,1,0:T(8,128)(2,1)S(1)} %get-tuple-element.20), channel_id=1, source_target_pairs={{1,2},{3,4},{5,6},{7,8},{9,10},{11,12},{13,14},{15,16},{17,18},{19... | collective-permute-start | bytes 221192 | tf_op jit(solution)/shard_map/ppermute | solution.py:221
  49.4 5.9 %collective-permute-start.10 = (f32[128,128]{1,0:T(8,128)S(1)}, f32[128,128]{1,0:T(8,128)S(1)}, u32[]{:S(2)}, u32[]{:S(2)}) collective-permute-start(f32[128,128]{1,0:T(8,128)S(1)} %bitcast.29), channel_id=1, source_target_pairs={{0,128},{64,192},{128,0},{192,64},{1,129},{65,193},{129,1},{193,65... | collective-permute-start | bytes 196616 | tf_op jit(solution)/shard_map/ppermute | solution.py:217
  52.1 5.5 %collective-permute-start.11 = (f32[128,128]{1,0:T(8,128)S(1)}, f32[128,128]{1,0:T(8,128)S(1)}, u32[]{:S(2)}, u32[]{:S(2)}) collective-permute-start(f32[128,128]{1,0:T(8,128)S(1)} %bitcast.28), channel_id=1, source_target_pairs={{0,192},{64,128},{128,64},{192,0},{1,193},{65,129},{129,65},{193,1... | collective-permute-start | bytes 196616 | tf_op jit(solution)/shard_map/ppermute | solution.py:217
  53.2 4.3 %collective-permute-start.9 = (f32[128,128]{1,0:T(8,128)S(1)}, f32[128,128]{1,0:T(8,128)S(1)}, u32[]{:S(2)}, u32[]{:S(2)}) collective-permute-start(f32[128,128]{1,0:T(8,128)S(1)} %bitcast.27), channel_id=1, source_target_pairs={{0,64},{64,0},{128,192},{192,128},{1,65},{65,1},{129,193},{193,129... | collective-permute-start | bytes 196616 | tf_op jit(solution)/shard_map/ppermute | solution.py:217
  55.3 2.3 %copy-start.3 = (f32[128,128]{1,0:T(8,128)}, f32[128,128]{1,0:T(8,128)S(1)}, u32[]{:S(2)}) copy-start(f32[128,128]{1,0:T(8,128)S(1)} %collective-permute-done.10.p2) | copy-start | bytes 196612
  57.6 0.6 %copy-start.4 = (f32[128,128]{1,0:T(8,128)}, f32[128,128]{1,0:T(8,128)S(1)}, u32[]{:S(2)}) copy-start(f32[128,128]{1,0:T(8,128)S(1)} %collective-permute-done.11.p3) | copy-start | bytes 196612
  57.6 0.7 %copy-start.5 = (f32[128,128]{1,0:T(8,128)}, f32[128,128]{1,0:T(8,128)S(1)}, u32[]{:S(2)}) copy-start(f32[128,128]{1,0:T(8,128)S(1)} %collective-permute-done.9.p1) | copy-start | bytes 196612
where the time goes:
time: 62.3 us; the launch traced here: 61.9 us
  starting transfers between devices  21.3 us (34%)
  Pallas kernels  16.8 us (27%)
  waiting for transfers between devices  14.2 us (23%)
  local copies, waits for them, and re-layouts  7.39 us (12%)
  other arithmetic  1.84 us (3%)
    ppermute x6, starting transfers between devices, pair_up(): lax.ppermute(x, 'pix', [(a, b) for a, b in pairs] + [(b, a) for a, b in p...  13.3 us
    pallas_call x3, Pallas kernels, run_round(): pl.pallas_call(functools.partial(round_body, rounds), out_shape=out_shape...  12.8 us
    ppermute x6, waiting for transfers between devices, pair_up(): lax.ppermute(x, 'pix', [(a, b) for a, b in pairs] + [(b, a) for a, b in p...  9.9 us
    ppermute x6, starting transfers between devices, across(): return lax.ppermute(x, 'tm', [(t, t ^ k) for t in range(4)])  7.98 us
    ppermute x6, waiting for transfers between devices, across(): return lax.ppermute(x, 'tm', [(t, t ^ k) for t in range(4)])  4.33 us
    unnamed x13, local copies, waits for them, and re-layouts  3.77 us
    pallas_call x1, Pallas kernels, prepare(): pl.pallas_call(prepare_body, out_shape=(jax.ShapeDtypeStruct((3 * F, 12 *...  2.2 us
    reshape x1, local copies, waits for them, and re-layouts, shards(): return join(place, got).reshape(2, 4, C, 448).transpose(0, 2, 1, 3)  1.82 us
  transfers between devices with their start and end apart: 12, of which 4 were waited for; matrix products, arithmetic and copies ran while one was open for 4% of the time, Pallas kernels for 4%

commit v1 on v0

v1 whole, which is shorter than its diff:
```python
import functools

import jax
import jax.numpy as jnp
from jax import lax
from jax.experimental import pallas as pl
from jax.experimental.pallas import tpu as pltpu
from jax.sharding import PartitionSpec as P

TIMES = 8
C = 16
F = 128
L = 128
ROWS = 4
STARTS = (-1, 105, 215, 321)
SHIFTS = tuple(-start % L for start in STARTS)
CUTS = (114, 224, 334)
BF = jnp.bfloat16
F32 = jnp.float32


VM = pl.BlockSpec(memory_space=pltpu.VMEM)
SM = pl.BlockSpec(memory_space=pltpu.SMEM)


def by_tm(tm, values):
    return jnp.where(tm == 0, values[0], jnp.where(tm == 1, values[1], jnp.where(tm == 2, values[2], values[3])))


def enter_body(step, latent, embed, lat, to_a, to_b, small):
    tm, core = lax.axis_index("tm"), lax.axis_index("pix") % 2
    shift = by_tm(tm, SHIFTS)
    lane = lax.broadcasted_iota(jnp.int32, (C, L), 1)
    for r in range(ROWS):
        tiles = [jnp.zeros((C, L), F32)] + [latent[:, r, g * L:(g + 1) * L] for g in range(3)]
        tiles.append(jnp.concatenate([latent[:, r, 3 * L:], jnp.zeros((C, 4 * L - 448), F32)], axis=1))
        left, right = by_tm(tm, tiles[:4]), by_tm(tm, tiles[1:])
        lat[r] = jnp.where(lane < shift, pltpu.roll(left, shift, 1), pltpu.roll(right, shift, 1))
    for d in range(3):
        to_a[d] = lat[d + 1 - core].astype(BF)
        to_b[d] = lat[d + core].astype(BF)
    small[0:2] = embed[...]
    for d in range(2):
        small[2 + d:3 + d] = jnp.full((1, F), step[d], F32)


def enter(step, latent, embed):
    sent = jax.ShapeDtypeStruct((3, C, L), BF)
    return pl.pallas_call(
        enter_body,
        out_shape=(jax.ShapeDtypeStruct((ROWS, C, L), F32), sent, sent, jax.ShapeDtypeStruct((4, F), F32)),
        in_specs=[SM, VM, VM],
        out_specs=(VM,) * 4,
        compiler_params=pltpu.CompilerParams(vmem_limit_bytes=4 << 20),
        name="enter",
    )(step, latent, embed)


def prepare(tm, smalls, conv_in, conv_mid, conv_out, w_in, w_mid, w_out, steps, gathered, turned):
    w_mid[...] = jnp.zeros_like(w_mid)
    w_out[...] = jnp.zeros_like(w_out)
    turned[...] = jnp.zeros_like(turned)
    for a in range(3):
        for b in range(3):
            mid = conv_mid[a, b] * 0.5
            tail = conv_out[a, b]
            head = conv_in[a, b] * 0.5
            for q in range(2):
                w_mid[q * F:(q + 1) * F, ((a + q) * 3 + b) * F:((a + q) * 3 + b + 1) * F] = mid
                w_out[q * 48 + b * C:q * 48 + (b + 1) * C, (a + q) * F:(a + q + 1) * F] = tail
                turned[(a + q) * 48 + b * C:(a + q) * 48 + (b + 1) * C, q * F:(q + 1) * F] = head
    for k in range(4):
        gathered[tm ^ k] = smalls[k][...]
    embed = jnp.concatenate([gathered[t, 0:2] for t in range(4)], axis=0) * 0.5
    steps[...] = jnp.concatenate([gathered[t, 2:4] for t in range(4)], axis=0)
    high = embed.astype(BF).astype(F32)
    rest = embed - high
    middle = rest.astype(BF).astype(F32)
    tail = jnp.concatenate([high, middle, rest - middle, jnp.zeros((40, F), F32)], axis=0).astype(BF)
    for q in range(2):
        turned[192:, q * F:(q + 1) * F] = tail
    w_in[:2 * F] = turned[...].astype(F32).T.astype(BF)
    w_in[2 * F:] = jnp.zeros((F, 2 * F), BF)


def silu2(v):
    return v + v * jnp.tanh(v)


def round_body(rounds, *refs):
    pix, tm = lax.axis_index("pix"), lax.axis_index("tm")
    core = pix % 2
    last = rounds == 2
    if rounds == 0:
        lat, from_a, from_b, *smalls = refs[:7]
        conv_in, conv_mid, conv_out, nxt, to_a, to_b, w_in, w_mid, w_out, steps, *rest = refs[7:]
        prior = None
        prepare(tm, smalls, conv_in, conv_mid, conv_out, w_in, w_mid, w_out, steps, *rest[16:])
    else:
        lat, from_a, from_b, prior, w_in, w_mid, w_out, steps = refs[:8]
        if last:
            out, rest, ready = refs[8:12], refs[12:], refs[-1]
        else:
            nxt, to_a, to_b, *rest = refs[8:]
    low, hid, sec = rest[:2], rest[2:10], rest[10:16]
    groups = [(t0, min(4, TIMES - t0)) for t0 in (rounds, rounds + 4)]

    lane = lax.broadcasted_iota(jnp.int32, (C, L), 1)
    column = jnp.where(((tm == 0) & (lane == 0)) | ((tm == 3) & (lane == L - 1)), 0.0, 1.0)

    def state(t, row):
        return lat[row] if rounds == 0 else prior[t, row]

    def spread(x):
        x = x * column
        return jnp.concatenate([pltpu.roll(x, 1, 1) * column, x, pltpu.roll(x, L - 1, 1) * column], axis=0).astype(BF)

    def fill(g):
        t0, n = groups[g]
        for w in range(10):
            for i in range(n if rounds else 1):
                if 3 <= w < 7:
                    x = state(t0 + i, w - 3)
                else:
                    d = w if w < 3 else w - 7
                    at = (t0 + i - rounds, d) if rounds else (d,)
                    a, b = from_a[at].astype(F32), from_b[at].astype(F32)
                    x = jnp.where((core == 0) == (w < 3), b, a)
                x = spread(x)
                for lanes in ([i] if rounds else range(n)):
                    low[g][w * 48:(w + 1) * 48, lanes * L:(lanes + 1) * L] = x

    def weights(ref, top_inside, bottom_inside):
        top = 0 if top_inside is None else pl.multiple_of(jnp.where(top_inside, 0, 2 * F), F)
        bottom = F if bottom_inside is None else pl.multiple_of(jnp.where(bottom_inside, F, 2 * F), F)
        return jnp.concatenate([ref[pl.ds(top, F), :], ref[pl.ds(bottom, F), :]], axis=0)

    above, below = pix > 0, pix < 63

    def hidden_pair(g, p):
        t0, n = groups[g]
        width = n * L
        r = lax.broadcasted_iota(jnp.int32, (64, width), 0)
        c = lax.broadcasted_iota(jnp.int32, (64, width), 1)
        edge = ((tm == 0) & ((c & 127) == 0)) | ((tm == 3) & ((c & 127) == L - 1))
        pick = jnp.where(((r & 7) == t0 + (c >> 7)) & (r < 24) & jnp.logical_not(edge), 1.0, 0.0).astype(BF)
        rhs = jnp.concatenate([low[g][2 * p * 48:2 * p * 48 + 192, :width], pick], axis=0)
        inside = above if p == 0 else below if p == 3 else None
        v = silu2(jnp.dot(weights(w_in, inside, inside), rhs, preferred_element_type=F32))
        to = hid[g * 4 + p]
        for i in range(n):
            for q in range(2):
                x = v[q * F:(q + 1) * F, i * L:(i + 1) * L]
                at = q * 384
                to[at:at + F, i * L:(i + 1) * L] = pltpu.roll(x, 1, 1).astype(BF)
                to[at + F:at + 2 * F, i * L:(i + 1) * L] = x.astype(BF)
                to[at + 2 * F:at + 3 * F, i * L:(i + 1) * L] = pltpu.roll(x, L - 1, 1).astype(BF)

    def second_pair(g, p):
        width = groups[g][1] * L
        rhs = jnp.concatenate([hid[g * 4 + p][:, :width], hid[g * 4 + p + 1][:, :width]], axis=0)
        w = weights(w_mid, above if p == 0 else None, below if p == 2 else None)
        sec[g * 3 + p][:, :width] = silu2(jnp.dot(w, rhs, preferred_element_type=F32)).astype(BF)

    def keep(t, row, value):
        ready[pl.ds(((t // 2) ^ tm) * 128 + (t % 2) * 64 + row, C, stride=ROWS), :] = value

    totals = [jnp.zeros((C, L), F32) if rounds == 0 else prior[0, row] for row in range(ROWS)]

    def out_pair(g, p):
        t0, n = groups[g]
        width = n * L
        rhs = jnp.concatenate([sec[g * 3 + p][:, :width], sec[g * 3 + p + 1][:, :width]], axis=0)
        y = jnp.dot(w_out[...], rhs, preferred_element_type=F32)
        for q in range(2):
            row = 2 * p + q
            for i in range(n):
                t = t0 + i
                part = y[q * 48:(q + 1) * 48, i * L:(i + 1) * L]
                conv = pltpu.roll(part[:C] * column, 1, 1) + part[C:2 * C] + pltpu.roll(part[2 * C:] * column, L - 1, 1)
                totals[row] = totals[row] + steps[t:t + 1] * (state(t, row) + conv)
                value = lat[row] + totals[row]
                if last:
                    keep(t, row, value)
                else:
                    nxt[t + 1, row] = value
                    if t == rounds:
                        nxt[0, row] = totals[row]

    fill(0)
    for p in range(4):
        hidden_pair(0, p)
    fill(1)
    second_pair(0, 0)
    hidden_pair(1, 0)
    second_pair(0, 1)
    hidden_pair(1, 1)
    second_pair(0, 2)
    hidden_pair(1, 2)
    out_pair(0, 0)
    hidden_pair(1, 3)
    out_pair(0, 1)
    for p in range(3):
        second_pair(1, p)
    for p in range(2):
        out_pair(1, p)

    for row in range(ROWS):
        if rounds == 1:
            nxt[1, row] = prior[1, row]
        if last:
            for t in range(2):
                keep(t, row, prior[t + 1, row])
    if last:
        for k in range(4):
            out[k][...] = ready[k * 128:(k + 1) * 128].reshape(32, ROWS, L)
    else:
        for t in range(rounds + 1, TIMES):
            for d in range(3):
                to_a[t - rounds - 1, d] = nxt[t, d + 1 - core].astype(BF)
                to_b[t - rounds - 1, d] = nxt[t, d + core].astype(BF)


def run_round(rounds, *args):
    scratch = [pltpu.VMEM((480, 4 * L), BF)] * 2 + [pltpu.VMEM((768, 4 * L), BF)] * 8 + [pltpu.VMEM((2 * F, 4 * L), BF)] * 6
    if rounds == 2:
        out_shape = (jax.ShapeDtypeStruct((32, ROWS, L), F32),) * 4
        scratch += [pltpu.VMEM((512, L), F32)]
    else:
        sent = jax.ShapeDtypeStruct((TIMES - 1 - rounds, 3, C, L), BF)
        out_shape = (jax.ShapeDtypeStruct((TIMES + 1, ROWS, C, L), F32), sent, sent)
    if rounds == 0:
        tables = ((3 * F, 2 * F), (3 * F, 12 * F), (96, 4 * F))
        out_shape += tuple(jax.ShapeDtypeStruct(shape, BF) for shape in tables) + (jax.ShapeDtypeStruct((TIMES, F), F32),)
        scratch += [pltpu.VMEM((4, 4, F), F32), pltpu.VMEM((2 * F, 2 * F), BF)]
    return pl.pallas_call(
        functools.partial(round_body, rounds),
        out_shape=out_shape,
        in_specs=[VM] * len(args),
        out_specs=(VM,) * len(out_shape),
        scratch_shapes=scratch,
        compiler_params=pltpu.CompilerParams(vmem_limit_bytes=40 << 20),
        name="round%d" % rounds,
    )(*args)


def join_body(p0, p1, p2, p3, out):
    tm = lax.axis_index("tm")
    pieces = [p0[...], p1[...], p2[...], p3[...]]
    lane = lax.broadcasted_iota(jnp.int32, pieces[0].shape, 2)
    placed = []
    for t in range(4):
        x = by_tm(t ^ tm, pieces)
        placed.append(pltpu.roll(x, STARTS[t] % L, 2))
    for g in range(3):
        out[:, :, g * L:(g + 1) * L] = jnp.where(lane < CUTS[g] - g * L, placed[g], placed[g + 1])
    out[:, :, 3 * L:] = placed[3][:, :, :448 - 3 * L]


def join(pieces):
    return pl.pallas_call(
        join_body,
        out_shape=jax.ShapeDtypeStruct((32, ROWS, 448), F32),
        in_specs=[VM] * 4,
        out_specs=VM,
        compiler_params=pltpu.CompilerParams(vmem_limit_bytes=8 << 20),
        name="join",
    )(*pieces)


def across(x, k):
    return lax.ppermute(x, "tm", [(t, t ^ k) for t in range(4)])


def pair_up(x, pairs):
    return lax.ppermute(x, "pix", [(a, b) for a, b in pairs] + [(b, a) for a, b in pairs])


CORES = [(2 * k, 2 * k + 1) for k in range(32)]
CHIPS = [(2 * k + 1, 2 * k + 2) for k in range(31)]


def shards(latent, step_size, time_embed, conv_in, conv_mid, conv_out):
    lat, to_a, to_b, small = enter(step_size, latent, time_embed)
    from_b = pair_up(to_b, CHIPS)
    smalls = [small] + [across(small, k) for k in (1, 2, 3)]
    from_a = pair_up(to_a, CORES)
    prior, to_a, to_b, *tables = run_round(0, lat, from_a, from_b, *smalls, conv_in.transpose(0, 1, 3, 2), conv_mid, conv_out)
    from_b, from_a = pair_up(to_b, CHIPS), pair_up(to_a, CORES)
    prior, to_a, to_b = run_round(1, lat, from_a, from_b, prior, *tables)
    from_b, from_a = pair_up(to_b, CHIPS), pair_up(to_a, CORES)
    pieces = run_round(2, lat, from_a, from_b, prior, *tables)
    got = [pieces[0]] + [across(pieces[k], k) for k in (1, 2, 3)]
    return join(got).reshape(2, C, ROWS, 448)


def solution(mesh):
    in_specs = (P(None, "pix", None), P("tm"), P("tm", None), P(), P(), P())
    out_specs = P("tm", None, "pix", None)
    return jax.shard_map(shards, mesh=mesh, in_specs=in_specs, out_specs=out_specs, check_vma=False)
```

time: 62.3 us -> 59 us (0.947)
  Pallas kernels: 16.8 us -> 13.5 us
  waiting for transfers between devices: 14.2 us -> 16.9 us
  local copies, waits for them, and re-layouts: 7.39 us -> 4.73 us
  starting transfers between devices: 21.3 us -> 23.4 us
  other arithmetic: 1.84 us -> 0 us
    ppermute x6, waiting for transfers between devices: 4.33 us -> 7.38 us  [across(): return lax.ppermute(x, 'tm', [(t, t ^ k) for t in range(4)])]
    pallas_call x2, Pallas kernels: 4 us -> 1.67 us  [the longest x1 0.92 us: join(): pl.pallas_call(join_body, out_shape=jax.ShapeDtypeStruct((32, ROWS, 448),...]
    reshape x2 -> x0, local copies, waits for them, and re-layouts: 1.93 us -> none  [the longest x1 1.82 us: shards(): return join(place, got).reshape(2, 4, C, 448).transpose(0, 2, 1, 3)]
    ppermute x6, starting transfers between devices: 13.3 us -> 14.5 us  [pair_up(): lax.ppermute(x, 'pix', [(a, b) for a, b in pairs] + [(b, a) for a, b in p...]
    ppermute x6, starting transfers between devices: 7.98 us -> 8.97 us  [across(): return lax.ppermute(x, 'tm', [(t, t ^ k) for t in range(4)])]
    pallas_call x3, Pallas kernels: 12.8 us -> 11.9 us  [run_round(): pl.pallas_call(functools.partial(round_body, rounds), out_shape=out_shape...]
    unnamed x13 -> x12, local copies, waits for them, and re-layouts: 3.77 us -> 4.73 us
    concatenate x2 -> x0, local copies, waits for them, and re-layouts: 0.85 us -> none  [the longest x1 0.73 us: shards(): jnp.concatenate([time_embed, jnp.broadcast_to(step_size[:, None], (2, F))])]
  transfers between devices with their start and end apart: 12 -> 12, of which waited for: 4 -> 6; matrix products, arithmetic and copies ran while one was open for 4% -> 0% of each run, Pallas kernels for 4% -> 0%
where the time goes in v1:
time: 59 us; the launch traced here: 58.7 us
  starting transfers between devices  23.4 us (40%)
  waiting for transfers between devices  16.9 us (29%)
  Pallas kernels  13.5 us (23%)
  local copies, waits for them, and re-layouts  4.73 us (8%)
    ppermute x6, starting transfers between devices, pair_up(): lax.ppermute(x, 'pix', [(a, b) for a, b in pairs] + [(b, a) for a, b in p...  14.5 us
    pallas_call x3, Pallas kernels, run_round(): pl.pallas_call(functools.partial(round_body, rounds), out_shape=out_shape...  11.9 us
    ppermute x6, waiting for transfers between devices, pair_up(): lax.ppermute(x, 'pix', [(a, b) for a, b in pairs] + [(b, a) for a, b in p...  9.48 us
    ppermute x6, starting transfers between devices, across(): return lax.ppermute(x, 'tm', [(t, t ^ k) for t in range(4)])  8.97 us
    ppermute x6, waiting for transfers between devices, across(): return lax.ppermute(x, 'tm', [(t, t ^ k) for t in range(4)])  7.38 us
    unnamed x12, local copies, waits for them, and re-layouts  4.73 us
  transfers between devices with their start and end apart: 12, of which 6 were waited for; matrix products, arithmetic and copies ran while one was open for 0% of the time, Pallas kernels for 0%

profile of v1, /device:TPU:24, one launch (start us, length us, event | category | flops | bytes accessed | tf_op | source)
XLA Modules:
  0.0 58.7 jit_solution(7595613647489212038)
XLA Ops:
  0.0 0.0 copy-start.1
  0.0 0.9 %copy-done.1 = f32[16,4,448]{2,1,0:T(4,128)S(1)} copy-done((f32[16,4,448]{2,1,0:T(4,128)S(1)}, f32[16,4,448]{2,1,0:T(4,128)}, u32[]{:S(2)}) %copy-start.1) | copy-done | bytes 114712
  0.9 0.0 copy-start.4
  0.9 0.7 %copy-done.4 = f32[2,128]{1,0:T(2,128)S(1)} copy-done((f32[2,128]{1,0:T(2,128)S(1)}, f32[2,128]{1,0:T(2,128)}, u32[]{:S(2)}) %copy-start.4) | copy-done | bytes 1048
  1.6 0.0 copy-start.5
  1.6 0.7 %copy-done.5 = f32[2]{0:T(128)S(1)} copy-done((f32[2]{0:T(128)S(1)}, f32[2]{0:T(128)}, u32[]{:S(2)}) %copy-start.5) | copy-done | bytes 32
  2.2 0.7 %enter.1 = (f32[4,16,128]{2,1,0:T(8,128)S(1)}, bf16[3,16,128]{2,1,0:T(8,128)(2,1)S(1)}, bf16[3,16,128]{2,1,0:T(8,128)(2,1)S(1)}, f32[4,128]{1,0:T(4,128)S(1)}) custom-call(f32[2]{0:T(128)S(1)} %copy-done.5, f32[16,4,448]{2,1,0:T(4,128)S(1)} %copy-done.1, f32[2,128]{1,0:T(2,128)S(1)} %copy-done.4), custom_call_target="tpu_custom_call" | custom-call | tf_op jit(solution)/shard_map/enter/pallas_call | solution.py:49
  3.0 0.1 collective-permute-start
  3.1 8.0 %collective-permute-start.1 = (bf16[3,16,128]{2,1,0:T(8,128)(2,1)S(1)}, bf16[3,16,128]{2,1,0:T(8,128)(2,1)S(1)}, u32[]{:S(2)}, u32[]{:S(2)}) collective-permute-start(bf16[3,16,128]{2,1,0:T(8,128)(2,1)S(1)} %get-tuple-element.25), channel_id=1, source_target_pairs={{1,2},{3,4},{5,6},{7,8},{9,10},{11,12},{13,14},{15,16},{17,18},{19... | collective-permute-start | bytes 36872 | tf_op jit(solution)/shard_map/ppermute | solution.py:276
  11.1 2.8 %collective-permute-start.4 = (f32[4,128]{1,0:T(4,128)S(1)}, f32[4,128]{1,0:T(4,128)S(1)}, u32[]{:S(2)}, u32[]{:S(2)}) collective-permute-start(f32[4,128]{1,0:T(4,128)S(1)} %get-tuple-element.26.refs_3_), channel_id=1, source_target_pairs={{0,192},{64,128},{128,64},{192,0},{1,193},{65,129},{129,65},{193,1... | collective-permute-start | bytes 6152 | tf_op jit(solution)/shard_map/ppermute | solution.py:272
  14.0 0.8 %collective-permute-start.3 = (f32[4,128]{1,0:T(4,128)S(1)}, f32[4,128]{1,0:T(4,128)S(1)}, u32[]{:S(2)}, u32[]{:S(2)}) collective-permute-start(f32[4,128]{1,0:T(4,128)S(1)} %get-tuple-element.26.refs_3_), channel_id=1, source_target_pairs={{0,128},{64,192},{128,0},{192,64},{1,129},{65,193},{129,1},{193,65... | collective-permute-start | bytes 6152 | tf_op jit(solution)/shard_map/ppermute | solution.py:272
  14.8 0.5 collective-permute-start.2
  15.3 0.7 %collective-permute-done.4.refs_6_ = f32[4,128]{1,0:T(4,128)S(1)} collective-permute-done((f32[4,128]{1,0:T(4,128)S(1)}, f32[4,128]{1,0:T(4,128)S(1)}, u32[]{:S(2)}, u32[]{:S(2)}) %collective-permute-start.4) | collective-permute-done | bytes 2080 | tf_op jit(solution)/shard_map/ppermute | solution.py:272
  16.0 3.1 %collective-permute-done.3.refs_5_ = f32[4,128]{1,0:T(4,128)S(1)} collective-permute-done((f32[4,128]{1,0:T(4,128)S(1)}, f32[4,128]{1,0:T(4,128)S(1)}, u32[]{:S(2)}, u32[]{:S(2)}) %collective-permute-start.3) | collective-permute-done | bytes 2080 | tf_op jit(solution)/shard_map/ppermute | solution.py:272
  19.0 0.0 collective-permute-done.2.refs_4_
  19.0 0.0 collective-permute-done.refs_1_
  19.1 0.0 collective-permute-done.1.refs_2_
  19.1 0.0 copy-start
  19.1 1.0 %copy-done = bf16[3,3,128,128]{3,2,1,0:T(8,128)(2,1)S(1)} copy-done((bf16[3,3,128,128]{3,2,1,0:T(8,128)(2,1)S(1)}, bf16[3,3,128,128]{3,2,1,0:T(8,128)(2,1)}, u32[]{:S(2)}) %copy-start) | copy-done | bytes 294936
  20.0 0.0 copy-start.2
  20.0 0.8 %copy-done.2 = bf16[3,3,128,16]{2,3,1,0:T(8,128)(2,1)S(1)} copy-done((bf16[3,3,128,16]{2,3,1,0:T(8,128)(2,1)S(1)}, bf16[3,3,128,16]{2,3,1,0:T(8,128)(2,1)}, u32[]{:S(2)}) %copy-start.2) | copy-done | bytes 36888
  20.8 0.0 copy-start.3
  20.8 0.8 %copy-done.3 = bf16[3,3,16,128]{3,2,1,0:T(8,128)(2,1)S(1)} copy-done((bf16[3,3,16,128]{3,2,1,0:T(8,128)(2,1)S(1)}, bf16[3,3,16,128]{3,2,1,0:T(8,128)(2,1)}, u32[]{:S(2)}) %copy-start.3) | copy-done | bytes 36888
  21.6 4.4 %round0.1 = (f32[9,4,16,128]{3,2,1,0:T(8,128)S(1)}, bf16[7,3,16,128]{3,2,1,0:T(8,128)(2,1)S(1)}, bf16[7,3,16,128]{3,2,1,0:T(8,128)(2,1)S(1)}, bf16[384,256]{1,0:...) custom-call(f32[4,16,128]{2,1,0:T(8,128)S(1)} %get-tuple-element.23.refs_0_, ...), custom_call_target="tpu_custom_call" | custom-call | tf_op jit(solution)/shard_map/round0/pallas_call | solution.py:236
  26.0 0.1 collective-permute-start.5
  26.1 3.0 %collective-permute-start.6 = (bf16[7,3,16,128]{3,2,1,0:T(8,128)(2,1)S(1)}, bf16[7,3,16,128]{3,2,1,0:T(8,128)(2,1)S(1)}, u32[]{:S(2)}, u32[]{:S(2)}) collective-permute-start(bf16[7,3,16,128]{3,2,1,0:T(8,128)(2,1)S(1)} %get-tuple-element.28), channel_id=1, source_target_pairs={{1,2},{3,4},{5,6},{7,8},{9,10},{11,12},{13,14},{15,16},{17,18},{19... | collective-permute-start | bytes 258056 | tf_op jit(solution)/shard_map/ppermute | solution.py:276
  29.1 0.0 collective-permute-done.5.refs_1_
  29.1 4.9 %collective-permute-done.6.refs_2_ = bf16[7,3,16,128]{3,2,1,0:T(8,128)(2,1)S(1)} collective-permute-done((bf16[7,3,16,128]{3,2,1,0:T(8,128)(2,1)S(1)}, bf16[7,3,16,128]{3,2,1,0:T(8,128)(2,1)S(1)}, u32[]{:S(2)}, u32[]{:S(2)}) %collective-permute-start.6) | collective-permute-done | bytes 86048 | tf_op jit(solution)/shard_map/ppermute | solution.py:276
  34.0 4.0 %round1.1 = (f32[9,4,16,128]{3,2,1,0:T(8,128)S(1)}, bf16[6,3,16,128]{3,2,1,0:T(8,128)(2,1)S(1)}, bf16[6,3,16,128]{3,2,1,0:T(8,128)(2,1)S(1)}) custom-call(f32[4,16,128]{2,1,0:T(8,128)S(1)} %get-tuple-element.23.refs_0_, bf16[7,3,16,128]{3,2,1,0:T(8,128)(2,1)S(1)} %collective-permute-done.5.refs_1_, ...), custom_call_target="tpu_custom_call" | custom-call | tf_op jit(solution)/shard_map/round1/pallas_call | solution.py:236
  38.0 0.1 collective-permute-start.7
  38.1 3.2 %collective-permute-start.8 = (bf16[6,3,16,128]{3,2,1,0:T(8,128)(2,1)S(1)}, bf16[6,3,16,128]{3,2,1,0:T(8,128)(2,1)S(1)}, u32[]{:S(2)}, u32[]{:S(2)}) collective-permute-start(bf16[6,3,16,128]{3,2,1,0:T(8,128)(2,1)S(1)} %get-tuple-element.35), channel_id=1, source_target_pairs={{1,2},{3,4},{5,6},{7,8},{9,10},{11,12},{13,14},{15,16},{17,18},{19... | collective-permute-start | bytes 221192 | tf_op jit(solution)/shard_map/ppermute | solution.py:276
  41.3 0.0 collective-permute-done.7.refs_1_
  41.3 4.6 %collective-permute-done.8.refs_2_ = bf16[6,3,16,128]{3,2,1,0:T(8,128)(2,1)S(1)} collective-permute-done((bf16[6,3,16,128]{3,2,1,0:T(8,128)(2,1)S(1)}, bf16[6,3,16,128]{3,2,1,0:T(8,128)(2,1)S(1)}, u32[]{:S(2)}, u32[]{:S(2)}) %collective-permute-start.8) | collective-permute-done | bytes 73760 | tf_op jit(solution)/shard_map/ppermute | solution.py:276
  45.9 3.5 %round2.1 = (f32[32,4,128]{2,1,0:T(4,128)S(1)}, f32[32,4,128]{2,1,0:T(4,128)S(1)}, f32[32,4,128]{2,1,0:T(4,128)S(1)}, f32[32,4,128]{2,1,0:T(4,128)S(1)}) custom-call(f32[4,16,128]{2,1,0:T(8,128)S(1)} %get-tuple-element.23.refs_0_, bf16[6,3,16,128]{3,2,1,0:T(8,128)(2,1)S(1)} %collective-permute-done.7.refs_1_, ...), custom_call_target="tpu_custom_call" | custom-call | tf_op jit(solution)/shard_map/round2/pallas_call | solution.py:236
  49.3 0.3 collective-permute-start.9
  49.6 2.6 %collective-permute-start.10 = (f32[32,4,128]{2,1,0:T(4,128)S(1)}, f32[32,4,128]{2,1,0:T(4,128)S(1)}, u32[]{:S(2)}, u32[]{:S(2)}) collective-permute-start(f32[32,4,128]{2,1,0:T(4,128)S(1)} %get-tuple-element.39), channel_id=1, source_target_pairs={{0,128},{64,192},{128,0},{192,64},{1,129},{65,193},{129,1},{193,65... | collective-permute-start | bytes 196616 | tf_op jit(solution)/shard_map/ppermute | solution.py:272
  52.3 1.9 %collective-permute-start.11 = (f32[32,4,128]{2,1,0:T(4,128)S(1)}, f32[32,4,128]{2,1,0:T(4,128)S(1)}, u32[]{:S(2)}, u32[]{:S(2)}) collective-permute-start(f32[32,4,128]{2,1,0:T(4,128)S(1)} %get-tuple-element.40), channel_id=1, source_target_pairs={{0,192},{64,128},{128,64},{192,0},{1,193},{65,129},{129,65},{193,1... | collective-permute-start | bytes 196616 | tf_op jit(solution)/shard_map/ppermute | solution.py:272
  54.1 0.0 collective-permute-done.9.p1
  54.1 1.3 %collective-permute-done.10.p2 = f32[32,4,128]{2,1,0:T(4,128)S(1)} collective-permute-done((f32[32,4,128]{2,1,0:T(4,128)S(1)}, f32[32,4,128]{2,1,0:T(4,128)S(1)}, u32[]{:S(2)}, u32[]{:S(2)}) %collective-permute-start.10) | collective-permute-done | bytes 65568 | tf_op jit(solution)/shard_map/ppermute | solution.py:272
  55.4 2.3 %collective-permute-done.11.p3 = f32[32,4,128]{2,1,0:T(4,128)S(1)} collective-permute-done((f32[32,4,128]{2,1,0:T(4,128)S(1)}, f32[32,4,128]{2,1,0:T(4,128)S(1)}, u32[]{:S(2)}, u32[]{:S(2)}) %collective-permute-start.11) | collective-permute-done | bytes 65568 | tf_op jit(solution)/shard_map/ppermute | solution.py:272
  57.8 0.9 %join.1 = f32[32,4,448]{2,1,0:T(4,128)} custom-call(f32[32,4,128]{2,1,0:T(4,128)S(1)} %get-tuple-element.37.p0, f32[32,4,128]{2,1,0:T(4,128)S(1)} %collective-permute-done.9.p1, f32[32,4,128]{2,1,0:T(4,128)S(1)} %collective-permute-done.10.p2, f32[32,4,128]{2,1,0:T(4,128)S(1)} %collective-permute-done.11.p3), custom_call_target="tpu_custom_call" | custom-call | tf_op jit(solution)/shard_map/join/pallas_call | solution.py:261
Async XLA Ops:
  0.0 0.9 %copy-start.1 = (f32[16,4,448]{2,1,0:T(4,128)S(1)}, f32[16,4,448]{2,1,0:T(4,128)}, u32[]{:S(2)}) copy-start(f32[16,4,448]{2,1,0:T(4,128)} %latent.1) | copy-start | bytes 344068
  0.9 0.7 %copy-start.4 = (f32[2,128]{1,0:T(2,128)S(1)}, f32[2,128]{1,0:T(2,128)}, u32[]{:S(2)}) copy-start(f32[2,128]{1,0:T(2,128)} %embed.1) | copy-start | bytes 3076
  1.6 0.7 %copy-start.5 = (f32[2]{0:T(128)S(1)}, f32[2]{0:T(128)}, u32[]{:S(2)}) copy-start(f32[2]{0:T(128)} %step.1) | copy-start | bytes 28
  3.0 16.1 %collective-permute-start = (bf16[3,16,128]{2,1,0:T(8,128)(2,1)S(1)}, bf16[3,16,128]{2,1,0:T(8,128)(2,1)S(1)}, u32[]{:S(2)}, u32[]{:S(2)}) collective-permute-start(bf16[3,16,128]{2,1,0:T(8,128)(2,1)S(1)} %get-tuple-element.24), channel_id=1, source_target_pairs={{0,1},{2,3},{4,5},{6,7},{8,9},{10,11},{12,13},{14,15},{16,17},{18,... | collective-permute-start | bytes 36872 | tf_op jit(solution)/shard_map/ppermute | solution.py:276
  3.1 16.0 %collective-permute-start.1 = (bf16[3,16,128]{2,1,0:T(8,128)(2,1)S(1)}, bf16[3,16,128]{2,1,0:T(8,128)(2,1)S(1)}, u32[]{:S(2)}, u32[]{:S(2)}) collective-permute-start(bf16[3,16,128]{2,1,0:T(8,128)(2,1)S(1)} %get-tuple-element.25), channel_id=1, source_target_pairs={{1,2},{3,4},{5,6},{7,8},{9,10},{11,12},{13,14},{15,16},{17,18},{19... | collective-permute-start | bytes 36872 | tf_op jit(solution)/shard_map/ppermute | solution.py:276
  11.1 4.9 %collective-permute-start.4 = (f32[4,128]{1,0:T(4,128)S(1)}, f32[4,128]{1,0:T(4,128)S(1)}, u32[]{:S(2)}, u32[]{:S(2)}) collective-permute-start(f32[4,128]{1,0:T(4,128)S(1)} %get-tuple-element.26.refs_3_), channel_id=1, source_target_pairs={{0,192},{64,128},{128,64},{192,0},{1,193},{65,129},{129,65},{193,1... | collective-permute-start | bytes 6152 | tf_op jit(solution)/shard_map/ppermute | solution.py:272
  14.0 5.1 %collective-permute-start.3 = (f32[4,128]{1,0:T(4,128)S(1)}, f32[4,128]{1,0:T(4,128)S(1)}, u32[]{:S(2)}, u32[]{:S(2)}) collective-permute-start(f32[4,128]{1,0:T(4,128)S(1)} %get-tuple-element.26.refs_3_), channel_id=1, source_target_pairs={{0,128},{64,192},{128,0},{192,64},{1,129},{65,193},{129,1},{193,65... | collective-permute-start | bytes 6152 | tf_op jit(solution)/shard_map/ppermute | solution.py:272
  14.8 4.3 %collective-permute-start.2 = (f32[4,128]{1,0:T(4,128)S(1)}, f32[4,128]{1,0:T(4,128)S(1)}, u32[]{:S(2)}, u32[]{:S(2)}) collective-permute-start(f32[4,128]{1,0:T(4,128)S(1)} %get-tuple-element.26.refs_3_), channel_id=1, source_target_pairs={{0,64},{64,0},{128,192},{192,128},{1,65},{65,1},{129,193},{193,129... | collective-permute-start | bytes 6152 | tf_op jit(solution)/shard_map/ppermute | solution.py:272
  19.1 1.0 %copy-start = (bf16[3,3,128,128]{3,2,1,0:T(8,128)(2,1)S(1)}, bf16[3,3,128,128]{3,2,1,0:T(8,128)(2,1)}, u32[]{:S(2)}) copy-start(bf16[3,3,128,128]{3,2,1,0:T(8,128)(2,1)} %refs_8_.1) | copy-start | bytes 884740
  20.0 0.8 %copy-start.2 = (bf16[3,3,128,16]{2,3,1,0:T(8,128)(2,1)S(1)}, bf16[3,3,128,16]{2,3,1,0:T(8,128)(2,1)}, u32[]{:S(2)}) copy-start(bf16[3,3,128,16]{2,3,1,0:T(8,128)(2,1)} %param.9) | copy-start | bytes 110596
  20.8 0.8 %copy-start.3 = (bf16[3,3,16,128]{3,2,1,0:T(8,128)(2,1)S(1)}, bf16[3,3,16,128]{3,2,1,0:T(8,128)(2,1)}, u32[]{:S(2)}) copy-start(bf16[3,3,16,128]{3,2,1,0:T(8,128)(2,1)} %refs_9_.1) | copy-start | bytes 110596
  26.0 3.1 %collective-permute-start.5 = (bf16[7,3,16,128]{3,2,1,0:T(8,128)(2,1)S(1)}, bf16[7,3,16,128]{3,2,1,0:T(8,128)(2,1)S(1)}, u32[]{:S(2)}, u32[]{:S(2)}) collective-permute-start(bf16[7,3,16,128]{3,2,1,0:T(8,128)(2,1)S(1)} %get-tuple-element.27), channel_id=1, source_target_pairs={{0,1},{2,3},{4,5},{6,7},{8,9},{10,11},{12,13},{14,15},{16,17},{18,... | collective-permute-start | bytes 258056 | tf_op jit(solution)/shard_map/ppermute | solution.py:276
  26.1 7.9 %collective-permute-start.6 = (bf16[7,3,16,128]{3,2,1,0:T(8,128)(2,1)S(1)}, bf16[7,3,16,128]{3,2,1,0:T(8,128)(2,1)S(1)}, u32[]{:S(2)}, u32[]{:S(2)}) collective-permute-start(bf16[7,3,16,128]{3,2,1,0:T(8,128)(2,1)S(1)} %get-tuple-element.28), channel_id=1, source_target_pairs={{1,2},{3,4},{5,6},{7,8},{9,10},{11,12},{13,14},{15,16},{17,18},{19... | collective-permute-start | bytes 258056 | tf_op jit(solution)/shard_map/ppermute | solution.py:276
  38.0 3.3 %collective-permute-start.7 = (bf16[6,3,16,128]{3,2,1,0:T(8,128)(2,1)S(1)}, bf16[6,3,16,128]{3,2,1,0:T(8,128)(2,1)S(1)}, u32[]{:S(2)}, u32[]{:S(2)}) collective-permute-start(bf16[6,3,16,128]{3,2,1,0:T(8,128)(2,1)S(1)} %get-tuple-element.34), channel_id=1, source_target_pairs={{0,1},{2,3},{4,5},{6,7},{8,9},{10,11},{12,13},{14,15},{16,17},{18,... | collective-permute-start | bytes 221192 | tf_op jit(solution)/shard_map/ppermute | solution.py:276
  38.1 7.8 %collective-permute-start.8 = (bf16[6,3,16,128]{3,2,1,0:T(8,128)(2,1)S(1)}, bf16[6,3,16,128]{3,2,1,0:T(8,128)(2,1)S(1)}, u32[]{:S(2)}, u32[]{:S(2)}) collective-permute-start(bf16[6,3,16,128]{3,2,1,0:T(8,128)(2,1)S(1)} %get-tuple-element.35), channel_id=1, source_target_pairs={{1,2},{3,4},{5,6},{7,8},{9,10},{11,12},{13,14},{15,16},{17,18},{19... | collective-permute-start | bytes 221192 | tf_op jit(solution)/shard_map/ppermute | solution.py:276
  49.3 4.8 %collective-permute-start.9 = (f32[32,4,128]{2,1,0:T(4,128)S(1)}, f32[32,4,128]{2,1,0:T(4,128)S(1)}, u32[]{:S(2)}, u32[]{:S(2)}) collective-permute-start(f32[32,4,128]{2,1,0:T(4,128)S(1)} %get-tuple-element.38), channel_id=1, source_target_pairs={{0,64},{64,0},{128,192},{192,128},{1,65},{65,1},{129,193},{193,129... | collective-permute-start | bytes 196616 | tf_op jit(solution)/shard_map/ppermute | solution.py:272
  49.6 5.8 %collective-permute-start.10 = (f32[32,4,128]{2,1,0:T(4,128)S(1)}, f32[32,4,128]{2,1,0:T(4,128)S(1)}, u32[]{:S(2)}, u32[]{:S(2)}) collective-permute-start(f32[32,4,128]{2,1,0:T(4,128)S(1)} %get-tuple-element.39), channel_id=1, source_target_pairs={{0,128},{64,192},{128,0},{192,64},{1,129},{65,193},{129,1},{193,65... | collective-permute-start | bytes 196616 | tf_op jit(solution)/shard_map/ppermute | solution.py:272
  52.3 5.5 %collective-permute-start.11 = (f32[32,4,128]{2,1,0:T(4,128)S(1)}, f32[32,4,128]{2,1,0:T(4,128)S(1)}, u32[]{:S(2)}, u32[]{:S(2)}) collective-permute-start(f32[32,4,128]{2,1,0:T(4,128)S(1)} %get-tuple-element.40), channel_id=1, source_target_pairs={{0,192},{64,128},{128,64},{192,0},{1,193},{65,129},{129,65},{193,1... | collective-permute-start | bytes 196616 | tf_op jit(solution)/shard_map/ppermute | solution.py:272

commit v2 on v1

v2 whole, which is shorter than its diff:
```python
import functools

import jax
import jax.numpy as jnp
from jax import lax
from jax.experimental import pallas as pl
from jax.experimental.pallas import tpu as pltpu
from jax.sharding import PartitionSpec as P

TIMES = 8
C = 16
F = 128
L = 128
ROWS = 4
STARTS = (-1, 105, 215, 321)
SHIFTS = tuple(-start % L for start in STARTS)
CUTS = (114, 224, 334)
BF = jnp.bfloat16
F32 = jnp.float32


VM = pl.BlockSpec(memory_space=pltpu.VMEM)
ANY = pl.BlockSpec(memory_space=pl.ANY)


def by_tm(tm, values):
    return jnp.where(tm == 0, values[0], jnp.where(tm == 1, values[1], jnp.where(tm == 2, values[2], values[3])))


def enter_body(step, latent, embed, lat, to_a, to_b, small, step_s, latent_v, embed_v, sems):
    copies = [pltpu.make_async_copy(x, y, sems.at[i]) for i, (x, y) in enumerate(((latent, latent_v), (embed, embed_v), (step, step_s)))]
    for copy in copies:
        copy.start()
    for copy in copies:
        copy.wait()
    tm, core = lax.axis_index("tm"), lax.axis_index("pix") % 2
    shift = by_tm(tm, SHIFTS)
    lane = lax.broadcasted_iota(jnp.int32, (C, L), 1)
    for r in range(ROWS):
        tiles = [jnp.zeros((C, L), F32)] + [latent_v[:, r, g * L:(g + 1) * L] for g in range(3)]
        tiles.append(jnp.concatenate([latent_v[:, r, 3 * L:], jnp.zeros((C, 4 * L - 448), F32)], axis=1))
        left, right = by_tm(tm, tiles[:4]), by_tm(tm, tiles[1:])
        lat[r + core * (3 - 2 * r)] = jnp.where(lane < shift, pltpu.roll(left, shift, 1), pltpu.roll(right, shift, 1))
    for d in range(3):
        to_b[d] = lat[d].astype(BF)
        to_a[d] = lat[3 - d].astype(BF)
    small[0:2] = embed_v[...]
    for d in range(2):
        small[2 + d:3 + d] = jnp.full((1, F), step_s[d], F32)


def enter(step, latent, embed):
    sent = jax.ShapeDtypeStruct((3, C, L), BF)
    return pl.pallas_call(
        enter_body,
        out_shape=(jax.ShapeDtypeStruct((ROWS, C, L), F32), sent, sent, jax.ShapeDtypeStruct((4, F), F32)),
        in_specs=[ANY] * 3,
        out_specs=(VM,) * 4,
        scratch_shapes=[
            pltpu.SMEM((2,), F32),
            pltpu.VMEM((C, ROWS, 448), F32),
            pltpu.VMEM((2, F), F32),
            pltpu.SemaphoreType.DMA((3,)),
        ],
        compiler_params=pltpu.CompilerParams(vmem_limit_bytes=4 << 20),
        name="enter",
    )(step, latent, embed)


def prepare_body(conv_in, conv_mid, conv_out, w_in, w_mid, w_out, in_v, mid_v, out_v, turned, sems):
    copies = [pltpu.make_async_copy(x, y, sems.at[i]) for i, (x, y) in enumerate(((conv_in, in_v), (conv_mid, mid_v), (conv_out, out_v)))]
    for copy in copies:
        copy.start()
    core = lax.axis_index("pix") % 2
    w_mid[...] = jnp.zeros_like(w_mid)
    w_out[...] = jnp.zeros_like(w_out)
    turned[...] = jnp.zeros_like(turned)
    for copy in copies:
        copy.wait()
    for a in range(3):
        row = a + core * (2 - 2 * a)
        for b in range(3):
            mid = mid_v[row, b] * 0.5
            tail = out_v[row, b]
            head = in_v[row, b] * 0.5
            for q in range(2):
                w_mid[(b * 2 + q) * F:(b * 2 + q + 1) * F, (a + q) * F:(a + q + 1) * F] = mid
                w_out[q * 48 + b * C:q * 48 + (b + 1) * C, (a + q) * F:(a + q + 1) * F] = tail
                turned[(a + q) * 48 + b * C:(a + q) * 48 + (b + 1) * C, q * F:(q + 1) * F] = head
    w_in[:2 * F] = turned[...].astype(F32).T.astype(BF)
    w_in[2 * F:] = jnp.zeros((F, 2 * F), BF)


def prepare(conv_in, conv_mid, conv_out):
    shapes = ((3 * F, 2 * F), (7 * F, 4 * F), (96, 4 * F))
    return pl.pallas_call(
        prepare_body,
        out_shape=tuple(jax.ShapeDtypeStruct(shape, BF) for shape in shapes),
        in_specs=[ANY] * 3,
        out_specs=(VM,) * 3,
        scratch_shapes=[
            pltpu.VMEM((3, 3, C, F), BF),
            pltpu.VMEM((3, 3, F, F), BF),
            pltpu.VMEM((3, 3, C, F), BF),
            pltpu.VMEM((2 * F, 2 * F), BF),
            pltpu.SemaphoreType.DMA((3,)),
        ],
        compiler_params=pltpu.CompilerParams(vmem_limit_bytes=8 << 20),
        name="prepare",
    )(conv_in, conv_mid, conv_out)


def tables(tm, smalls, w_conv, w_in, steps, gathered):
    for k in range(4):
        gathered[tm ^ k] = smalls[k][...]
    embed = jnp.concatenate([gathered[t, 0:2] for t in range(4)], axis=0) * 0.5
    steps[...] = jnp.concatenate([gathered[t, 2:4] for t in range(4)], axis=0)
    high = embed.astype(BF).astype(F32)
    rest = embed - high
    middle = rest.astype(BF).astype(F32)
    tail = jnp.concatenate([jnp.zeros((64, F), F32), high, middle, rest - middle, jnp.zeros((40, F), F32)], axis=0)
    tail = tail.T.astype(BF)
    w_in[:, :F] = w_conv[:, :F]
    for q in range(2):
        w_in[q * F:(q + 1) * F, F:] = w_conv[q * F:(q + 1) * F, F:] + tail
    w_in[2 * F:, F:] = w_conv[2 * F:, F:]


def silu2(v):
    return v + v * jnp.tanh(v)


def groups_of(rounds):
    return [(t0, min(4, TIMES - t0)) for t0 in (rounds, rounds + 4)]


class Round:
    def __init__(self, rounds, lat, prior, halo, w_in, w_mid, low, hid, sec):
        self.rounds, self.lat, self.prior, self.halo = rounds, lat, prior, halo
        self.w_in, self.w_mid, self.low, self.hid, self.sec = w_in, w_mid, low, hid, sec
        pix, self.tm = lax.axis_index("pix"), lax.axis_index("tm")
        self.core = pix % 2
        self.inside = (pix > 0) & (pix < 63)
        self.groups = groups_of(rounds)
        lane = lax.broadcasted_iota(jnp.int32, (C, L), 1)
        self.column = jnp.where(((self.tm == 0) & (lane == 0)) | ((self.tm == 3) & (lane == L - 1)), 0.0, 1.0)

    def state(self, t, row):
        return self.lat[row] if self.rounds == 0 else self.prior[t, row]

    def fill(self, g, rows):
        t0, n = self.groups[g]
        rounds, column = self.rounds, self.column
        for w in rows:
            for i in range(n if rounds else 1):
                if 3 <= w < 7:
                    x = self.state(t0 + i, w - 3)
                else:
                    d = 2 - w if w < 3 else w - 7
                    x = self.halo[(t0 + i - rounds, d) if rounds else (d,)].astype(F32)
                x = x * column
                x = jnp.concatenate([pltpu.roll(x, 1, 1) * column, x, pltpu.roll(x, L - 1, 1) * column], axis=0).astype(BF)
                for lanes in ([i] if rounds else range(n)):
                    self.low[g][(w - rows[0]) * 48:(w - rows[0] + 1) * 48, lanes * L:(lanes + 1) * L] = x

    def hidden_pair(self, g, p, first_row):
        t0, n = self.groups[g]
        width = n * L
        r = lax.broadcasted_iota(jnp.int32, (64, width), 0)
        c = lax.broadcasted_iota(jnp.int32, (64, width), 1)
        edge = ((self.tm == 0) & ((c & 127) == 0)) | ((self.tm == 3) & ((c & 127) == L - 1))
        pick = jnp.where(((r & 7) == t0 + (c >> 7)) & (r < 24) & jnp.logical_not(edge), 1.0, 0.0).astype(BF)
        at = (2 * p - first_row) * 48
        rhs = jnp.concatenate([self.low[g][at:at + 192, :width], pick], axis=0)
        w = self.w_in[:2 * F]
        if p == 0:
            w = jnp.concatenate([self.w_in[pl.ds(self.block(q, 2), F), :] for q in range(2)], axis=0)
        v = silu2(jnp.dot(w, rhs, preferred_element_type=F32))
        self.hid(g, p)[:, :width] = v.astype(BF)

    def block(self, normal, zero):
        return pl.multiple_of(jnp.where(self.inside, normal * F, zero * F), F)

    def second_pair(self, g, p):
        _, n = self.groups[g]
        w = self.w_mid[:6 * F]
        if p == 0:
            blocks = []
            for b in range(3):
                blocks += [self.w_mid[pl.ds(self.block(2 * b, 6), F), :], self.w_mid[(2 * b + 1) * F:(2 * b + 2) * F]]
            w = jnp.concatenate(blocks, axis=0)
        for i0 in range(0, n, 2):
            lanes = slice(i0 * L, min(i0 + 2, n) * L)
            rhs = jnp.concatenate([self.hid(g, p)[:, lanes], self.hid(g, p + 1)[:, lanes]], axis=0)
            y = jnp.dot(w, rhs, preferred_element_type=F32)
            for i in range(i0, min(i0 + 2, n)):
                part = y[:, (i - i0) * L:(i - i0 + 1) * L]
                v = pltpu.roll(part[:2 * F], 1, 1) + part[2 * F:4 * F] + pltpu.roll(part[4 * F:], L - 1, 1)
                self.sec(g, p)[:, i * L:(i + 1) * L] = silu2(v).astype(BF)


def first_part(rounds, *refs):
    if rounds == 0:
        lat, from_a, *smalls = refs[:6]
        w_conv, w_mid, h0, h1, s0, s1, w_in, steps, low0, low1, h3_0, h3_1, gathered = refs[6:]
        tables(lax.axis_index("tm"), smalls, w_conv, w_in, steps, gathered)
        prior = None
    else:
        lat, from_a, prior, w_in, w_mid, h0, h1, s0, s1, low0, low1, h3_0, h3_1 = refs
    r = Round(rounds, lat, prior, from_a, w_in, w_mid, (low0, low1), lambda g, p: ((h0, h1), (h3_0, h3_1))[p - 2][g], lambda g, p: (s0, s1)[g])
    rows = list(range(4, 10))
    for g in range(2):
        r.fill(g, rows)
        r.hidden_pair(g, 2, 4)
        r.hidden_pair(g, 3, 4)
    for g in range(2):
        r.second_pair(g, 2)


def second_part(rounds, *refs):
    lat, from_b = refs[:2]
    prior = refs[2] if rounds else None
    h0, h1, s0, s1, w_in, w_mid, w_out, steps, *rest = refs[3 if rounds else 2:]
    last = rounds == 2
    if last:
        out, rest = rest[:4], rest[4:]
        ready = rest.pop()
    else:
        nxt, to_a, to_b, *rest = rest
    low, hid, sec = rest[:2], rest[2:6], rest[6:10]
    r = Round(rounds, lat, prior, from_b, w_in, w_mid, low, lambda g, p: hid[g * 2 + p] if p < 2 else (h0, h1)[g], lambda g, p: sec[g * 2 + p] if p < 2 else (s0, s1)[g])
    core, tm, column = r.core, r.tm, r.column

    def keep(t, row, value):
        ready[pl.ds(((t // 2) ^ tm) * 128 + (t % 2) * 64 + row + core * (3 - 2 * row), C, stride=ROWS), :] = value

    totals = [jnp.zeros((C, L), F32) if rounds == 0 else prior[0, row] for row in range(ROWS)]

    def out_pair(g, p):
        t0, n = r.groups[g]
        width = n * L
        rhs = jnp.concatenate([r.sec(g, p)[:, :width], r.sec(g, p + 1)[:, :width]], axis=0)
        y = jnp.dot(w_out[...], rhs, preferred_element_type=F32)
        for q in range(2):
            row = 2 * p + q
            for i in range(n):
                t = t0 + i
                part = y[q * 48:(q + 1) * 48, i * L:(i + 1) * L]
                conv = pltpu.roll(part[:C] * column, 1, 1) + part[C:2 * C] + pltpu.roll(part[2 * C:] * column, L - 1, 1)
                totals[row] = totals[row] + steps[t:t + 1] * (r.state(t, row) + conv)
                value = lat[row] + totals[row]
                if last:
                    keep(t, row, value)
                else:
                    nxt[t + 1, row] = value
                    if t == rounds:
                        nxt[0, row] = totals[row]
                    if t < TIMES - 1 and row < 3:
                        to_b[t - rounds, row] = value.astype(BF)
                    if t < TIMES - 1 and row > 0:
                        to_a[t - rounds, 3 - row] = value.astype(BF)

    rows = list(range(6))
    r.fill(0, rows)
    r.hidden_pair(0, 0, 0)
    r.hidden_pair(0, 1, 0)
    r.fill(1, rows)
    r.second_pair(0, 1)
    r.hidden_pair(1, 1, 0)
    r.second_pair(0, 0)
    r.hidden_pair(1, 0, 0)
    out_pair(0, 1)
    out_pair(0, 0)
    r.second_pair(1, 1)
    out_pair(1, 1)
    r.second_pair(1, 0)
    out_pair(1, 0)

    for row in range(ROWS):
        if rounds == 1:
            nxt[1, row] = prior[1, row]
        if last:
            for t in range(2):
                keep(t, row, prior[t + 1, row])
    if last:
        for k in range(4):
            out[k][...] = ready[k * 128:(k + 1) * 128].reshape(32, ROWS, L)


def call(body, rounds, args, out_shape, scratch):
    return pl.pallas_call(
        functools.partial(body, rounds),
        out_shape=out_shape,
        in_specs=[VM] * len(args),
        out_specs=(VM,) * len(out_shape),
        scratch_shapes=scratch,
        compiler_params=pltpu.CompilerParams(vmem_limit_bytes=24 << 20),
    )(*args)


PAIR = (2 * F, 4 * L)
LOW = [pltpu.VMEM((288, 4 * L), BF)] * 2


def run_first(rounds, *args):
    out_shape = (jax.ShapeDtypeStruct(PAIR, BF),) * 4
    scratch = LOW + [pltpu.VMEM(PAIR, BF)] * 2
    if rounds == 0:
        out_shape += (jax.ShapeDtypeStruct((3 * F, 2 * F), BF), jax.ShapeDtypeStruct((TIMES, F), F32))
        scratch += [pltpu.VMEM((4, 4, F), F32)]
    return call(first_part, rounds, args, out_shape, scratch)


def run_second(rounds, *args):
    scratch = LOW + [pltpu.VMEM(PAIR, BF)] * 8
    if rounds == 2:
        out_shape = (jax.ShapeDtypeStruct((32, ROWS, L), F32),) * 4
        scratch += [pltpu.VMEM((512, L), F32)]
    else:
        sent = jax.ShapeDtypeStruct((TIMES - 1 - rounds, 3, C, L), BF)
        out_shape = (jax.ShapeDtypeStruct((TIMES + 1, ROWS, C, L), F32), sent, sent)
    return call(second_part, rounds, args, out_shape, scratch)


def join_body(p0, p1, p2, p3, out):
    tm = lax.axis_index("tm")
    pieces = [p0[...], p1[...], p2[...], p3[...]]
    lane = lax.broadcasted_iota(jnp.int32, pieces[0].shape, 2)
    placed = []
    for t in range(4):
        x = by_tm(t ^ tm, pieces)
        placed.append(pltpu.roll(x, STARTS[t] % L, 2))
    for g in range(3):
        out[:, :, g * L:(g + 1) * L] = jnp.where(lane < CUTS[g] - g * L, placed[g], placed[g + 1])
    out[:, :, 3 * L:] = placed[3][:, :, :448 - 3 * L]


def join(pieces):
    return pl.pallas_call(
        join_body,
        out_shape=jax.ShapeDtypeStruct((32, ROWS, 448), F32),
        in_specs=[VM] * 4,
        out_specs=VM,
        compiler_params=pltpu.CompilerParams(vmem_limit_bytes=8 << 20),
        name="join",
    )(*pieces)


def across(x, k):
    return lax.ppermute(x, "tm", [(t, t ^ k) for t in range(4)])


def pair_up(x, pairs):
    return lax.ppermute(x, "pix", [(a, b) for a, b in pairs] + [(b, a) for a, b in pairs])


CORES = [(2 * k, 2 * k + 1) for k in range(32)]
CHIPS = [(2 * k + 1, 2 * k + 2) for k in range(31)]


def shards(latent, step_size, time_embed, conv_in, conv_mid, conv_out):
    lat, to_a, to_b, small = enter(step_size, latent, time_embed)
    smalls = [small]
    for k in (1, 2, 3):
        smalls.append(across(small, k))
    w_conv, w_mid, w_out = prepare(conv_in.transpose(0, 1, 3, 2), conv_mid, conv_out)
    prior = ()
    for rounds in range(3):
        from_b = pair_up(to_b, CHIPS)
        from_a = pair_up(to_a, CORES)
        if rounds == 0:
            *kept, w_in, steps = run_first(0, lat, from_a, *smalls, w_conv, w_mid)
        else:
            kept = run_first(rounds, lat, from_a, *prior, w_in, w_mid)
        done = run_second(rounds, lat, from_b, *prior, *kept, w_in, w_mid, w_out, steps)
        if rounds < 2:
            *prior, to_a, to_b = done
    got = [done[0]] + [across(done[k], k) for k in (1, 2, 3)]
    return join(got).reshape(2, C, ROWS, 448)


def solution(mesh):
    in_specs = (P(None, "pix", None), P("tm"), P("tm", None), P(), P(), P())
    out_specs = P("tm", None, "pix", None)
    return jax.shard_map(shards, mesh=mesh, in_specs=in_specs, out_specs=out_specs, check_vma=False)
```

time: 59 us -> 56.8 us (0.963)
  waiting for transfers between devices: 16.9 us -> 12.8 us
  Pallas kernels: 13.5 us -> 17 us
  local copies, waits for them, and re-layouts: 4.73 us -> 3.21 us
    pallas_call x3 -> x7, Pallas kernels: 11.9 us -> 15.2 us  [the longest x6 14.7 us: call(): pl.pallas_call(functools.partial(body, rounds), out_shape=out_shape, in_s...]
    ppermute x6, waiting for transfers between devices: 9.48 us -> 6.82 us  [pair_up(): lax.ppermute(x, 'pix', [(a, b) for a, b in pairs] + [(b, a) for a, b in p...]
    unnamed x12, local copies, waits for them, and re-layouts: 4.73 us -> 3.21 us
    ppermute x6, waiting for transfers between devices: 7.38 us -> 5.94 us  [across(): return lax.ppermute(x, 'tm', [(t, t ^ k) for t in range(4)])]
  transfers between devices with their start and end apart: 12 -> 12, of which waited for: 6 -> 5; matrix products, arithmetic and copies ran while one was open for 0% -> 0% of each run, Pallas kernels for 0% -> 8%
where the time goes in v2:
time: 56.8 us; the launch traced here: 56.6 us
  starting transfers between devices  23.5 us (41%)
  Pallas kernels  17 us (30%)
  waiting for transfers between devices  12.8 us (23%)
  local copies, waits for them, and re-layouts  3.21 us (6%)
    pallas_call x6, Pallas kernels, call(): pl.pallas_call(functools.partial(body, rounds), out_shape=out_shape, in_s...  14.7 us
    ppermute x6, starting transfers between devices, pair_up(): lax.ppermute(x, 'pix', [(a, b) for a, b in pairs] + [(b, a) for a, b in p...  14.5 us
    ppermute x6, starting transfers between devices, across(): return lax.ppermute(x, 'tm', [(t, t ^ k) for t in range(4)])  8.97 us
    ppermute x6, waiting for transfers between devices, pair_up(): lax.ppermute(x, 'pix', [(a, b) for a, b in pairs] + [(b, a) for a, b in p...  6.82 us
    ppermute x6, waiting for transfers between devices, across(): return lax.ppermute(x, 'tm', [(t, t ^ k) for t in range(4)])  5.94 us
    unnamed x12, local copies, waits for them, and re-layouts  3.21 us
  transfers between devices with their start and end apart: 12, of which 5 were waited for; matrix products, arithmetic and copies ran while one was open for 0% of the time, Pallas kernels for 8%

profile of v2, /device:TPU:24, one launch (start us, length us, event | category | flops | bytes accessed | tf_op | source)
XLA Modules:
  0.0 56.6 jit_solution(1311331513412920)
XLA Ops:
  0.0 0.0 copy-start.1
  0.0 0.9 %copy-done.1 = f32[16,4,448]{2,1,0:T(4,128)S(1)} copy-done((f32[16,4,448]{2,1,0:T(4,128)S(1)}, f32[16,4,448]{2,1,0:T(4,128)}, u32[]{:S(2)}) %copy-start.1) | copy-done | bytes 114712
  0.9 0.0 copy-start.4
  0.9 0.7 %copy-done.4 = f32[2,128]{1,0:T(2,128)S(1)} copy-done((f32[2,128]{1,0:T(2,128)S(1)}, f32[2,128]{1,0:T(2,128)}, u32[]{:S(2)}) %copy-start.4) | copy-done | bytes 1048
  1.6 0.0 copy-start.5
  1.6 0.7 %copy-done.5 = f32[2]{0:T(128)S(1)} copy-done((f32[2]{0:T(128)S(1)}, f32[2]{0:T(128)}, u32[]{:S(2)}) %copy-start.5) | copy-done | bytes 32
  2.2 0.0 copy-start.2
  2.2 0.0 copy-start.3
  2.2 0.9 %enter.1 = (f32[4,16,128]{2,1,0:T(8,128)S(1)}, bf16[3,16,128]{2,1,0:T(8,128)(2,1)S(1)}, bf16[3,16,128]{2,1,0:T(8,128)(2,1)S(1)}, f32[4,128]{1,0:T(4,128)S(1)}) custom-call(f32[2]{0:T(128)S(1)} %copy-done.5, f32[16,4,448]{2,1,0:T(4,128)S(1)} %copy-done.1, f32[2,128]{1,0:T(2,128)S(1)} %copy-done.4), custom_call_target="tpu_custom_call" | custom-call | tf_op jit(solution)/shard_map/enter/pallas_call | solution.py:54
  3.2 0.1 collective-permute-start.1
  3.3 8.0 %collective-permute-start = (bf16[3,16,128]{2,1,0:T(8,128)(2,1)S(1)}, bf16[3,16,128]{2,1,0:T(8,128)(2,1)S(1)}, u32[]{:S(2)}, u32[]{:S(2)}) collective-permute-start(bf16[3,16,128]{2,1,0:T(8,128)(2,1)S(1)} %get-tuple-element.37), channel_id=1, source_target_pairs={{1,2},{3,4},{5,6},{7,8},{9,10},{11,12},{13,14},{15,16},{17,18},{19... | collective-permute-start | bytes 36872 | tf_op jit(solution)/shard_map/ppermute | solution.py:354
  11.3 2.8 %collective-permute-start.4 = (f32[4,128]{1,0:T(4,128)S(1)}, f32[4,128]{1,0:T(4,128)S(1)}, u32[]{:S(2)}, u32[]{:S(2)}) collective-permute-start(f32[4,128]{1,0:T(4,128)S(1)} %get-tuple-element.39.refs_2_), channel_id=1, source_target_pairs={{0,192},{64,128},{128,64},{192,0},{1,193},{65,129},{129,65},{193,1... | collective-permute-start | bytes 6152 | tf_op jit(solution)/shard_map/ppermute | solution.py:350
  14.2 0.8 %collective-permute-start.3 = (f32[4,128]{1,0:T(4,128)S(1)}, f32[4,128]{1,0:T(4,128)S(1)}, u32[]{:S(2)}, u32[]{:S(2)}) collective-permute-start(f32[4,128]{1,0:T(4,128)S(1)} %get-tuple-element.39.refs_2_), channel_id=1, source_target_pairs={{0,128},{64,192},{128,0},{192,64},{1,129},{65,193},{129,1},{193,65... | collective-permute-start | bytes 6152 | tf_op jit(solution)/shard_map/ppermute | solution.py:350
  15.0 0.5 collective-permute-start.2
  15.5 0.0 copy-done.2
  15.5 0.0 copy-done.3
  15.5 0.0 copy-start
  15.5 1.0 %copy-done = bf16[3,3,128,128]{3,2,1,0:T(8,128)(2,1)S(1)} copy-done((bf16[3,3,128,128]{3,2,1,0:T(8,128)(2,1)S(1)}, bf16[3,3,128,128]{3,2,1,0:T(8,128)(2,1)}, u32[]{:S(2)}) %copy-start) | copy-done | bytes 294936
  16.5 0.5 prepare.1
  16.9 0.0 collective-permute-done.4.refs_5_
  16.9 2.3 %collective-permute-done.3.refs_4_ = f32[4,128]{1,0:T(4,128)S(1)} collective-permute-done((f32[4,128]{1,0:T(4,128)S(1)}, f32[4,128]{1,0:T(4,128)S(1)}, u32[]{:S(2)}, u32[]{:S(2)}) %collective-permute-start.3) | collective-permute-done | bytes 2080 | tf_op jit(solution)/shard_map/ppermute | solution.py:350
  19.3 0.0 collective-permute-done.2.refs_3_
  19.3 0.0 collective-permute-done.1.refs_1_
  19.3 1.5 %shard_map.64 = (bf16[256,512]{1,0:T(8,128)(2,1)S(1)}, bf16[256,512]{1,0:T(8,128)(2,1)S(1)}, bf16[256,512]{1,0:T(8,128)(2,1)S(1)}, bf16[256,512]{1,0:T(8,128)(2,...) custom-call(f32[4,16,128]{2,1,0:T(8,128)S(1)} %get-tuple-element.36.refs_0_, ...), custom_call_target="tpu_custom_call" | custom-call | tf_op jit(solution)/shard_map/pallas_call | solution.py:291
  20.8 0.0 collective-permute-done.refs_1_
  20.8 3.6 %shard_map.65 = (f32[9,4,16,128]{3,2,1,0:T(8,128)S(1)}, bf16[7,3,16,128]{3,2,1,0:T(8,128)(2,1)S(1)}, bf16[7,3,16,128]{3,2,1,0:T(8,128)(2,1)S(1)}) custom-call(f32[4,16,128]{2,1,0:T(8,128)S(1)} %get-tuple-element.36.refs_0_, bf16[3,16,128]{2,1,0:T(8,128)(2,1)S(1)} %collective-permute-done.refs_1_, bf16[256,512]{1,0:T(8,128)(2,1)S(1)} %get-tuple-element.42.refs_2_, ...), custom_call_target="tpu_custom_call" | custom-call | tf_op jit(solution)/shard_map/pallas_call | solution.py:291
  24.4 0.1 collective-permute-start.6
  24.5 3.0 %collective-permute-start.5 = (bf16[7,3,16,128]{3,2,1,0:T(8,128)(2,1)S(1)}, bf16[7,3,16,128]{3,2,1,0:T(8,128)(2,1)S(1)}, u32[]{:S(2)}, u32[]{:S(2)}) collective-permute-start(bf16[7,3,16,128]{3,2,1,0:T(8,128)(2,1)S(1)} %get-tuple-element.49), channel_id=1, source_target_pairs={{1,2},{3,4},{5,6},{7,8},{9,10},{11,12},{13,14},{15,16},{17,18},{19... | collective-permute-start | bytes 258056 | tf_op jit(solution)/shard_map/ppermute | solution.py:354
  27.5 0.0 collective-permute-done.6.refs_1_
  27.5 1.5 %shard_map.66 = (bf16[256,512]{1,0:T(8,128)(2,1)S(1)}, bf16[256,512]{1,0:T(8,128)(2,1)S(1)}, bf16[256,512]{1,0:T(8,128)(2,1)S(1)}, bf16[256,512]{1,0:T(8,128)(2,1)S(1)}) custom-call(f32[4,16,128]{2,1,0:T(8,128)S(1)} %get-tuple-element.36.refs_0_, bf16[7,3,16,128]{3,2,1,0:T(8,128)(2,1)S(1)} %collective-permute-done.6.refs_1_, ...), custom_call_target="tpu_custom_call" | custom-call | tf_op jit(solution)/shard_map/pallas_call | solution.py:291
  29.1 3.4 %collective-permute-done.5.refs_1_ = bf16[7,3,16,128]{3,2,1,0:T(8,128)(2,1)S(1)} collective-permute-done((bf16[7,3,16,128]{3,2,1,0:T(8,128)(2,1)S(1)}, bf16[7,3,16,128]{3,2,1,0:T(8,128)(2,1)S(1)}, u32[]{:S(2)}, u32[]{:S(2)}) %collective-permute-start.5) | collective-permute-done | bytes 86048 | tf_op jit(solution)/shard_map/ppermute | solution.py:354
  32.4 3.5 %shard_map.67 = (f32[9,4,16,128]{3,2,1,0:T(8,128)S(1)}, bf16[6,3,16,128]{3,2,1,0:T(8,128)(2,1)S(1)}, bf16[6,3,16,128]{3,2,1,0:T(8,128)(2,1)S(1)}) custom-call(f32[4,16,128]{2,1,0:T(8,128)S(1)} %get-tuple-element.36.refs_0_, bf16[7,3,16,128]{3,2,1,0:T(8,128)(2,1)S(1)} %collective-permute-done.5.refs_1_, f32[9,4,16,128]{3,2,1,0:T(8,128)S(1)} %get-tuple-element.50.refs_2_, ...), custom_call_target="tpu_custom_call" | custom-call | tf_op jit(solution)/shard_map/pallas_call | solution.py:291
  36.0 0.3 collective-permute-start.8
  36.2 3.0 %collective-permute-start.7 = (bf16[6,3,16,128]{3,2,1,0:T(8,128)(2,1)S(1)}, bf16[6,3,16,128]{3,2,1,0:T(8,128)(2,1)S(1)}, u32[]{:S(2)}, u32[]{:S(2)}) collective-permute-start(bf16[6,3,16,128]{3,2,1,0:T(8,128)(2,1)S(1)} %get-tuple-element.56), channel_id=1, source_target_pairs={{1,2},{3,4},{5,6},{7,8},{9,10},{11,12},{13,14},{15,16},{17,18},{19... | collective-permute-start | bytes 221192 | tf_op jit(solution)/shard_map/ppermute | solution.py:354
  39.2 0.0 collective-permute-done.8.refs_1_
  39.3 1.3 %shard_map.68 = (bf16[256,512]{1,0:T(8,128)(2,1)S(1)}, bf16[256,512]{1,0:T(8,128)(2,1)S(1)}, bf16[256,512]{1,0:T(8,128)(2,1)S(1)}, bf16[256,512]{1,0:T(8,128)(2,1)S(1)}) custom-call(f32[4,16,128]{2,1,0:T(8,128)S(1)} %get-tuple-element.36.refs_0_, bf16[6,3,16,128]{3,2,1,0:T(8,128)(2,1)S(1)} %collective-permute-done.8.refs_1_, ...), custom_call_target="tpu_custom_call" | custom-call | tf_op jit(solution)/shard_map/pallas_call | solution.py:291
  40.6 3.5 %collective-permute-done.7.refs_1_ = bf16[6,3,16,128]{3,2,1,0:T(8,128)(2,1)S(1)} collective-permute-done((bf16[6,3,16,128]{3,2,1,0:T(8,128)(2,1)S(1)}, bf16[6,3,16,128]{3,2,1,0:T(8,128)(2,1)S(1)}, u32[]{:S(2)}, u32[]{:S(2)}) %collective-permute-start.7) | collective-permute-done | bytes 73760 | tf_op jit(solution)/shard_map/ppermute | solution.py:354
  44.0 3.3 %shard_map.69 = (f32[32,4,128]{2,1,0:T(4,128)S(1)}, f32[32,4,128]{2,1,0:T(4,128)S(1)}, f32[32,4,128]{2,1,0:T(4,128)S(1)}, f32[32,4,128]{2,1,0:T(4,128)S(1)}) custom-call(f32[4,16,128]{2,1,0:T(8,128)S(1)} %get-tuple-element.36.refs_0_, bf16[6,3,16,128]{3,2,1,0:T(8,128)(2,1)S(1)} %collective-permute-done.7.refs_1_, ...), custom_call_target="tpu_custom_call" | custom-call | tf_op jit(solution)/shard_map/pallas_call | solution.py:291
  47.3 0.3 collective-permute-start.9
  47.6 2.6 %collective-permute-start.10 = (f32[32,4,128]{2,1,0:T(4,128)S(1)}, f32[32,4,128]{2,1,0:T(4,128)S(1)}, u32[]{:S(2)}, u32[]{:S(2)}) collective-permute-start(f32[32,4,128]{2,1,0:T(4,128)S(1)} %get-tuple-element.65), channel_id=1, source_target_pairs={{0,128},{64,192},{128,0},{192,64},{1,129},{65,193},{129,1},{193,65... | collective-permute-start | bytes 196616 | tf_op jit(solution)/shard_map/ppermute | solution.py:350
  50.2 1.9 %collective-permute-start.11 = (f32[32,4,128]{2,1,0:T(4,128)S(1)}, f32[32,4,128]{2,1,0:T(4,128)S(1)}, u32[]{:S(2)}, u32[]{:S(2)}) collective-permute-start(f32[32,4,128]{2,1,0:T(4,128)S(1)} %get-tuple-element.66), channel_id=1, source_target_pairs={{0,192},{64,128},{128,64},{192,0},{1,193},{65,129},{129,65},{193,1... | collective-permute-start | bytes 196616 | tf_op jit(solution)/shard_map/ppermute | solution.py:350
  52.1 0.0 collective-permute-done.9.p1
  52.1 1.3 %collective-permute-done.10.p2 = f32[32,4,128]{2,1,0:T(4,128)S(1)} collective-permute-done((f32[32,4,128]{2,1,0:T(4,128)S(1)}, f32[32,4,128]{2,1,0:T(4,128)S(1)}, u32[]{:S(2)}, u32[]{:S(2)}) %collective-permute-start.10) | collective-permute-done | bytes 65568 | tf_op jit(solution)/shard_map/ppermute | solution.py:350
  53.4 2.3 %collective-permute-done.11.p3 = f32[32,4,128]{2,1,0:T(4,128)S(1)} collective-permute-done((f32[32,4,128]{2,1,0:T(4,128)S(1)}, f32[32,4,128]{2,1,0:T(4,128)S(1)}, u32[]{:S(2)}, u32[]{:S(2)}) %collective-permute-start.11) | collective-permute-done | bytes 65568 | tf_op jit(solution)/shard_map/ppermute | solution.py:350
  55.7 0.9 %join.1 = f32[32,4,448]{2,1,0:T(4,128)} custom-call(f32[32,4,128]{2,1,0:T(4,128)S(1)} %get-tuple-element.63.p0, f32[32,4,128]{2,1,0:T(4,128)S(1)} %collective-permute-done.9.p1, f32[32,4,128]{2,1,0:T(4,128)S(1)} %collective-permute-done.10.p2, f32[32,4,128]{2,1,0:T(4,128)S(1)} %collective-permute-done.11.p3), custom_call_target="tpu_custom_call" | custom-call | tf_op jit(solution)/shard_map/join/pallas_call | solution.py:339
Async XLA Ops:
  0.0 0.9 %copy-start.1 = (f32[16,4,448]{2,1,0:T(4,128)S(1)}, f32[16,4,448]{2,1,0:T(4,128)}, u32[]{:S(2)}) copy-start(f32[16,4,448]{2,1,0:T(4,128)} %latent.1) | copy-start | bytes 344068
  0.9 0.7 %copy-start.4 = (f32[2,128]{1,0:T(2,128)S(1)}, f32[2,128]{1,0:T(2,128)}, u32[]{:S(2)}) copy-start(f32[2,128]{1,0:T(2,128)} %embed.1) | copy-start | bytes 3076
  1.6 0.7 %copy-start.5 = (f32[2]{0:T(128)S(1)}, f32[2]{0:T(128)}, u32[]{:S(2)}) copy-start(f32[2]{0:T(128)} %step.1) | copy-start | bytes 28
  2.2 13.3 %copy-start.2 = (bf16[3,3,128,16]{2,3,1,0:T(8,128)(2,1)S(1)}, bf16[3,3,128,16]{2,3,1,0:T(8,128)(2,1)}, u32[]{:S(2)}) copy-start(bf16[3,3,128,16]{2,3,1,0:T(8,128)(2,1)} %param.9) | copy-start | bytes 110596
  2.2 13.3 %copy-start.3 = (bf16[3,3,16,128]{3,2,1,0:T(8,128)(2,1)S(1)}, bf16[3,3,16,128]{3,2,1,0:T(8,128)(2,1)}, u32[]{:S(2)}) copy-start(bf16[3,3,16,128]{3,2,1,0:T(8,128)(2,1)} %conv_out.1) | copy-start | bytes 110596
  3.2 16.1 %collective-permute-start.1 = (bf16[3,16,128]{2,1,0:T(8,128)(2,1)S(1)}, bf16[3,16,128]{2,1,0:T(8,128)(2,1)S(1)}, u32[]{:S(2)}, u32[]{:S(2)}) collective-permute-start(bf16[3,16,128]{2,1,0:T(8,128)(2,1)S(1)} %get-tuple-element.38), channel_id=1, source_target_pairs={{0,1},{2,3},{4,5},{6,7},{8,9},{10,11},{12,13},{14,15},{16,17},{18,... | collective-permute-start | bytes 36872 | tf_op jit(solution)/shard_map/ppermute | solution.py:354
  3.3 17.5 %collective-permute-start = (bf16[3,16,128]{2,1,0:T(8,128)(2,1)S(1)}, bf16[3,16,128]{2,1,0:T(8,128)(2,1)S(1)}, u32[]{:S(2)}, u32[]{:S(2)}) collective-permute-start(bf16[3,16,128]{2,1,0:T(8,128)(2,1)S(1)} %get-tuple-element.37), channel_id=1, source_target_pairs={{1,2},{3,4},{5,6},{7,8},{9,10},{11,12},{13,14},{15,16},{17,18},{19... | collective-permute-start | bytes 36872 | tf_op jit(solution)/shard_map/ppermute | solution.py:354
  11.3 5.6 %collective-permute-start.4 = (f32[4,128]{1,0:T(4,128)S(1)}, f32[4,128]{1,0:T(4,128)S(1)}, u32[]{:S(2)}, u32[]{:S(2)}) collective-permute-start(f32[4,128]{1,0:T(4,128)S(1)} %get-tuple-element.39.refs_2_), channel_id=1, source_target_pairs={{0,192},{64,128},{128,64},{192,0},{1,193},{65,129},{129,65},{193,1... | collective-permute-start | bytes 6152 | tf_op jit(solution)/shard_map/ppermute | solution.py:350
  14.2 5.1 %collective-permute-start.3 = (f32[4,128]{1,0:T(4,128)S(1)}, f32[4,128]{1,0:T(4,128)S(1)}, u32[]{:S(2)}, u32[]{:S(2)}) collective-permute-start(f32[4,128]{1,0:T(4,128)S(1)} %get-tuple-element.39.refs_2_), channel_id=1, source_target_pairs={{0,128},{64,192},{128,0},{192,64},{1,129},{65,193},{129,1},{193,65... | collective-permute-start | bytes 6152 | tf_op jit(solution)/shard_map/ppermute | solution.py:350
  15.0 4.3 %collective-permute-start.2 = (f32[4,128]{1,0:T(4,128)S(1)}, f32[4,128]{1,0:T(4,128)S(1)}, u32[]{:S(2)}, u32[]{:S(2)}) collective-permute-start(f32[4,128]{1,0:T(4,128)S(1)} %get-tuple-element.39.refs_2_), channel_id=1, source_target_pairs={{0,64},{64,0},{128,192},{192,128},{1,65},{65,1},{129,193},{193,129... | collective-permute-start | bytes 6152 | tf_op jit(solution)/shard_map/ppermute | solution.py:350
  15.5 1.0 %copy-start = (bf16[3,3,128,128]{3,2,1,0:T(8,128)(2,1)S(1)}, bf16[3,3,128,128]{3,2,1,0:T(8,128)(2,1)}, u32[]{:S(2)}) copy-start(bf16[3,3,128,128]{3,2,1,0:T(8,128)(2,1)} %conv_mid.1) | copy-start | bytes 884740
  24.4 3.1 %collective-permute-start.6 = (bf16[7,3,16,128]{3,2,1,0:T(8,128)(2,1)S(1)}, bf16[7,3,16,128]{3,2,1,0:T(8,128)(2,1)S(1)}, u32[]{:S(2)}, u32[]{:S(2)}) collective-permute-start(bf16[7,3,16,128]{3,2,1,0:T(8,128)(2,1)S(1)} %get-tuple-element.51), channel_id=1, source_target_pairs={{0,1},{2,3},{4,5},{6,7},{8,9},{10,11},{12,13},{14,15},{16,17},{18,... | collective-permute-start | bytes 258056 | tf_op jit(solution)/shard_map/ppermute | solution.py:354
  24.5 7.9 %collective-permute-start.5 = (bf16[7,3,16,128]{3,2,1,0:T(8,128)(2,1)S(1)}, bf16[7,3,16,128]{3,2,1,0:T(8,128)(2,1)S(1)}, u32[]{:S(2)}, u32[]{:S(2)}) collective-permute-start(bf16[7,3,16,128]{3,2,1,0:T(8,128)(2,1)S(1)} %get-tuple-element.49), channel_id=1, source_target_pairs={{1,2},{3,4},{5,6},{7,8},{9,10},{11,12},{13,14},{15,16},{17,18},{19... | collective-permute-start | bytes 258056 | tf_op jit(solution)/shard_map/ppermute | solution.py:354
  36.0 3.3 %collective-permute-start.8 = (bf16[6,3,16,128]{3,2,1,0:T(8,128)(2,1)S(1)}, bf16[6,3,16,128]{3,2,1,0:T(8,128)(2,1)S(1)}, u32[]{:S(2)}, u32[]{:S(2)}) collective-permute-start(bf16[6,3,16,128]{3,2,1,0:T(8,128)(2,1)S(1)} %get-tuple-element.58), channel_id=1, source_target_pairs={{0,1},{2,3},{4,5},{6,7},{8,9},{10,11},{12,13},{14,15},{16,17},{18,... | collective-permute-start | bytes 221192 | tf_op jit(solution)/shard_map/ppermute | solution.py:354
  36.2 7.8 %collective-permute-start.7 = (bf16[6,3,16,128]{3,2,1,0:T(8,128)(2,1)S(1)}, bf16[6,3,16,128]{3,2,1,0:T(8,128)(2,1)S(1)}, u32[]{:S(2)}, u32[]{:S(2)}) collective-permute-start(bf16[6,3,16,128]{3,2,1,0:T(8,128)(2,1)S(1)} %get-tuple-element.56), channel_id=1, source_target_pairs={{1,2},{3,4},{5,6},{7,8},{9,10},{11,12},{13,14},{15,16},{17,18},{19... | collective-permute-start | bytes 221192 | tf_op jit(solution)/shard_map/ppermute | solution.py:354
  47.3 4.8 %collective-permute-start.9 = (f32[32,4,128]{2,1,0:T(4,128)S(1)}, f32[32,4,128]{2,1,0:T(4,128)S(1)}, u32[]{:S(2)}, u32[]{:S(2)}) collective-permute-start(f32[32,4,128]{2,1,0:T(4,128)S(1)} %get-tuple-element.64), channel_id=1, source_target_pairs={{0,64},{64,0},{128,192},{192,128},{1,65},{65,1},{129,193},{193,129... | collective-permute-start | bytes 196616 | tf_op jit(solution)/shard_map/ppermute | solution.py:350
  47.6 5.8 %collective-permute-start.10 = (f32[32,4,128]{2,1,0:T(4,128)S(1)}, f32[32,4,128]{2,1,0:T(4,128)S(1)}, u32[]{:S(2)}, u32[]{:S(2)}) collective-permute-start(f32[32,4,128]{2,1,0:T(4,128)S(1)} %get-tuple-element.65), channel_id=1, source_target_pairs={{0,128},{64,192},{128,0},{192,64},{1,129},{65,193},{129,1},{193,65... | collective-permute-start | bytes 196616 | tf_op jit(solution)/shard_map/ppermute | solution.py:350
  50.2 5.5 %collective-permute-start.11 = (f32[32,4,128]{2,1,0:T(4,128)S(1)}, f32[32,4,128]{2,1,0:T(4,128)S(1)}, u32[]{:S(2)}, u32[]{:S(2)}) collective-permute-start(f32[32,4,128]{2,1,0:T(4,128)S(1)} %get-tuple-element.66), channel_id=1, source_target_pairs={{0,192},{64,128},{128,64},{192,0},{1,193},{65,129},{129,65},{193,1... | collective-permute-start | bytes 196616 | tf_op jit(solution)/shard_map/ppermute | solution.py:350

commit v3 on v2

--- a/solution.py
+++ b/solution.py
@@ -6,6 +6,7 @@
 from jax.experimental import pallas as pl
 from jax.experimental.pallas import tpu as pltpu
 from jax.sharding import PartitionSpec as P
+
 
 TIMES = 8
 C = 16
@@ -20,7 +21,7 @@
 
 
 VM = pl.BlockSpec(memory_space=pltpu.VMEM)
-ANY = pl.BlockSpec(memory_space=pl.ANY)
+ANY = pl.BlockSpec(memory_space=pltpu.HBM)
 
 
 def by_tm(tm, values):
@@ -64,7 +65,7 @@
         ],
         compiler_params=pltpu.CompilerParams(vmem_limit_bytes=4 << 20),
         name="enter",
-    )(step, latent, embed)
+    )(*[pltpu.with_memory_space_constraint(v, pltpu.HBM) for v in (step, latent, embed)])
 
 
 def prepare_body(conv_in, conv_mid, conv_out, w_in, w_mid, w_out, in_v, mid_v, out_v, turned, sems):
@@ -107,7 +108,7 @@
         ],
         compiler_params=pltpu.CompilerParams(vmem_limit_bytes=8 << 20),
         name="prepare",
-    )(conv_in, conv_mid, conv_out)
+    )(*[pltpu.with_memory_space_constraint(v, pltpu.HBM) for v in (conv_in, conv_mid, conv_out)])
 
 
 def tables(tm, smalls, w_conv, w_in, steps, gathered):

time: 56.8 us -> 54.8 us (0.965)
  local copies, waits for them, and re-layouts: 3.21 us -> 0 us
  Pallas kernels: 17 us -> 18 us
    unnamed x12 -> x0, local copies, waits for them, and re-layouts: 3.21 us -> none
    pallas_call x1, Pallas kernels: 0.45 us -> 1.24 us  [prepare(): pl.pallas_call(prepare_body, out_shape=tuple((jax.ShapeDtypeStruct(shape,...]
  transfers between devices with their start and end apart: 12 -> 12, of which waited for: 5 -> 5; matrix products, arithmetic and copies ran while one was open for 0% -> 0% of each run, Pallas kernels for 8% -> 10%
where the time goes in v3:
time: 54.8 us; the launch traced here: 54.6 us
  starting transfers between devices  23.5 us (43%)
  Pallas kernels  18 us (33%)
  waiting for transfers between devices  12.9 us (24%)
    pallas_call x6, Pallas kernels, call(): pl.pallas_call(functools.partial(body, rounds), out_shape=out_shape, in_s...  14.7 us
    ppermute x6, starting transfers between devices, pair_up(): lax.ppermute(x, 'pix', [(a, b) for a, b in pairs] + [(b, a) for a, b in p...  14.5 us
    ppermute x6, starting transfers between devices, across(): return lax.ppermute(x, 'tm', [(t, t ^ k) for t in range(4)])  8.97 us
    ppermute x6, waiting for transfers between devices, pair_up(): lax.ppermute(x, 'pix', [(a, b) for a, b in pairs] + [(b, a) for a, b in p...  6.82 us
    ppermute x6, waiting for transfers between devices, across(): return lax.ppermute(x, 'tm', [(t, t ^ k) for t in range(4)])  6.12 us
    pallas_call x1, Pallas kernels, prepare(): pl.pallas_call(prepare_body, out_shape=tuple((jax.ShapeDtypeStruct(shape,...  1.24 us
    pallas_call x1, Pallas kernels, enter(): pl.pallas_call(enter_body, out_shape=(jax.ShapeDtypeStruct((ROWS, C, L),...  1.15 us
  transfers between devices with their start and end apart: 12, of which 5 were waited for; matrix products, arithmetic and copies ran while one was open for 0% of the time, Pallas kernels for 10%

profile of v3, /device:TPU:24, one launch (start us, length us, event | category | flops | bytes accessed | tf_op | source)
XLA Modules:
  0.0 54.6 jit_solution(10282898650035877680)
XLA Ops:
  0.0 1.2 %enter.1 = (f32[4,16,128]{2,1,0:T(8,128)S(1)}, bf16[3,16,128]{2,1,0:T(8,128)(2,1)S(1)}, bf16[3,16,128]{2,1,0:T(8,128)(2,1)S(1)}, f32[4,128]{1,0:T(4,128)S(1)}) custom-call(f32[2]{0:T(128)} %step.1, f32[16,4,448]{2,1,0:T(4,128)} %latent.1, f32[2,128]{1,0:T(2,128)} %embed.1), custom_call_target="tpu_custom_call" | custom-call | tf_op jit(solution)/shard_map/enter/pallas_call | solution.py:55
  1.2 0.1 collective-permute-start.1
  1.3 8.0 %collective-permute-start = (bf16[3,16,128]{2,1,0:T(8,128)(2,1)S(1)}, bf16[3,16,128]{2,1,0:T(8,128)(2,1)S(1)}, u32[]{:S(2)}, u32[]{:S(2)}) collective-permute-start(bf16[3,16,128]{2,1,0:T(8,128)(2,1)S(1)} %get-tuple-element.37), channel_id=1, source_target_pairs={{1,2},{3,4},{5,6},{7,8},{9,10},{11,12},{13,14},{15,16},{17,18},{19... | collective-permute-start | bytes 36872 | tf_op jit(solution)/shard_map/ppermute | solution.py:355
  9.3 2.8 %collective-permute-start.4 = (f32[4,128]{1,0:T(4,128)S(1)}, f32[4,128]{1,0:T(4,128)S(1)}, u32[]{:S(2)}, u32[]{:S(2)}) collective-permute-start(f32[4,128]{1,0:T(4,128)S(1)} %get-tuple-element.39.refs_2_), channel_id=1, source_target_pairs={{0,192},{64,128},{128,64},{192,0},{1,193},{65,129},{129,65},{193,1... | collective-permute-start | bytes 6152 | tf_op jit(solution)/shard_map/ppermute | solution.py:351
  12.1 0.8 %collective-permute-start.3 = (f32[4,128]{1,0:T(4,128)S(1)}, f32[4,128]{1,0:T(4,128)S(1)}, u32[]{:S(2)}, u32[]{:S(2)}) collective-permute-start(f32[4,128]{1,0:T(4,128)S(1)} %get-tuple-element.39.refs_2_), channel_id=1, source_target_pairs={{0,128},{64,192},{128,0},{192,64},{1,129},{65,193},{129,1},{193,65... | collective-permute-start | bytes 6152 | tf_op jit(solution)/shard_map/ppermute | solution.py:351
  12.9 0.5 collective-permute-start.2
  13.5 1.2 %prepare.1 = (bf16[384,256]{1,0:T(8,128)(2,1)S(1)}, bf16[896,512]{1,0:T(8,128)(2,1)S(1)}, bf16[96,512]{1,0:T(8,128)(2,1)S(1)}) custom-call(bf16[3,3,16,128]{3,2,1,0:T(8,128)(2,1)} %bitcast.2, bf16[3,3,128,128]{3,2,1,0:T(8,128)(2,1)} %conv_mid.1, bf16[3,3,16,128]{3,2,1,0:T(8,128)(2,1)} %conv_out.1), custom_call_target="tpu_custom_call" | custom-call | tf_op jit(solution)/shard_map/prepare/pallas_call | solution.py:97
  14.7 0.0 collective-permute-done.4.refs_5_
  14.7 2.5 %collective-permute-done.3.refs_4_ = f32[4,128]{1,0:T(4,128)S(1)} collective-permute-done((f32[4,128]{1,0:T(4,128)S(1)}, f32[4,128]{1,0:T(4,128)S(1)}, u32[]{:S(2)}, u32[]{:S(2)}) %collective-permute-start.3) | collective-permute-done | bytes 2080 | tf_op jit(solution)/shard_map/ppermute | solution.py:351
  17.2 0.0 collective-permute-done.2.refs_3_
  17.2 0.0 collective-permute-done.1.refs_1_
  17.2 1.5 %shard_map.64 = (bf16[256,512]{1,0:T(8,128)(2,1)S(1)}, bf16[256,512]{1,0:T(8,128)(2,1)S(1)}, bf16[256,512]{1,0:T(8,128)(2,1)S(1)}, bf16[256,512]{1,0:T(8,128)(2,...) custom-call(f32[4,16,128]{2,1,0:T(8,128)S(1)} %get-tuple-element.36.refs_0_, ...), custom_call_target="tpu_custom_call" | custom-call | tf_op jit(solution)/shard_map/pallas_call | solution.py:292
  18.8 0.0 collective-permute-done.refs_1_
  18.8 3.6 %shard_map.65 = (f32[9,4,16,128]{3,2,1,0:T(8,128)S(1)}, bf16[7,3,16,128]{3,2,1,0:T(8,128)(2,1)S(1)}, bf16[7,3,16,128]{3,2,1,0:T(8,128)(2,1)S(1)}) custom-call(f32[4,16,128]{2,1,0:T(8,128)S(1)} %get-tuple-element.36.refs_0_, bf16[3,16,128]{2,1,0:T(8,128)(2,1)S(1)} %collective-permute-done.refs_1_, bf16[256,512]{1,0:T(8,128)(2,1)S(1)} %get-tuple-element.42.refs_2_, ...), custom_call_target="tpu_custom_call" | custom-call | tf_op jit(solution)/shard_map/pallas_call | solution.py:292
  22.4 0.1 collective-permute-start.6
  22.5 3.0 %collective-permute-start.5 = (bf16[7,3,16,128]{3,2,1,0:T(8,128)(2,1)S(1)}, bf16[7,3,16,128]{3,2,1,0:T(8,128)(2,1)S(1)}, u32[]{:S(2)}, u32[]{:S(2)}) collective-permute-start(bf16[7,3,16,128]{3,2,1,0:T(8,128)(2,1)S(1)} %get-tuple-element.49), channel_id=1, source_target_pairs={{1,2},{3,4},{5,6},{7,8},{9,10},{11,12},{13,14},{15,16},{17,18},{19... | collective-permute-start | bytes 258056 | tf_op jit(solution)/shard_map/ppermute | solution.py:355
  25.5 0.0 collective-permute-done.6.refs_1_
  25.5 1.5 %shard_map.66 = (bf16[256,512]{1,0:T(8,128)(2,1)S(1)}, bf16[256,512]{1,0:T(8,128)(2,1)S(1)}, bf16[256,512]{1,0:T(8,128)(2,1)S(1)}, bf16[256,512]{1,0:T(8,128)(2,1)S(1)}) custom-call(f32[4,16,128]{2,1,0:T(8,128)S(1)} %get-tuple-element.36.refs_0_, bf16[7,3,16,128]{3,2,1,0:T(8,128)(2,1)S(1)} %collective-permute-done.6.refs_1_, ...), custom_call_target="tpu_custom_call" | custom-call | tf_op jit(solution)/shard_map/pallas_call | solution.py:292
  27.0 3.4 %collective-permute-done.5.refs_1_ = bf16[7,3,16,128]{3,2,1,0:T(8,128)(2,1)S(1)} collective-permute-done((bf16[7,3,16,128]{3,2,1,0:T(8,128)(2,1)S(1)}, bf16[7,3,16,128]{3,2,1,0:T(8,128)(2,1)S(1)}, u32[]{:S(2)}, u32[]{:S(2)}) %collective-permute-start.5) | collective-permute-done | bytes 86048 | tf_op jit(solution)/shard_map/ppermute | solution.py:355
  30.4 3.5 %shard_map.67 = (f32[9,4,16,128]{3,2,1,0:T(8,128)S(1)}, bf16[6,3,16,128]{3,2,1,0:T(8,128)(2,1)S(1)}, bf16[6,3,16,128]{3,2,1,0:T(8,128)(2,1)S(1)}) custom-call(f32[4,16,128]{2,1,0:T(8,128)S(1)} %get-tuple-element.36.refs_0_, bf16[7,3,16,128]{3,2,1,0:T(8,128)(2,1)S(1)} %collective-permute-done.5.refs_1_, f32[9,4,16,128]{3,2,1,0:T(8,128)S(1)} %get-tuple-element.50.refs_2_, ...), custom_call_target="tpu_custom_call" | custom-call | tf_op jit(solution)/shard_map/pallas_call | solution.py:292
  33.9 0.3 collective-permute-start.8
  34.2 3.0 %collective-permute-start.7 = (bf16[6,3,16,128]{3,2,1,0:T(8,128)(2,1)S(1)}, bf16[6,3,16,128]{3,2,1,0:T(8,128)(2,1)S(1)}, u32[]{:S(2)}, u32[]{:S(2)}) collective-permute-start(bf16[6,3,16,128]{3,2,1,0:T(8,128)(2,1)S(1)} %get-tuple-element.56), channel_id=1, source_target_pairs={{1,2},{3,4},{5,6},{7,8},{9,10},{11,12},{13,14},{15,16},{17,18},{19... | collective-permute-start | bytes 221192 | tf_op jit(solution)/shard_map/ppermute | solution.py:355
  37.2 0.0 collective-permute-done.8.refs_1_
  37.2 1.3 %shard_map.68 = (bf16[256,512]{1,0:T(8,128)(2,1)S(1)}, bf16[256,512]{1,0:T(8,128)(2,1)S(1)}, bf16[256,512]{1,0:T(8,128)(2,1)S(1)}, bf16[256,512]{1,0:T(8,128)(2,1)S(1)}) custom-call(f32[4,16,128]{2,1,0:T(8,128)S(1)} %get-tuple-element.36.refs_0_, bf16[6,3,16,128]{3,2,1,0:T(8,128)(2,1)S(1)} %collective-permute-done.8.refs_1_, ...), custom_call_target="tpu_custom_call" | custom-call | tf_op jit(solution)/shard_map/pallas_call | solution.py:292
  38.5 3.5 %collective-permute-done.7.refs_1_ = bf16[6,3,16,128]{3,2,1,0:T(8,128)(2,1)S(1)} collective-permute-done((bf16[6,3,16,128]{3,2,1,0:T(8,128)(2,1)S(1)}, bf16[6,3,16,128]{3,2,1,0:T(8,128)(2,1)S(1)}, u32[]{:S(2)}, u32[]{:S(2)}) %collective-permute-start.7) | collective-permute-done | bytes 73760 | tf_op jit(solution)/shard_map/ppermute | solution.py:355
  42.0 3.3 %shard_map.69 = (f32[32,4,128]{2,1,0:T(4,128)S(1)}, f32[32,4,128]{2,1,0:T(4,128)S(1)}, f32[32,4,128]{2,1,0:T(4,128)S(1)}, f32[32,4,128]{2,1,0:T(4,128)S(1)}) custom-call(f32[4,16,128]{2,1,0:T(8,128)S(1)} %get-tuple-element.36.refs_0_, bf16[6,3,16,128]{3,2,1,0:T(8,128)(2,1)S(1)} %collective-permute-done.7.refs_1_, ...), custom_call_target="tpu_custom_call" | custom-call | tf_op jit(solution)/shard_map/pallas_call | solution.py:292
  45.3 0.3 collective-permute-start.9
  45.6 2.6 %collective-permute-start.10 = (f32[32,4,128]{2,1,0:T(4,128)S(1)}, f32[32,4,128]{2,1,0:T(4,128)S(1)}, u32[]{:S(2)}, u32[]{:S(2)}) collective-permute-start(f32[32,4,128]{2,1,0:T(4,128)S(1)} %get-tuple-element.65), channel_id=1, source_target_pairs={{0,128},{64,192},{128,0},{192,64},{1,129},{65,193},{129,1},{193,65... | collective-permute-start | bytes 196616 | tf_op jit(solution)/shard_map/ppermute | solution.py:351
  48.2 1.9 %collective-permute-start.11 = (f32[32,4,128]{2,1,0:T(4,128)S(1)}, f32[32,4,128]{2,1,0:T(4,128)S(1)}, u32[]{:S(2)}, u32[]{:S(2)}) collective-permute-start(f32[32,4,128]{2,1,0:T(4,128)S(1)} %get-tuple-element.66), channel_id=1, source_target_pairs={{0,192},{64,128},{128,64},{192,0},{1,193},{65,129},{129,65},{193,1... | collective-permute-start | bytes 196616 | tf_op jit(solution)/shard_map/ppermute | solution.py:351
  50.0 0.0 collective-permute-done.9.p1
  50.0 1.3 %collective-permute-done.10.p2 = f32[32,4,128]{2,1,0:T(4,128)S(1)} collective-permute-done((f32[32,4,128]{2,1,0:T(4,128)S(1)}, f32[32,4,128]{2,1,0:T(4,128)S(1)}, u32[]{:S(2)}, u32[]{:S(2)}) %collective-permute-start.10) | collective-permute-done | bytes 65568 | tf_op jit(solution)/shard_map/ppermute | solution.py:351
  51.3 2.3 %collective-permute-done.11.p3 = f32[32,4,128]{2,1,0:T(4,128)S(1)} collective-permute-done((f32[32,4,128]{2,1,0:T(4,128)S(1)}, f32[32,4,128]{2,1,0:T(4,128)S(1)}, u32[]{:S(2)}, u32[]{:S(2)}) %collective-permute-start.11) | collective-permute-done | bytes 65568 | tf_op jit(solution)/shard_map/ppermute | solution.py:351
  53.7 0.9 %join.1 = f32[32,4,448]{2,1,0:T(4,128)} custom-call(f32[32,4,128]{2,1,0:T(4,128)S(1)} %get-tuple-element.63.p0, f32[32,4,128]{2,1,0:T(4,128)S(1)} %collective-permute-done.9.p1, f32[32,4,128]{2,1,0:T(4,128)S(1)} %collective-permute-done.10.p2, f32[32,4,128]{2,1,0:T(4,128)S(1)} %collective-permute-done.11.p3), custom_call_target="tpu_custom_call" | custom-call | tf_op jit(solution)/shard_map/join/pallas_call | solution.py:340
Async XLA Ops:
  1.2 16.1 %collective-permute-start.1 = (bf16[3,16,128]{2,1,0:T(8,128)(2,1)S(1)}, bf16[3,16,128]{2,1,0:T(8,128)(2,1)S(1)}, u32[]{:S(2)}, u32[]{:S(2)}) collective-permute-start(bf16[3,16,128]{2,1,0:T(8,128)(2,1)S(1)} %get-tuple-element.38), channel_id=1, source_target_pairs={{0,1},{2,3},{4,5},{6,7},{8,9},{10,11},{12,13},{14,15},{16,17},{18,... | collective-permute-start | bytes 36872 | tf_op jit(solution)/shard_map/ppermute | solution.py:355
  1.3 17.5 %collective-permute-start = (bf16[3,16,128]{2,1,0:T(8,128)(2,1)S(1)}, bf16[3,16,128]{2,1,0:T(8,128)(2,1)S(1)}, u32[]{:S(2)}, u32[]{:S(2)}) collective-permute-start(bf16[3,16,128]{2,1,0:T(8,128)(2,1)S(1)} %get-tuple-element.37), channel_id=1, source_target_pairs={{1,2},{3,4},{5,6},{7,8},{9,10},{11,12},{13,14},{15,16},{17,18},{19... | collective-permute-start | bytes 36872 | tf_op jit(solution)/shard_map/ppermute | solution.py:355
  9.3 5.4 %collective-permute-start.4 = (f32[4,128]{1,0:T(4,128)S(1)}, f32[4,128]{1,0:T(4,128)S(1)}, u32[]{:S(2)}, u32[]{:S(2)}) collective-permute-start(f32[4,128]{1,0:T(4,128)S(1)} %get-tuple-element.39.refs_2_), channel_id=1, source_target_pairs={{0,192},{64,128},{128,64},{192,0},{1,193},{65,129},{129,65},{193,1... | collective-permute-start | bytes 6152 | tf_op jit(solution)/shard_map/ppermute | solution.py:351
  12.1 5.1 %collective-permute-start.3 = (f32[4,128]{1,0:T(4,128)S(1)}, f32[4,128]{1,0:T(4,128)S(1)}, u32[]{:S(2)}, u32[]{:S(2)}) collective-permute-start(f32[4,128]{1,0:T(4,128)S(1)} %get-tuple-element.39.refs_2_), channel_id=1, source_target_pairs={{0,128},{64,192},{128,0},{192,64},{1,129},{65,193},{129,1},{193,65... | collective-permute-start | bytes 6152 | tf_op jit(solution)/shard_map/ppermute | solution.py:351
  12.9 4.3 %collective-permute-start.2 = (f32[4,128]{1,0:T(4,128)S(1)}, f32[4,128]{1,0:T(4,128)S(1)}, u32[]{:S(2)}, u32[]{:S(2)}) collective-permute-start(f32[4,128]{1,0:T(4,128)S(1)} %get-tuple-element.39.refs_2_), channel_id=1, source_target_pairs={{0,64},{64,0},{128,192},{192,128},{1,65},{65,1},{129,193},{193,129... | collective-permute-start | bytes 6152 | tf_op jit(solution)/shard_map/ppermute | solution.py:351
  22.4 3.1 %collective-permute-start.6 = (bf16[7,3,16,128]{3,2,1,0:T(8,128)(2,1)S(1)}, bf16[7,3,16,128]{3,2,1,0:T(8,128)(2,1)S(1)}, u32[]{:S(2)}, u32[]{:S(2)}) collective-permute-start(bf16[7,3,16,128]{3,2,1,0:T(8,128)(2,1)S(1)} %get-tuple-element.51), channel_id=1, source_target_pairs={{0,1},{2,3},{4,5},{6,7},{8,9},{10,11},{12,13},{14,15},{16,17},{18,... | collective-permute-start | bytes 258056 | tf_op jit(solution)/shard_map/ppermute | solution.py:355
  22.5 7.9 %collective-permute-start.5 = (bf16[7,3,16,128]{3,2,1,0:T(8,128)(2,1)S(1)}, bf16[7,3,16,128]{3,2,1,0:T(8,128)(2,1)S(1)}, u32[]{:S(2)}, u32[]{:S(2)}) collective-permute-start(bf16[7,3,16,128]{3,2,1,0:T(8,128)(2,1)S(1)} %get-tuple-element.49), channel_id=1, source_target_pairs={{1,2},{3,4},{5,6},{7,8},{9,10},{11,12},{13,14},{15,16},{17,18},{19... | collective-permute-start | bytes 258056 | tf_op jit(solution)/shard_map/ppermute | solution.py:355
  33.9 3.3 %collective-permute-start.8 = (bf16[6,3,16,128]{3,2,1,0:T(8,128)(2,1)S(1)}, bf16[6,3,16,128]{3,2,1,0:T(8,128)(2,1)S(1)}, u32[]{:S(2)}, u32[]{:S(2)}) collective-permute-start(bf16[6,3,16,128]{3,2,1,0:T(8,128)(2,1)S(1)} %get-tuple-element.58), channel_id=1, source_target_pairs={{0,1},{2,3},{4,5},{6,7},{8,9},{10,11},{12,13},{14,15},{16,17},{18,... | collective-permute-start | bytes 221192 | tf_op jit(solution)/shard_map/ppermute | solution.py:355
  34.2 7.8 %collective-permute-start.7 = (bf16[6,3,16,128]{3,2,1,0:T(8,128)(2,1)S(1)}, bf16[6,3,16,128]{3,2,1,0:T(8,128)(2,1)S(1)}, u32[]{:S(2)}, u32[]{:S(2)}) collective-permute-start(bf16[6,3,16,128]{3,2,1,0:T(8,128)(2,1)S(1)} %get-tuple-element.56), channel_id=1, source_target_pairs={{1,2},{3,4},{5,6},{7,8},{9,10},{11,12},{13,14},{15,16},{17,18},{19... | collective-permute-start | bytes 221192 | tf_op jit(solution)/shard_map/ppermute | solution.py:355
  45.3 4.8 %collective-permute-start.9 = (f32[32,4,128]{2,1,0:T(4,128)S(1)}, f32[32,4,128]{2,1,0:T(4,128)S(1)}, u32[]{:S(2)}, u32[]{:S(2)}) collective-permute-start(f32[32,4,128]{2,1,0:T(4,128)S(1)} %get-tuple-element.64), channel_id=1, source_target_pairs={{0,64},{64,0},{128,192},{192,128},{1,65},{65,1},{129,193},{193,129... | collective-permute-start | bytes 196616 | tf_op jit(solution)/shard_map/ppermute | solution.py:351
  45.6 5.8 %collective-permute-start.10 = (f32[32,4,128]{2,1,0:T(4,128)S(1)}, f32[32,4,128]{2,1,0:T(4,128)S(1)}, u32[]{:S(2)}, u32[]{:S(2)}) collective-permute-start(f32[32,4,128]{2,1,0:T(4,128)S(1)} %get-tuple-element.65), channel_id=1, source_target_pairs={{0,128},{64,192},{128,0},{192,64},{1,129},{65,193},{129,1},{193,65... | collective-permute-start | bytes 196616 | tf_op jit(solution)/shard_map/ppermute | solution.py:351
  48.2 5.5 %collective-permute-start.11 = (f32[32,4,128]{2,1,0:T(4,128)S(1)}, f32[32,4,128]{2,1,0:T(4,128)S(1)}, u32[]{:S(2)}, u32[]{:S(2)}) collective-permute-start(f32[32,4,128]{2,1,0:T(4,128)S(1)} %get-tuple-element.66), channel_id=1, source_target_pairs={{0,192},{64,128},{128,64},{192,0},{1,193},{65,129},{129,65},{193,1... | collective-permute-start | bytes 196616 | tf_op jit(solution)/shard_map/ppermute | solution.py:351

commit v4 on v3

--- a/solution.py
+++ b/solution.py
@@ -28,39 +28,49 @@
     return jnp.where(tm == 0, values[0], jnp.where(tm == 1, values[1], jnp.where(tm == 2, values[2], values[3])))
 
 
-def enter_body(step, latent, embed, lat, to_a, to_b, small, step_s, latent_v, embed_v, sems):
+def pieces_of(x):
+    high = x.astype(BF).astype(F32)
+    rest = x - high
+    middle = rest.astype(BF).astype(F32)
+    return high, middle, rest - middle
+
+
+def enter_body(step, latent, embed, lat, to_a, to_b, small, step_s, latent_v, embed_v, other, sems):
     copies = [pltpu.make_async_copy(x, y, sems.at[i]) for i, (x, y) in enumerate(((latent, latent_v), (embed, embed_v), (step, step_s)))]
     for copy in copies:
         copy.start()
     for copy in copies:
         copy.wait()
     tm, core = lax.axis_index("tm"), lax.axis_index("pix") % 2
-    shift = by_tm(tm, SHIFTS)
     lane = lax.broadcasted_iota(jnp.int32, (C, L), 1)
     for r in range(ROWS):
         tiles = [jnp.zeros((C, L), F32)] + [latent_v[:, r, g * L:(g + 1) * L] for g in range(3)]
         tiles.append(jnp.concatenate([latent_v[:, r, 3 * L:], jnp.zeros((C, 4 * L - 448), F32)], axis=1))
-        left, right = by_tm(tm, tiles[:4]), by_tm(tm, tiles[1:])
-        lat[r + core * (3 - 2 * r)] = jnp.where(lane < shift, pltpu.roll(left, shift, 1), pltpu.roll(right, shift, 1))
+        for t, to in ((tm, lat), (tm ^ 2, other)):
+            shift = by_tm(t, SHIFTS)
+            left, right = by_tm(t, tiles[:4]), by_tm(t, tiles[1:])
+            to[r + core * (3 - 2 * r)] = jnp.where(lane < shift, pltpu.roll(left, shift, 1), pltpu.roll(right, shift, 1))
     for d in range(3):
         to_b[d] = lat[d].astype(BF)
-        to_a[d] = lat[3 - d].astype(BF)
-    small[0:2] = embed_v[...]
-    for d in range(2):
-        small[2 + d:3 + d] = jnp.full((1, F), step_s[d], F32)
+        to_a[d] = other[3 - d].astype(BF)
+    rows = jnp.concatenate([embed_v[...]] + [jnp.full((1, F), step_s[d], F32) for d in range(2)], axis=0)
+    table = jnp.concatenate([*pieces_of(rows), jnp.zeros((4, F), F32)], axis=0).astype(BF)
+    small[...] = table
+    to_a[3] = table
 
 
 def enter(step, latent, embed):
-    sent = jax.ShapeDtypeStruct((3, C, L), BF)
+    shapes = ((4, C, L), (3, C, L), (16, F))
     return pl.pallas_call(
         enter_body,
-        out_shape=(jax.ShapeDtypeStruct((ROWS, C, L), F32), sent, sent, jax.ShapeDtypeStruct((4, F), F32)),
+        out_shape=(jax.ShapeDtypeStruct((ROWS, C, L), F32),) + tuple(jax.ShapeDtypeStruct(shape, BF) for shape in shapes),
         in_specs=[ANY] * 3,
         out_specs=(VM,) * 4,
         scratch_shapes=[
             pltpu.SMEM((2,), F32),
             pltpu.VMEM((C, ROWS, 448), F32),
             pltpu.VMEM((2, F), F32),
+            pltpu.VMEM((ROWS, C, L), F32),
             pltpu.SemaphoreType.DMA((3,)),
         ],
         compiler_params=pltpu.CompilerParams(vmem_limit_bytes=4 << 20),
@@ -113,13 +123,10 @@
 
 def tables(tm, smalls, w_conv, w_in, steps, gathered):
     for k in range(4):
-        gathered[tm ^ k] = smalls[k][...]
-    embed = jnp.concatenate([gathered[t, 0:2] for t in range(4)], axis=0) * 0.5
-    steps[...] = jnp.concatenate([gathered[t, 2:4] for t in range(4)], axis=0)
-    high = embed.astype(BF).astype(F32)
-    rest = embed - high
-    middle = rest.astype(BF).astype(F32)
-    tail = jnp.concatenate([jnp.zeros((64, F), F32), high, middle, rest - middle, jnp.zeros((40, F), F32)], axis=0)
+        gathered[tm ^ k] = smalls[k].astype(F32)
+    high, middle, rest = [jnp.concatenate([gathered[t, at:at + 2] for t in range(4)], axis=0) * 0.5 for at in (0, 4, 8)]
+    steps[...] = sum(jnp.concatenate([gathered[t, at:at + 2] for t in range(4)], axis=0) for at in (2, 6, 10))
+    tail = jnp.concatenate([jnp.zeros((64, F), F32), high, middle, rest, jnp.zeros((40, F), F32)], axis=0)
     tail = tail.T.astype(BF)
     w_in[:, :F] = w_conv[:, :F]
     for q in range(2):
@@ -132,7 +139,7 @@
 
 
 def groups_of(rounds):
-    return [(t0, min(4, TIMES - t0)) for t0 in (rounds, rounds + 4)]
+    return [(t0, min(2, TIMES - t0)) for t0 in range(rounds, TIMES, 2)]
 
 
 class Round:
@@ -190,46 +197,48 @@
             for b in range(3):
                 blocks += [self.w_mid[pl.ds(self.block(2 * b, 6), F), :], self.w_mid[(2 * b + 1) * F:(2 * b + 2) * F]]
             w = jnp.concatenate(blocks, axis=0)
-        for i0 in range(0, n, 2):
-            lanes = slice(i0 * L, min(i0 + 2, n) * L)
-            rhs = jnp.concatenate([self.hid(g, p)[:, lanes], self.hid(g, p + 1)[:, lanes]], axis=0)
-            y = jnp.dot(w, rhs, preferred_element_type=F32)
-            for i in range(i0, min(i0 + 2, n)):
-                part = y[:, (i - i0) * L:(i - i0 + 1) * L]
-                v = pltpu.roll(part[:2 * F], 1, 1) + part[2 * F:4 * F] + pltpu.roll(part[4 * F:], L - 1, 1)
-                self.sec(g, p)[:, i * L:(i + 1) * L] = silu2(v).astype(BF)
+        lanes = slice(0, n * L)
+        rhs = jnp.concatenate([self.hid(g, p)[:, lanes], self.hid(g, p + 1)[:, lanes]], axis=0)
+        y = jnp.dot(w, rhs, preferred_element_type=F32)
+        for i in range(n):
+            part = y[:, i * L:(i + 1) * L]
+            v = pltpu.roll(part[:2 * F], 1, 1) + part[2 * F:4 * F] + pltpu.roll(part[4 * F:], L - 1, 1)
+            self.sec(g, p)[:, i * L:(i + 1) * L] = silu2(v).astype(BF)
 
 
 def first_part(rounds, *refs):
     if rounds == 0:
-        lat, from_a, *smalls = refs[:6]
-        w_conv, w_mid, h0, h1, s0, s1, w_in, steps, low0, low1, h3_0, h3_1, gathered = refs[6:]
-        tables(lax.axis_index("tm"), smalls, w_conv, w_in, steps, gathered)
+        lat, from_a, own, one, three, w_conv, w_mid, kept_h, kept_s, w_in, steps, *rest = refs
+        smalls = [own[...], one[...], from_a[3], three[...]]
+        tables(lax.axis_index("tm"), smalls, w_conv, w_in, steps, rest.pop())
         prior = None
     else:
-        lat, from_a, prior, w_in, w_mid, h0, h1, s0, s1, low0, low1, h3_0, h3_1 = refs
-    r = Round(rounds, lat, prior, from_a, w_in, w_mid, (low0, low1), lambda g, p: ((h0, h1), (h3_0, h3_1))[p - 2][g], lambda g, p: (s0, s1)[g])
+        lat, from_a, prior, w_in, w_mid, kept_h, kept_s, *rest = refs
+    low, last_h = rest[:4], rest[4:]
+    r = Round(rounds, lat, prior, from_a, w_in, w_mid, low, lambda g, p: kept_h.at[g] if p == 2 else last_h[g], lambda g, p: kept_s.at[g])
     rows = list(range(4, 10))
-    for g in range(2):
-        r.fill(g, rows)
-        r.hidden_pair(g, 2, 4)
-        r.hidden_pair(g, 3, 4)
-    for g in range(2):
-        r.second_pair(g, 2)
+    units = len(r.groups)
+    for g in range(units + 1):
+        if g < units:
+            r.fill(g, rows)
+            r.hidden_pair(g, 2, 4)
+            r.hidden_pair(g, 3, 4)
+        if g:
+            r.second_pair(g - 1, 2)
 
 
 def second_part(rounds, *refs):
     lat, from_b = refs[:2]
     prior = refs[2] if rounds else None
-    h0, h1, s0, s1, w_in, w_mid, w_out, steps, *rest = refs[3 if rounds else 2:]
+    kept_h, kept_s, w_in, w_mid, w_out, steps, *rest = refs[3 if rounds else 2:]
     last = rounds == 2
     if last:
         out, rest = rest[:4], rest[4:]
         ready = rest.pop()
     else:
         nxt, to_a, to_b, *rest = rest
-    low, hid, sec = rest[:2], rest[2:6], rest[6:10]
-    r = Round(rounds, lat, prior, from_b, w_in, w_mid, low, lambda g, p: hid[g * 2 + p] if p < 2 else (h0, h1)[g], lambda g, p: sec[g * 2 + p] if p < 2 else (s0, s1)[g])
+    low, hid, sec = rest[:4], rest[4:12], rest[12:20]
+    r = Round(rounds, lat, prior, from_b, w_in, w_mid, low, lambda g, p: hid[g * 2 + p] if p < 2 else kept_h.at[g], lambda g, p: sec[g * 2 + p] if p < 2 else kept_s.at[g])
     core, tm, column = r.core, r.tm, r.column
 
     def keep(t, row, value):
@@ -262,20 +271,18 @@
                         to_a[t - rounds, 3 - row] = value.astype(BF)
 
     rows = list(range(6))
-    r.fill(0, rows)
-    r.hidden_pair(0, 0, 0)
-    r.hidden_pair(0, 1, 0)
-    r.fill(1, rows)
-    r.second_pair(0, 1)
-    r.hidden_pair(1, 1, 0)
-    r.second_pair(0, 0)
-    r.hidden_pair(1, 0, 0)
-    out_pair(0, 1)
-    out_pair(0, 0)
-    r.second_pair(1, 1)
-    out_pair(1, 1)
-    r.second_pair(1, 0)
-    out_pair(1, 0)
+    units = len(r.groups)
+    for g in range(units + 2):
+        if g < units:
+            r.fill(g, rows)
+            r.hidden_pair(g, 1, 0)
+            r.hidden_pair(g, 0, 0)
+        if 0 < g <= units:
+            r.second_pair(g - 1, 1)
+            r.second_pair(g - 1, 0)
+        if g > 1:
+            out_pair(g - 2, 1)
+            out_pair(g - 2, 0)
 
     for row in range(ROWS):
         if rounds == 1:
@@ -299,21 +306,21 @@
     )(*args)
 
 
-PAIR = (2 * F, 4 * L)
-LOW = [pltpu.VMEM((288, 4 * L), BF)] * 2
+PAIR = (2 * F, 2 * L)
+LOW = [pltpu.VMEM((288, 2 * L), BF)] * 4
 
 
 def run_first(rounds, *args):
-    out_shape = (jax.ShapeDtypeStruct(PAIR, BF),) * 4
-    scratch = LOW + [pltpu.VMEM(PAIR, BF)] * 2
+    out_shape = (jax.ShapeDtypeStruct((len(groups_of(rounds)),) + PAIR, BF),) * 2
+    scratch = LOW + [pltpu.VMEM(PAIR, BF)] * 4
     if rounds == 0:
         out_shape += (jax.ShapeDtypeStruct((3 * F, 2 * F), BF), jax.ShapeDtypeStruct((TIMES, F), F32))
-        scratch += [pltpu.VMEM((4, 4, F), F32)]
+        scratch += [pltpu.VMEM((4, 16, F), F32)]
     return call(first_part, rounds, args, out_shape, scratch)
 
 
 def run_second(rounds, *args):
-    scratch = LOW + [pltpu.VMEM(PAIR, BF)] * 8
+    scratch = LOW + [pltpu.VMEM(PAIR, BF)] * 16
     if rounds == 2:
         out_shape = (jax.ShapeDtypeStruct((32, ROWS, L), F32),) * 4
         scratch += [pltpu.VMEM((512, L), F32)]
@@ -355,6 +362,12 @@
     return lax.ppermute(x, "pix", [(a, b) for a, b in pairs] + [(b, a) for a, b in pairs])
 
 
+def partner_of_other_half(x):
+    pixels = lax.axis_size("pix")
+    pairs = [(t * pixels + p, (t ^ 2) * pixels + (p ^ 1)) for t in range(4) for p in range(pixels)]
+    return lax.ppermute(x, ("tm", "pix"), pairs)
+
+
 CORES = [(2 * k, 2 * k + 1) for k in range(32)]
 CHIPS = [(2 * k + 1, 2 * k + 2) for k in range(31)]
 
@@ -362,13 +375,13 @@
 def shards(latent, step_size, time_embed, conv_in, conv_mid, conv_out):
     lat, to_a, to_b, small = enter(step_size, latent, time_embed)
     smalls = [small]
-    for k in (1, 2, 3):
+    for k in (1, 3):
         smalls.append(across(small, k))
     w_conv, w_mid, w_out = prepare(conv_in.transpose(0, 1, 3, 2), conv_mid, conv_out)
     prior = ()
     for rounds in range(3):
         from_b = pair_up(to_b, CHIPS)
-        from_a = pair_up(to_a, CORES)
+        from_a = pair_up(to_a, CORES) if rounds else partner_of_other_half(to_a)
         if rounds == 0:
             *kept, w_in, steps = run_first(0, lat, from_a, *smalls, w_conv, w_mid)
         else:
@@ -376,7 +389,9 @@
         done = run_second(rounds, lat, from_b, *prior, *kept, w_in, w_mid, w_out, steps)
         if rounds < 2:
             *prior, to_a, to_b = done
-    got = [done[0]] + [across(done[k], k) for k in (1, 2, 3)]
+    got = [done[0]]
+    for k in (1, 2, 3):
+        got.append(across(done[k], k))
     return join(got).reshape(2, C, ROWS, 448)
 
 

time: 54.8 us -> 53 us (0.967)
  Pallas kernels: 18 us -> 16.4 us
    ppermute x6 -> x5, starting transfers between devices: 8.97 us -> 6.01 us  [across(): return lax.ppermute(x, 'tm', [(t, t ^ k) for t in range(4)])]
    ppermute x0 -> x1, starting transfers between devices: none -> 2.55 us  [partner_of_other_half(): return lax.ppermute(x, ('tm', 'pix'), pairs)]
    pallas_call x6, Pallas kernels: 14.7 us -> 13 us  [call(): pl.pallas_call(functools.partial(body, rounds), out_shape=out_shape, in_s...]
    ppermute x6 -> x5, waiting for transfers between devices: 6.12 us -> 6.68 us  [across(): return lax.ppermute(x, 'tm', [(t, t ^ k) for t in range(4)])]
    ppermute x6 -> x5, waiting for transfers between devices: 6.82 us -> 6.5 us  [pair_up(): lax.ppermute(x, 'pix', [(a, b) for a, b in pairs] + [(b, a) for a, b in p...]
    ppermute x6 -> x5, starting transfers between devices: 14.5 us -> 14.6 us  [pair_up(): lax.ppermute(x, 'pix', [(a, b) for a, b in pairs] + [(b, a) for a, b in p...]
  transfers between devices with their start and end apart: 12 -> 11, of which waited for: 5 -> 5; matrix products, arithmetic and copies ran while one was open for 0% -> 0% of each run, Pallas kernels for 10% -> 11%
where the time goes in v4:
time: 53 us; the launch traced here: 52.8 us
  starting transfers between devices  23.1 us (44%)
  Pallas kernels  16.4 us (31%)
  waiting for transfers between devices  13.2 us (25%)
    ppermute x5, starting transfers between devices, pair_up(): lax.ppermute(x, 'pix', [(a, b) for a, b in pairs] + [(b, a) for a, b in p...  14.6 us
    pallas_call x6, Pallas kernels, call(): pl.pallas_call(functools.partial(body, rounds), out_shape=out_shape, in_s...  13 us
    ppermute x5, waiting for transfers between devices, across(): return lax.ppermute(x, 'tm', [(t, t ^ k) for t in range(4)])  6.68 us
    ppermute x5, waiting for transfers between devices, pair_up(): lax.ppermute(x, 'pix', [(a, b) for a, b in pairs] + [(b, a) for a, b in p...  6.5 us
    ppermute x5, starting transfers between devices, across(): return lax.ppermute(x, 'tm', [(t, t ^ k) for t in range(4)])  6.01 us
    ppermute x1, starting transfers between devices, partner_of_other_half(): return lax.ppermute(x, ('tm', 'pix'), pairs)  2.55 us
    pallas_call x1, Pallas kernels, prepare(): pl.pallas_call(prepare_body, out_shape=tuple((jax.ShapeDtypeStruct(shape,...  1.24 us
    pallas_call x1, Pallas kernels, enter(): pl.pallas_call(enter_body, out_shape=(jax.ShapeDtypeStruct((ROWS, C, L),...  1.2 us
  transfers between devices with their start and end apart: 11, of which 5 were waited for; matrix products, arithmetic and copies ran while one was open for 0% of the time, Pallas kernels for 11%

profile of v4, /device:TPU:24, one launch (start us, length us, event | category | flops | bytes accessed | tf_op | source)
XLA Modules:
  0.0 52.8 jit_solution(789443120810447524)
XLA Ops:
  0.0 1.2 %enter.1 = (f32[4,16,128]{2,1,0:T(8,128)S(1)}, bf16[4,16,128]{2,1,0:T(8,128)(2,1)S(1)}, bf16[3,16,128]{2,1,0:T(8,128)(2,1)S(1)}, bf16[16,128]{1,0:T(8,128)(2,1)S(1)}) custom-call(f32[2]{0:T(128)} %step.1, f32[16,4,448]{2,1,0:T(4,128)} %latent.1, f32[2,128]{1,0:T(2,128)} %embed.1), custom_call_target="tpu_custom_call" | custom-call | tf_op jit(solution)/shard_map/enter/pallas_call | solution.py:64
  1.2 2.5 %collective-permute-start.1 = (bf16[4,16,128]{2,1,0:T(8,128)(2,1)S(1)}, bf16[4,16,128]{2,1,0:T(8,128)(2,1)S(1)}, u32[]{:S(2)}, u32[]{:S(2)}) collective-permute-start(bf16[4,16,128]{2,1,0:T(8,128)(2,1)S(1)} %get-tuple-element.32), channel_id=1, source_target_pairs={{0,129},{1,128},{2,131},{3,130},{4,133},{5,132},{6,135},{7,134},{8... | collective-permute-start | bytes 49160 | tf_op jit(solution)/shard_map/ppermute | solution.py:368
  3.8 8.2 %collective-permute-start = (bf16[3,16,128]{2,1,0:T(8,128)(2,1)S(1)}, bf16[3,16,128]{2,1,0:T(8,128)(2,1)S(1)}, u32[]{:S(2)}, u32[]{:S(2)}) collective-permute-start(bf16[3,16,128]{2,1,0:T(8,128)(2,1)S(1)} %get-tuple-element.31), channel_id=1, source_target_pairs={{1,2},{3,4},{5,6},{7,8},{9,10},{11,12},{13,14},{15,16},{17,18},{19... | collective-permute-start | bytes 36872 | tf_op jit(solution)/shard_map/ppermute | solution.py:362
  12.0 1.2 %collective-permute-start.3 = (bf16[16,128]{1,0:T(8,128)(2,1)S(1)}, bf16[16,128]{1,0:T(8,128)(2,1)S(1)}, u32[]{:S(2)}, u32[]{:S(2)}) collective-permute-start(bf16[16,128]{1,0:T(8,128)(2,1)S(1)} %get-tuple-element.33.refs_2_), channel_id=1, source_target_pairs={{0,192},{64,128},{128,64},{192,0},{1,193},{65,129},{129,65},{193,1... | collective-permute-start | bytes 12296 | tf_op jit(solution)/shard_map/ppermute | solution.py:358
  13.2 0.0 collective-permute-start.2
  13.2 1.2 %prepare.1 = (bf16[384,256]{1,0:T(8,128)(2,1)S(1)}, bf16[896,512]{1,0:T(8,128)(2,1)S(1)}, bf16[96,512]{1,0:T(8,128)(2,1)S(1)}) custom-call(bf16[3,3,16,128]{3,2,1,0:T(8,128)(2,1)} %bitcast.2, bf16[3,3,128,128]{3,2,1,0:T(8,128)(2,1)} %conv_mid.1, bf16[3,3,16,128]{3,2,1,0:T(8,128)(2,1)} %conv_out.1), custom_call_target="tpu_custom_call" | custom-call | tf_op jit(solution)/shard_map/prepare/pallas_call | solution.py:107
  14.5 2.4 %collective-permute-done.3.refs_4_ = bf16[16,128]{1,0:T(8,128)(2,1)S(1)} collective-permute-done((bf16[16,128]{1,0:T(8,128)(2,1)S(1)}, bf16[16,128]{1,0:T(8,128)(2,1)S(1)}, u32[]{:S(2)}, u32[]{:S(2)}) %collective-permute-start.3) | collective-permute-done | bytes 4128 | tf_op jit(solution)/shard_map/ppermute | solution.py:358
  16.9 0.0 collective-permute-done.2.refs_3_
  16.9 0.0 collective-permute-done.1.refs_1_
  16.9 1.6 %shard_map.64 = (bf16[4,256,256]{2,1,0:T(8,128)(2,1)S(1)}, bf16[4,256,256]{2,1,0:T(8,128)(2,1)S(1)}, bf16[384,256]{1,0:T(8,128)(2,1)S(1)}, f32[8,128]{1,0:T(8,128)S(1)}) custom-call(f32[4,16,128]{2,1,0:T(8,128)S(1)} %get-tuple-element.30.refs_0_, bf16[4,16,128]{2,1,0:T(8,128)(2,1)S(1)} %collective-permute-done.1.refs_1_, ...), custom_call_target="tpu_custom_call" | custom-call | tf_op jit(solution)/shard_map/pallas_call | solution.py:299
  18.5 0.0 collective-permute-done.refs_1_
  18.5 3.1 %shard_map.65 = (f32[9,4,16,128]{3,2,1,0:T(8,128)S(1)}, bf16[7,3,16,128]{3,2,1,0:T(8,128)(2,1)S(1)}, bf16[7,3,16,128]{3,2,1,0:T(8,128)(2,1)S(1)}) custom-call(f32[4,16,128]{2,1,0:T(8,128)S(1)} %get-tuple-element.30.refs_0_, bf16[3,16,128]{2,1,0:T(8,128)(2,1)S(1)} %collective-permute-done.refs_1_, bf16[4,256,256]{2,1,0:T(8,128)(2,1)S(1)} %get-tuple-element.36.refs_2_, ...), custom_call_target="tpu_custom_call" | custom-call | tf_op jit(solution)/shard_map/pallas_call | solution.py:299
  21.6 0.1 collective-permute-start.5
  21.7 3.0 %collective-permute-start.4 = (bf16[7,3,16,128]{3,2,1,0:T(8,128)(2,1)S(1)}, bf16[7,3,16,128]{3,2,1,0:T(8,128)(2,1)S(1)}, u32[]{:S(2)}, u32[]{:S(2)}) collective-permute-start(bf16[7,3,16,128]{3,2,1,0:T(8,128)(2,1)S(1)} %get-tuple-element.41), channel_id=1, source_target_pairs={{1,2},{3,4},{5,6},{7,8},{9,10},{11,12},{13,14},{15,16},{17,18},{19... | collective-permute-start | bytes 258056 | tf_op jit(solution)/shard_map/ppermute | solution.py:362
  24.7 0.0 collective-permute-done.5.refs_1_
  24.7 1.6 %shard_map.66 = (bf16[4,256,256]{2,1,0:T(8,128)(2,1)S(1)}, bf16[4,256,256]{2,1,0:T(8,128)(2,1)S(1)}) custom-call(f32[4,16,128]{2,1,0:T(8,128)S(1)} %get-tuple-element.30.refs_0_, bf16[7,3,16,128]{3,2,1,0:T(8,128)(2,1)S(1)} %collective-permute-done.5.refs_1_, f32[9,4,16,128]{3,2,1,0:T(8,128)S(1)} %get-tuple-element.42.refs_2_, ...), custom_call_target="tpu_custom_call" | custom-call | tf_op jit(solution)/shard_map/pallas_call | solution.py:299
  26.3 3.3 %collective-permute-done.4.refs_1_ = bf16[7,3,16,128]{3,2,1,0:T(8,128)(2,1)S(1)} collective-permute-done((bf16[7,3,16,128]{3,2,1,0:T(8,128)(2,1)S(1)}, bf16[7,3,16,128]{3,2,1,0:T(8,128)(2,1)S(1)}, u32[]{:S(2)}, u32[]{:S(2)}) %collective-permute-start.4) | collective-permute-done | bytes 86048 | tf_op jit(solution)/shard_map/ppermute | solution.py:362
  29.6 2.9 %shard_map.67 = (f32[9,4,16,128]{3,2,1,0:T(8,128)S(1)}, bf16[6,3,16,128]{3,2,1,0:T(8,128)(2,1)S(1)}, bf16[6,3,16,128]{3,2,1,0:T(8,128)(2,1)S(1)}) custom-call(f32[4,16,128]{2,1,0:T(8,128)S(1)} %get-tuple-element.30.refs_0_, bf16[7,3,16,128]{3,2,1,0:T(8,128)(2,1)S(1)} %collective-permute-done.4.refs_1_, f32[9,4,16,128]{3,2,1,0:T(8,128)S(1)} %get-tuple-element.42.refs_2_, ...), custom_call_target="tpu_custom_call" | custom-call | tf_op jit(solution)/shard_map/pallas_call | solution.py:299
  32.5 0.1 collective-permute-start.7
  32.6 3.2 %collective-permute-start.6 = (bf16[6,3,16,128]{3,2,1,0:T(8,128)(2,1)S(1)}, bf16[6,3,16,128]{3,2,1,0:T(8,128)(2,1)S(1)}, u32[]{:S(2)}, u32[]{:S(2)}) collective-permute-start(bf16[6,3,16,128]{3,2,1,0:T(8,128)(2,1)S(1)} %get-tuple-element.46), channel_id=1, source_target_pairs={{1,2},{3,4},{5,6},{7,8},{9,10},{11,12},{13,14},{15,16},{17,18},{19... | collective-permute-start | bytes 221192 | tf_op jit(solution)/shard_map/ppermute | solution.py:362
  35.8 0.0 collective-permute-done.7.refs_1_
  35.8 1.3 %shard_map.68 = (bf16[3,256,256]{2,1,0:T(8,128)(2,1)S(1)}, bf16[3,256,256]{2,1,0:T(8,128)(2,1)S(1)}) custom-call(f32[4,16,128]{2,1,0:T(8,128)S(1)} %get-tuple-element.30.refs_0_, bf16[6,3,16,128]{3,2,1,0:T(8,128)(2,1)S(1)} %collective-permute-done.7.refs_1_, f32[9,4,16,128]{3,2,1,0:T(8,128)S(1)} %get-tuple-element.47.refs_2_, ...), custom_call_target="tpu_custom_call" | custom-call | tf_op jit(solution)/shard_map/pallas_call | solution.py:299
  37.1 3.2 %collective-permute-done.6.refs_1_ = bf16[6,3,16,128]{3,2,1,0:T(8,128)(2,1)S(1)} collective-permute-done((bf16[6,3,16,128]{3,2,1,0:T(8,128)(2,1)S(1)}, bf16[6,3,16,128]{3,2,1,0:T(8,128)(2,1)S(1)}, u32[]{:S(2)}, u32[]{:S(2)}) %collective-permute-start.6) | collective-permute-done | bytes 73760 | tf_op jit(solution)/shard_map/ppermute | solution.py:362
  40.4 2.5 %shard_map.69 = (f32[32,4,128]{2,1,0:T(4,128)S(1)}, f32[32,4,128]{2,1,0:T(4,128)S(1)}, f32[32,4,128]{2,1,0:T(4,128)S(1)}, f32[32,4,128]{2,1,0:T(4,128)S(1)}) custom-call(f32[4,16,128]{2,1,0:T(8,128)S(1)} %get-tuple-element.30.refs_0_, bf16[6,3,16,128]{3,2,1,0:T(8,128)(2,1)S(1)} %collective-permute-done.6.refs_1_, ...), custom_call_target="tpu_custom_call" | custom-call | tf_op jit(solution)/shard_map/pallas_call | solution.py:299
  42.9 0.1 collective-permute-start.8
  43.0 3.5 %collective-permute-start.9 = (f32[32,4,128]{2,1,0:T(4,128)S(1)}, f32[32,4,128]{2,1,0:T(4,128)S(1)}, u32[]{:S(2)}, u32[]{:S(2)}) collective-permute-start(f32[32,4,128]{2,1,0:T(4,128)S(1)} %get-tuple-element.53), channel_id=1, source_target_pairs={{0,128},{64,192},{128,0},{192,64},{1,129},{65,193},{129,1},{193,65... | collective-permute-start | bytes 196616 | tf_op jit(solution)/shard_map/ppermute | solution.py:358
  46.4 1.2 %collective-permute-start.10 = (f32[32,4,128]{2,1,0:T(4,128)S(1)}, f32[32,4,128]{2,1,0:T(4,128)S(1)}, u32[]{:S(2)}, u32[]{:S(2)}) collective-permute-start(f32[32,4,128]{2,1,0:T(4,128)S(1)} %get-tuple-element.54), channel_id=1, source_target_pairs={{0,192},{64,128},{128,64},{192,0},{1,193},{65,129},{129,65},{193,1... | collective-permute-start | bytes 196616 | tf_op jit(solution)/shard_map/ppermute | solution.py:358
  47.7 0.0 collective-permute-done.8.p1
  47.7 1.8 %collective-permute-done.9.p2 = f32[32,4,128]{2,1,0:T(4,128)S(1)} collective-permute-done((f32[32,4,128]{2,1,0:T(4,128)S(1)}, f32[32,4,128]{2,1,0:T(4,128)S(1)}, u32[]{:S(2)}, u32[]{:S(2)}) %collective-permute-start.9) | collective-permute-done | bytes 65568 | tf_op jit(solution)/shard_map/ppermute | solution.py:358
  49.5 2.5 %collective-permute-done.10.p3 = f32[32,4,128]{2,1,0:T(4,128)S(1)} collective-permute-done((f32[32,4,128]{2,1,0:T(4,128)S(1)}, f32[32,4,128]{2,1,0:T(4,128)S(1)}, u32[]{:S(2)}, u32[]{:S(2)}) %collective-permute-start.10) | collective-permute-done | bytes 65568 | tf_op jit(solution)/shard_map/ppermute | solution.py:358
  51.9 0.9 %join.1 = f32[32,4,448]{2,1,0:T(4,128)} custom-call(f32[32,4,128]{2,1,0:T(4,128)S(1)} %get-tuple-element.51.p0, f32[32,4,128]{2,1,0:T(4,128)S(1)} %collective-permute-done.8.p1, f32[32,4,128]{2,1,0:T(4,128)S(1)} %collective-permute-done.9.p2, f32[32,4,128]{2,1,0:T(4,128)S(1)} %collective-permute-done.10.p3), custom_call_target="tpu_custom_call" | custom-call | tf_op jit(solution)/shard_map/join/pallas_call | solution.py:347
Async XLA Ops:
  1.2 15.7 %collective-permute-start.1 = (bf16[4,16,128]{2,1,0:T(8,128)(2,1)S(1)}, bf16[4,16,128]{2,1,0:T(8,128)(2,1)S(1)}, u32[]{:S(2)}, u32[]{:S(2)}) collective-permute-start(bf16[4,16,128]{2,1,0:T(8,128)(2,1)S(1)} %get-tuple-element.32), channel_id=1, source_target_pairs={{0,129},{1,128},{2,131},{3,130},{4,133},{5,132},{6,135},{7,134},{8... | collective-permute-start | bytes 49160 | tf_op jit(solution)/shard_map/ppermute | solution.py:368
  3.8 14.8 %collective-permute-start = (bf16[3,16,128]{2,1,0:T(8,128)(2,1)S(1)}, bf16[3,16,128]{2,1,0:T(8,128)(2,1)S(1)}, u32[]{:S(2)}, u32[]{:S(2)}) collective-permute-start(bf16[3,16,128]{2,1,0:T(8,128)(2,1)S(1)} %get-tuple-element.31), channel_id=1, source_target_pairs={{1,2},{3,4},{5,6},{7,8},{9,10},{11,12},{13,14},{15,16},{17,18},{19... | collective-permute-start | bytes 36872 | tf_op jit(solution)/shard_map/ppermute | solution.py:362
  12.0 4.9 %collective-permute-start.3 = (bf16[16,128]{1,0:T(8,128)(2,1)S(1)}, bf16[16,128]{1,0:T(8,128)(2,1)S(1)}, u32[]{:S(2)}, u32[]{:S(2)}) collective-permute-start(bf16[16,128]{1,0:T(8,128)(2,1)S(1)} %get-tuple-element.33.refs_2_), channel_id=1, source_target_pairs={{0,192},{64,128},{128,64},{192,0},{1,193},{65,129},{129,65},{193,1... | collective-permute-start | bytes 12296 | tf_op jit(solution)/shard_map/ppermute | solution.py:358
  13.2 3.7 %collective-permute-start.2 = (bf16[16,128]{1,0:T(8,128)(2,1)S(1)}, bf16[16,128]{1,0:T(8,128)(2,1)S(1)}, u32[]{:S(2)}, u32[]{:S(2)}) collective-permute-start(bf16[16,128]{1,0:T(8,128)(2,1)S(1)} %get-tuple-element.33.refs_2_), channel_id=1, source_target_pairs={{0,64},{64,0},{128,192},{192,128},{1,65},{65,1},{129,193},{193,129... | collective-permute-start | bytes 12296 | tf_op jit(solution)/shard_map/ppermute | solution.py:358
  21.6 3.1 %collective-permute-start.5 = (bf16[7,3,16,128]{3,2,1,0:T(8,128)(2,1)S(1)}, bf16[7,3,16,128]{3,2,1,0:T(8,128)(2,1)S(1)}, u32[]{:S(2)}, u32[]{:S(2)}) collective-permute-start(bf16[7,3,16,128]{3,2,1,0:T(8,128)(2,1)S(1)} %get-tuple-element.43), channel_id=1, source_target_pairs={{0,1},{2,3},{4,5},{6,7},{8,9},{10,11},{12,13},{14,15},{16,17},{18,... | collective-permute-start | bytes 258056 | tf_op jit(solution)/shard_map/ppermute | solution.py:362
  21.7 7.9 %collective-permute-start.4 = (bf16[7,3,16,128]{3,2,1,0:T(8,128)(2,1)S(1)}, bf16[7,3,16,128]{3,2,1,0:T(8,128)(2,1)S(1)}, u32[]{:S(2)}, u32[]{:S(2)}) collective-permute-start(bf16[7,3,16,128]{3,2,1,0:T(8,128)(2,1)S(1)} %get-tuple-element.41), channel_id=1, source_target_pairs={{1,2},{3,4},{5,6},{7,8},{9,10},{11,12},{13,14},{15,16},{17,18},{19... | collective-permute-start | bytes 258056 | tf_op jit(solution)/shard_map/ppermute | solution.py:362
  32.5 3.3 %collective-permute-start.7 = (bf16[6,3,16,128]{3,2,1,0:T(8,128)(2,1)S(1)}, bf16[6,3,16,128]{3,2,1,0:T(8,128)(2,1)S(1)}, u32[]{:S(2)}, u32[]{:S(2)}) collective-permute-start(bf16[6,3,16,128]{3,2,1,0:T(8,128)(2,1)S(1)} %get-tuple-element.48), channel_id=1, source_target_pairs={{0,1},{2,3},{4,5},{6,7},{8,9},{10,11},{12,13},{14,15},{16,17},{18,... | collective-permute-start | bytes 221192 | tf_op jit(solution)/shard_map/ppermute | solution.py:362
  32.6 7.8 %collective-permute-start.6 = (bf16[6,3,16,128]{3,2,1,0:T(8,128)(2,1)S(1)}, bf16[6,3,16,128]{3,2,1,0:T(8,128)(2,1)S(1)}, u32[]{:S(2)}, u32[]{:S(2)}) collective-permute-start(bf16[6,3,16,128]{3,2,1,0:T(8,128)(2,1)S(1)} %get-tuple-element.46), channel_id=1, source_target_pairs={{1,2},{3,4},{5,6},{7,8},{9,10},{11,12},{13,14},{15,16},{17,18},{19... | collective-permute-start | bytes 221192 | tf_op jit(solution)/shard_map/ppermute | solution.py:362
  42.9 4.8 %collective-permute-start.8 = (f32[32,4,128]{2,1,0:T(4,128)S(1)}, f32[32,4,128]{2,1,0:T(4,128)S(1)}, u32[]{:S(2)}, u32[]{:S(2)}) collective-permute-start(f32[32,4,128]{2,1,0:T(4,128)S(1)} %get-tuple-element.52), channel_id=1, source_target_pairs={{0,64},{64,0},{128,192},{192,128},{1,65},{65,1},{129,193},{193,129... | collective-permute-start | bytes 196616 | tf_op jit(solution)/shard_map/ppermute | solution.py:358
  43.0 6.5 %collective-permute-start.9 = (f32[32,4,128]{2,1,0:T(4,128)S(1)}, f32[32,4,128]{2,1,0:T(4,128)S(1)}, u32[]{:S(2)}, u32[]{:S(2)}) collective-permute-start(f32[32,4,128]{2,1,0:T(4,128)S(1)} %get-tuple-element.53), channel_id=1, source_target_pairs={{0,128},{64,192},{128,0},{192,64},{1,129},{65,193},{129,1},{193,65... | collective-permute-start | bytes 196616 | tf_op jit(solution)/shard_map/ppermute | solution.py:358
  46.4 5.5 %collective-permute-start.10 = (f32[32,4,128]{2,1,0:T(4,128)S(1)}, f32[32,4,128]{2,1,0:T(4,128)S(1)}, u32[]{:S(2)}, u32[]{:S(2)}) collective-permute-start(f32[32,4,128]{2,1,0:T(4,128)S(1)} %get-tuple-element.54), channel_id=1, source_target_pairs={{0,192},{64,128},{128,64},{192,0},{1,193},{65,129},{129,65},{193,1... | collective-permute-start | bytes 196616 | tf_op jit(solution)/shard_map/ppermute | solution.py:358

commit v5 on v4

--- a/solution.py
+++ b/solution.py
@@ -143,15 +143,17 @@
 
 
 class Round:
-    def __init__(self, rounds, lat, prior, halo, w_in, w_mid, low, hid, sec):
+    def __init__(self, rounds, lat, prior, halo, w_in, w_mid, w_out, steps, low, first_row):
         self.rounds, self.lat, self.prior, self.halo = rounds, lat, prior, halo
-        self.w_in, self.w_mid, self.low, self.hid, self.sec = w_in, w_mid, low, hid, sec
+        self.w_in, self.w_mid, self.w_out, self.steps = w_in, w_mid, w_out, steps
+        self.low, self.first_row = low, first_row
         pix, self.tm = lax.axis_index("pix"), lax.axis_index("tm")
         self.core = pix % 2
         self.inside = (pix > 0) & (pix < 63)
         self.groups = groups_of(rounds)
         lane = lax.broadcasted_iota(jnp.int32, (C, L), 1)
         self.column = jnp.where(((self.tm == 0) & (lane == 0)) | ((self.tm == 3) & (lane == L - 1)), 0.0, 1.0)
+        self.totals = {}
 
     def state(self, t, row):
         return self.lat[row] if self.rounds == 0 else self.prior[t, row]
@@ -168,122 +170,138 @@
                     x = self.halo[(t0 + i - rounds, d) if rounds else (d,)].astype(F32)
                 x = x * column
                 x = jnp.concatenate([pltpu.roll(x, 1, 1) * column, x, pltpu.roll(x, L - 1, 1) * column], axis=0).astype(BF)
+                at = (w - self.first_row) * 48
                 for lanes in ([i] if rounds else range(n)):
-                    self.low[g][(w - rows[0]) * 48:(w - rows[0] + 1) * 48, lanes * L:(lanes + 1) * L] = x
-
-    def hidden_pair(self, g, p, first_row):
+                    self.low[g][at:at + 48, lanes * L:(lanes + 1) * L] = x
+
+    def block(self, row, last, normal, zero):
+        return normal * F if row > last else pl.multiple_of(jnp.where(self.inside, normal * F, zero * F), F)
+
+    def hidden(self, g, row, to):
         t0, n = self.groups[g]
         width = n * L
         r = lax.broadcasted_iota(jnp.int32, (64, width), 0)
         c = lax.broadcasted_iota(jnp.int32, (64, width), 1)
         edge = ((self.tm == 0) & ((c & 127) == 0)) | ((self.tm == 3) & ((c & 127) == L - 1))
         pick = jnp.where(((r & 7) == t0 + (c >> 7)) & (r < 24) & jnp.logical_not(edge), 1.0, 0.0).astype(BF)
-        at = (2 * p - first_row) * 48
+        at = (row - 1 - self.first_row) * 48
         rhs = jnp.concatenate([self.low[g][at:at + 192, :width], pick], axis=0)
-        w = self.w_in[:2 * F]
-        if p == 0:
-            w = jnp.concatenate([self.w_in[pl.ds(self.block(q, 2), F), :] for q in range(2)], axis=0)
-        v = silu2(jnp.dot(w, rhs, preferred_element_type=F32))
-        self.hid(g, p)[:, :width] = v.astype(BF)
-
-    def block(self, normal, zero):
-        return pl.multiple_of(jnp.where(self.inside, normal * F, zero * F), F)
-
-    def second_pair(self, g, p):
+        blocks = [self.w_in[pl.ds(self.block(row + q, 2, q, 2), F), :] for q in range(len(to))]
+        v = silu2(jnp.dot(jnp.concatenate(blocks, axis=0), rhs, preferred_element_type=F32)).astype(BF)
+        for q, (ref, place) in enumerate(to):
+            ref[place * F:(place + 1) * F, :width] = v[q * F:(q + 1) * F]
+
+    def second(self, g, row, sources, to):
         _, n = self.groups[g]
-        w = self.w_mid[:6 * F]
-        if p == 0:
-            blocks = []
-            for b in range(3):
-                blocks += [self.w_mid[pl.ds(self.block(2 * b, 6), F), :], self.w_mid[(2 * b + 1) * F:(2 * b + 2) * F]]
-            w = jnp.concatenate(blocks, axis=0)
-        lanes = slice(0, n * L)
-        rhs = jnp.concatenate([self.hid(g, p)[:, lanes], self.hid(g, p + 1)[:, lanes]], axis=0)
-        y = jnp.dot(w, rhs, preferred_element_type=F32)
+        count = len(to)
+        rhs = jnp.concatenate([ref[at * F:(at + k) * F, :n * L] for ref, at, k in sources], axis=0)
+        depth = (count + 2) * F
+        blocks = [self.w_mid[pl.ds(self.block(row + q, 2, 2 * b + q, 6), F), :depth] for b in range(3) for q in range(count)]
+        y = jnp.dot(jnp.concatenate(blocks, axis=0), rhs, preferred_element_type=F32)
+        m = count * F
         for i in range(n):
-            part = y[:, i * L:(i + 1) * L]
-            v = pltpu.roll(part[:2 * F], 1, 1) + part[2 * F:4 * F] + pltpu.roll(part[4 * F:], L - 1, 1)
-            self.sec(g, p)[:, i * L:(i + 1) * L] = silu2(v).astype(BF)
+            lanes = slice(i * L, (i + 1) * L)
+            part = y[:, lanes]
+            v = pltpu.roll(part[:m], 1, 1) + part[m:2 * m] + pltpu.roll(part[2 * m:], L - 1, 1)
+            v = silu2(v).astype(BF)
+            for q, (ref, place) in enumerate(to):
+                ref[place * F:(place + 1) * F, lanes] = v[q * F:(q + 1) * F]
+
+    def output(self, g, row, count, sources, emit):
+        t0, n = self.groups[g]
+        column = self.column
+        rhs = jnp.concatenate([ref[at * F:(at + k) * F, :n * L] for ref, at, k in sources], axis=0)
+        y = jnp.dot(self.w_out[:count * 48, :(count + 2) * F], rhs, preferred_element_type=F32)
+        for q in range(count):
+            own = row + q
+            if own not in self.totals:
+                self.totals[own] = jnp.zeros((C, L), F32) if self.rounds == 0 else self.prior[0, own]
+            for i in range(n):
+                t = t0 + i
+                part = y[q * 48:(q + 1) * 48, i * L:(i + 1) * L]
+                conv = pltpu.roll(part[:C] * column, 1, 1) + part[C:2 * C] + pltpu.roll(part[2 * C:] * column, L - 1, 1)
+                self.totals[own] = self.totals[own] + self.steps[t:t + 1] * (self.state(t, own) + conv)
+                emit(t, own, self.lat[own] + self.totals[own], self.totals[own])
 
 
 def first_part(rounds, *refs):
     if rounds == 0:
-        lat, from_a, own, one, three, w_conv, w_mid, kept_h, kept_s, w_in, steps, *rest = refs
+        lat, from_a, own, one, three, w_conv, w_mid, w_out, kept_h, kept_s, done, w_in, steps, *rest = refs
         smalls = [own[...], one[...], from_a[3], three[...]]
         tables(lax.axis_index("tm"), smalls, w_conv, w_in, steps, rest.pop())
         prior = None
     else:
-        lat, from_a, prior, w_in, w_mid, kept_h, kept_s, *rest = refs
-    low, last_h = rest[:4], rest[4:]
-    r = Round(rounds, lat, prior, from_a, w_in, w_mid, low, lambda g, p: kept_h.at[g] if p == 2 else last_h[g], lambda g, p: kept_s.at[g])
-    rows = list(range(4, 10))
+        lat, from_a, prior, w_in, steps, w_mid, w_out, kept_h, kept_s, done, *rest = refs
+    low, hid, sec = rest[:4], rest[4:8], rest[8:12]
+    r = Round(rounds, lat, prior, from_a, w_in, w_mid, w_out, steps, low, 3)
+
+    def emit(t, row, value, total):
+        done[t + 1] = value
+        if t == rounds:
+            done[0] = total
+
     units = len(r.groups)
-    for g in range(units + 1):
+    for g in range(units + 2):
         if g < units:
-            r.fill(g, rows)
-            r.hidden_pair(g, 2, 4)
-            r.hidden_pair(g, 3, 4)
-        if g:
-            r.second_pair(g - 1, 2)
+            r.fill(g, list(range(3, 10)))
+            r.hidden(g, 5, [(kept_h.at[g], 1), (hid[g], 0)])
+            r.hidden(g, 7, [(hid[g], 1), (hid[g], 2)])
+            r.hidden(g, 4, [(kept_h.at[g], 0)])
+        if 0 < g <= units:
+            k = g - 1
+            r.second(k, 6, [(kept_h.at[k], 1, 1), (hid[k], 0, 3)], [(kept_s.at[k], 1), (sec[k], 0)])
+            r.second(k, 5, [(kept_h.at[k], 0, 2), (hid[k], 0, 1)], [(kept_s.at[k], 0)])
+        if g > 1:
+            k = g - 2
+            r.output(k, 3, 1, [(kept_s.at[k], 0, 2), (sec[k], 0, 1)], emit)
 
 
 def second_part(rounds, *refs):
     lat, from_b = refs[:2]
     prior = refs[2] if rounds else None
-    kept_h, kept_s, w_in, w_mid, w_out, steps, *rest = refs[3 if rounds else 2:]
+    kept_h, kept_s, done, w_in, w_mid, w_out, steps, *rest = refs[3 if rounds else 2:]
     last = rounds == 2
     if last:
         out, rest = rest[:4], rest[4:]
         ready = rest.pop()
     else:
         nxt, to_a, to_b, *rest = rest
-    low, hid, sec = rest[:4], rest[4:12], rest[12:20]
-    r = Round(rounds, lat, prior, from_b, w_in, w_mid, low, lambda g, p: hid[g * 2 + p] if p < 2 else kept_h.at[g], lambda g, p: sec[g * 2 + p] if p < 2 else kept_s.at[g])
-    core, tm, column = r.core, r.tm, r.column
+    low, hid, sec = rest[:4], rest[4:8], rest[8:12]
+    r = Round(rounds, lat, prior, from_b, w_in, w_mid, w_out, steps, low, 0)
+    core, tm = r.core, r.tm
 
     def keep(t, row, value):
         ready[pl.ds(((t // 2) ^ tm) * 128 + (t % 2) * 64 + row + core * (3 - 2 * row), C, stride=ROWS), :] = value
 
-    totals = [jnp.zeros((C, L), F32) if rounds == 0 else prior[0, row] for row in range(ROWS)]
-
-    def out_pair(g, p):
-        t0, n = r.groups[g]
-        width = n * L
-        rhs = jnp.concatenate([r.sec(g, p)[:, :width], r.sec(g, p + 1)[:, :width]], axis=0)
-        y = jnp.dot(w_out[...], rhs, preferred_element_type=F32)
-        for q in range(2):
-            row = 2 * p + q
-            for i in range(n):
-                t = t0 + i
-                part = y[q * 48:(q + 1) * 48, i * L:(i + 1) * L]
-                conv = pltpu.roll(part[:C] * column, 1, 1) + part[C:2 * C] + pltpu.roll(part[2 * C:] * column, L - 1, 1)
-                totals[row] = totals[row] + steps[t:t + 1] * (r.state(t, row) + conv)
-                value = lat[row] + totals[row]
-                if last:
-                    keep(t, row, value)
-                else:
-                    nxt[t + 1, row] = value
-                    if t == rounds:
-                        nxt[0, row] = totals[row]
-                    if t < TIMES - 1 and row < 3:
-                        to_b[t - rounds, row] = value.astype(BF)
-                    if t < TIMES - 1 and row > 0:
-                        to_a[t - rounds, 3 - row] = value.astype(BF)
-
-    rows = list(range(6))
+    def emit(t, row, value, total):
+        if last:
+            keep(t, row, value)
+            return
+        nxt[t + 1, row] = value
+        if t == rounds:
+            nxt[0, row] = total
+        if t < TIMES - 1 and row < 3:
+            to_b[t - rounds, row] = value.astype(BF)
+        if t < TIMES - 1 and row > 0:
+            to_a[t - rounds, 3 - row] = value.astype(BF)
+
     units = len(r.groups)
     for g in range(units + 2):
         if g < units:
-            r.fill(g, rows)
-            r.hidden_pair(g, 1, 0)
-            r.hidden_pair(g, 0, 0)
+            r.fill(g, list(range(6)))
+            r.hidden(g, 2, [(hid[g], 1), (hid[g], 2)])
+            r.hidden(g, 1, [(hid[g], 0)])
         if 0 < g <= units:
-            r.second_pair(g - 1, 1)
-            r.second_pair(g - 1, 0)
+            k = g - 1
+            r.second(k, 2, [(hid[k], 0, 3), (kept_h.at[k], 0, 1)], [(sec[k], 0), (sec[k], 1)])
+            r.second(k, 4, [(hid[k], 2, 1), (kept_h.at[k], 0, 2)], [(sec[k], 2)])
         if g > 1:
-            out_pair(g - 2, 1)
-            out_pair(g - 2, 0)
-
+            k = g - 2
+            r.output(k, 0, 2, [(sec[k], 0, 3), (kept_s.at[k], 0, 1)], emit)
+            r.output(k, 2, 1, [(sec[k], 2, 1), (kept_s.at[k], 0, 2)], emit)
+
+    for t in range(rounds, TIMES):
+        emit(t, 3, done[t + 1], done[0])
     for row in range(ROWS):
         if rounds == 1:
             nxt[1, row] = prior[1, row]
@@ -307,12 +325,17 @@
 
 
 PAIR = (2 * F, 2 * L)
-LOW = [pltpu.VMEM((288, 2 * L), BF)] * 4
+
+
+def scratch_of(low_rows, sec_rows):
+    shapes = ((low_rows * 48, 2 * L), (3 * F, 2 * L), (sec_rows * F, 2 * L))
+    return [pltpu.VMEM(shape, BF) for shape in shapes for _ in range(4)]
 
 
 def run_first(rounds, *args):
-    out_shape = (jax.ShapeDtypeStruct((len(groups_of(rounds)),) + PAIR, BF),) * 2
-    scratch = LOW + [pltpu.VMEM(PAIR, BF)] * 4
+    units = len(groups_of(rounds))
+    out_shape = (jax.ShapeDtypeStruct((units,) + PAIR, BF),) * 2 + (jax.ShapeDtypeStruct((TIMES + 1, C, L), F32),)
+    scratch = scratch_of(7, 1)
     if rounds == 0:
         out_shape += (jax.ShapeDtypeStruct((3 * F, 2 * F), BF), jax.ShapeDtypeStruct((TIMES, F), F32))
         scratch += [pltpu.VMEM((4, 16, F), F32)]
@@ -320,7 +343,7 @@
 
 
 def run_second(rounds, *args):
-    scratch = LOW + [pltpu.VMEM(PAIR, BF)] * 16
+    scratch = scratch_of(6, 3)
     if rounds == 2:
         out_shape = (jax.ShapeDtypeStruct((32, ROWS, L), F32),) * 4
         scratch += [pltpu.VMEM((512, L), F32)]
@@ -383,9 +406,9 @@
         from_b = pair_up(to_b, CHIPS)
         from_a = pair_up(to_a, CORES) if rounds else partner_of_other_half(to_a)
         if rounds == 0:
-            *kept, w_in, steps = run_first(0, lat, from_a, *smalls, w_conv, w_mid)
+            *kept, w_in, steps = run_first(0, lat, from_a, *smalls, w_conv, w_mid, w_out)
         else:
-            kept = run_first(rounds, lat, from_a, *prior, w_in, w_mid)
+            kept = run_first(rounds, lat, from_a, *prior, w_in, steps, w_mid, w_out)
         done = run_second(rounds, lat, from_b, *prior, *kept, w_in, w_mid, w_out, steps)
         if rounds < 2:
             *prior, to_a, to_b = done

time: 53 us -> 52.5 us (level)
  waiting for transfers between devices: 13.2 us -> 11.8 us
  Pallas kernels: 16.4 us -> 17.2 us
    ppermute x5, waiting for transfers between devices: 6.5 us -> 5.1 us  [pair_up(): lax.ppermute(x, 'pix', [(a, b) for a, b in pairs] + [(b, a) for a, b in p...]
    pallas_call x6, Pallas kernels: 13 us -> 13.9 us  [call(): pl.pallas_call(functools.partial(body, rounds), out_shape=out_shape, in_s...]
  transfers between devices with their start and end apart: 11 -> 11, of which waited for: 5 -> 5; matrix products, arithmetic and copies ran while one was open for 0% -> 0% of each run, Pallas kernels for 11% -> 15%
where the time goes in v5:
time: 52.5 us; the launch traced here: 52.3 us
  starting transfers between devices  23.1 us (44%)
  Pallas kernels  17.2 us (33%)
  waiting for transfers between devices  11.8 us (22%)
    ppermute x5, starting transfers between devices, pair_up(): lax.ppermute(x, 'pix', [(a, b) for a, b in pairs] + [(b, a) for a, b in p...  14.6 us
    pallas_call x6, Pallas kernels, call(): pl.pallas_call(functools.partial(body, rounds), out_shape=out_shape, in_s...  13.9 us
    ppermute x5, waiting for transfers between devices, across(): return lax.ppermute(x, 'tm', [(t, t ^ k) for t in range(4)])  6.69 us
    ppermute x5, starting transfers between devices, across(): return lax.ppermute(x, 'tm', [(t, t ^ k) for t in range(4)])  6.01 us
    ppermute x5, waiting for transfers between devices, pair_up(): lax.ppermute(x, 'pix', [(a, b) for a, b in pairs] + [(b, a) for a, b in p...  5.1 us
    ppermute x1, starting transfers between devices, partner_of_other_half(): return lax.ppermute(x, ('tm', 'pix'), pairs)  2.55 us
    pallas_call x1, Pallas kernels, prepare(): pl.pallas_call(prepare_body, out_shape=tuple((jax.ShapeDtypeStruct(shape,...  1.24 us
    pallas_call x1, Pallas kernels, enter(): pl.pallas_call(enter_body, out_shape=(jax.ShapeDtypeStruct((ROWS, C, L),...  1.2 us
  transfers between devices with their start and end apart: 11, of which 5 were waited for; matrix products, arithmetic and copies ran while one was open for 0% of the time, Pallas kernels for 15%

profile of v5, /device:TPU:24, one launch (start us, length us, event | category | flops | bytes accessed | tf_op | source)
XLA Modules:
  0.0 52.3 jit_solution(1872701667650216494)
XLA Ops:
  0.0 1.2 %enter.1 = (f32[4,16,128]{2,1,0:T(8,128)S(1)}, bf16[4,16,128]{2,1,0:T(8,128)(2,1)S(1)}, bf16[3,16,128]{2,1,0:T(8,128)(2,1)S(1)}, bf16[16,128]{1,0:T(8,128)(2,1)S(1)}) custom-call(f32[2]{0:T(128)} %step.1, f32[16,4,448]{2,1,0:T(4,128)} %latent.1, f32[2,128]{1,0:T(2,128)} %embed.1), custom_call_target="tpu_custom_call" | custom-call | tf_op jit(solution)/shard_map/enter/pallas_call | solution.py:64
  1.2 2.5 %collective-permute-start.1 = (bf16[4,16,128]{2,1,0:T(8,128)(2,1)S(1)}, bf16[4,16,128]{2,1,0:T(8,128)(2,1)S(1)}, u32[]{:S(2)}, u32[]{:S(2)}) collective-permute-start(bf16[4,16,128]{2,1,0:T(8,128)(2,1)S(1)} %get-tuple-element.35), channel_id=1, source_target_pairs={{0,129},{1,128},{2,131},{3,130},{4,133},{5,132},{6,135},{7,134},{8... | collective-permute-start | bytes 49160 | tf_op jit(solution)/shard_map/ppermute | solution.py:391
  3.8 8.2 %collective-permute-start = (bf16[3,16,128]{2,1,0:T(8,128)(2,1)S(1)}, bf16[3,16,128]{2,1,0:T(8,128)(2,1)S(1)}, u32[]{:S(2)}, u32[]{:S(2)}) collective-permute-start(bf16[3,16,128]{2,1,0:T(8,128)(2,1)S(1)} %get-tuple-element.34), channel_id=1, source_target_pairs={{1,2},{3,4},{5,6},{7,8},{9,10},{11,12},{13,14},{15,16},{17,18},{19... | collective-permute-start | bytes 36872 | tf_op jit(solution)/shard_map/ppermute | solution.py:385
  12.0 1.2 %collective-permute-start.3 = (bf16[16,128]{1,0:T(8,128)(2,1)S(1)}, bf16[16,128]{1,0:T(8,128)(2,1)S(1)}, u32[]{:S(2)}, u32[]{:S(2)}) collective-permute-start(bf16[16,128]{1,0:T(8,128)(2,1)S(1)} %get-tuple-element.36.refs_2_), channel_id=1, source_target_pairs={{0,192},{64,128},{128,64},{192,0},{1,193},{65,129},{129,65},{193,1... | collective-permute-start | bytes 12296 | tf_op jit(solution)/shard_map/ppermute | solution.py:381
  13.2 0.0 collective-permute-start.2
  13.2 1.2 %prepare.1 = (bf16[384,256]{1,0:T(8,128)(2,1)S(1)}, bf16[896,512]{1,0:T(8,128)(2,1)S(1)}, bf16[96,512]{1,0:T(8,128)(2,1)S(1)}) custom-call(bf16[3,3,16,128]{3,2,1,0:T(8,128)(2,1)} %bitcast.2, bf16[3,3,128,128]{3,2,1,0:T(8,128)(2,1)} %conv_mid.1, bf16[3,3,16,128]{3,2,1,0:T(8,128)(2,1)} %conv_out.1), custom_call_target="tpu_custom_call" | custom-call | tf_op jit(solution)/shard_map/prepare/pallas_call | solution.py:107
  14.5 2.4 %collective-permute-done.3.refs_4_ = bf16[16,128]{1,0:T(8,128)(2,1)S(1)} collective-permute-done((bf16[16,128]{1,0:T(8,128)(2,1)S(1)}, bf16[16,128]{1,0:T(8,128)(2,1)S(1)}, u32[]{:S(2)}, u32[]{:S(2)}) %collective-permute-start.3) | collective-permute-done | bytes 4128 | tf_op jit(solution)/shard_map/ppermute | solution.py:381
  16.9 0.0 collective-permute-done.2.refs_3_
  16.9 0.0 collective-permute-done.1.refs_1_
  16.9 2.4 %shard_map.64 = (bf16[4,256,256]{2,1,0:T(8,128)(2,1)S(1)}, bf16[4,256,256]{2,1,0:T(8,128)(2,1)S(1)}, f32[9,16,128]{2,1,0:T(8,128)S(1)}, bf16[384,256]{1,0:T(8,128)(2,1)S(1)}, f32[8,128]{1,0:T(8,128)S(1)}) custom-call(f32[4,16,128]{2,1,0:T(8,128)S(1)} %get-tuple-element.33.refs_0_, bf16[4,16,128]{2,1,0:T(8,128)(2,1)S(1)} %collective-permute-done.1.refs_1_, ...), custom_call_target="tpu_custom_call" | custom-call | tf_op jit(solution)/shard_map/pallas_call | solution.py:317
  19.3 0.0 collective-permute-done.refs_1_
  19.3 2.5 %shard_map.65 = (f32[9,4,16,128]{3,2,1,0:T(8,128)S(1)}, bf16[7,3,16,128]{3,2,1,0:T(8,128)(2,1)S(1)}, bf16[7,3,16,128]{3,2,1,0:T(8,128)(2,1)S(1)}) custom-call(f32[4,16,128]{2,1,0:T(8,128)S(1)} %get-tuple-element.33.refs_0_, bf16[3,16,128]{2,1,0:T(8,128)(2,1)S(1)} %collective-permute-done.refs_1_, bf16[4,256,256]{2,1,0:T(8,128)(2,1)S(1)} %get-tuple-element.40.refs_2_, ...), custom_call_target="tpu_custom_call" | custom-call | tf_op jit(solution)/shard_map/pallas_call | solution.py:317
  21.8 0.1 collective-permute-start.5
  21.9 3.0 %collective-permute-start.4 = (bf16[7,3,16,128]{3,2,1,0:T(8,128)(2,1)S(1)}, bf16[7,3,16,128]{3,2,1,0:T(8,128)(2,1)S(1)}, u32[]{:S(2)}, u32[]{:S(2)}) collective-permute-start(bf16[7,3,16,128]{3,2,1,0:T(8,128)(2,1)S(1)} %get-tuple-element.45), channel_id=1, source_target_pairs={{1,2},{3,4},{5,6},{7,8},{9,10},{11,12},{13,14},{15,16},{17,18},{19... | collective-permute-start | bytes 258056 | tf_op jit(solution)/shard_map/ppermute | solution.py:385
  24.9 0.0 collective-permute-done.5.refs_1_
  24.9 2.4 %shard_map.66 = (bf16[4,256,256]{2,1,0:T(8,128)(2,1)S(1)}, bf16[4,256,256]{2,1,0:T(8,128)(2,1)S(1)}, f32[9,16,128]{2,1,0:T(8,128)S(1)}) custom-call(f32[4,16,128]{2,1,0:T(8,128)S(1)} %get-tuple-element.33.refs_0_, bf16[7,3,16,128]{3,2,1,0:T(8,128)(2,1)S(1)} %collective-permute-done.5.refs_1_, f32[9,4,16,128]{3,2,1,0:T(8,128)S(1)} %get-tuple-element.46.refs_2_, ...), custom_call_target="tpu_custom_call" | custom-call | tf_op jit(solution)/shard_map/pallas_call | solution.py:317
  27.4 2.5 %collective-permute-done.4.refs_1_ = bf16[7,3,16,128]{3,2,1,0:T(8,128)(2,1)S(1)} collective-permute-done((bf16[7,3,16,128]{3,2,1,0:T(8,128)(2,1)S(1)}, bf16[7,3,16,128]{3,2,1,0:T(8,128)(2,1)S(1)}, u32[]{:S(2)}, u32[]{:S(2)}) %collective-permute-start.4) | collective-permute-done | bytes 86048 | tf_op jit(solution)/shard_map/ppermute | solution.py:385
  29.8 2.5 %shard_map.67 = (f32[9,4,16,128]{3,2,1,0:T(8,128)S(1)}, bf16[6,3,16,128]{3,2,1,0:T(8,128)(2,1)S(1)}, bf16[6,3,16,128]{3,2,1,0:T(8,128)(2,1)S(1)}) custom-call(f32[4,16,128]{2,1,0:T(8,128)S(1)} %get-tuple-element.33.refs_0_, bf16[7,3,16,128]{3,2,1,0:T(8,128)(2,1)S(1)} %collective-permute-done.4.refs_1_, f32[9,4,16,128]{3,2,1,0:T(8,128)S(1)} %get-tuple-element.46.refs_2_, ...), custom_call_target="tpu_custom_call" | custom-call | tf_op jit(solution)/shard_map/pallas_call | solution.py:317
  32.3 0.1 collective-permute-start.7
  32.4 3.2 %collective-permute-start.6 = (bf16[6,3,16,128]{3,2,1,0:T(8,128)(2,1)S(1)}, bf16[6,3,16,128]{3,2,1,0:T(8,128)(2,1)S(1)}, u32[]{:S(2)}, u32[]{:S(2)}) collective-permute-start(bf16[6,3,16,128]{3,2,1,0:T(8,128)(2,1)S(1)} %get-tuple-element.51), channel_id=1, source_target_pairs={{1,2},{3,4},{5,6},{7,8},{9,10},{11,12},{13,14},{15,16},{17,18},{19... | collective-permute-start | bytes 221192 | tf_op jit(solution)/shard_map/ppermute | solution.py:385
  35.6 0.0 collective-permute-done.7.refs_1_
  35.6 1.9 %shard_map.68 = (bf16[3,256,256]{2,1,0:T(8,128)(2,1)S(1)}, bf16[3,256,256]{2,1,0:T(8,128)(2,1)S(1)}, f32[9,16,128]{2,1,0:T(8,128)S(1)}) custom-call(f32[4,16,128]{2,1,0:T(8,128)S(1)} %get-tuple-element.33.refs_0_, bf16[6,3,16,128]{3,2,1,0:T(8,128)(2,1)S(1)} %collective-permute-done.7.refs_1_, f32[9,4,16,128]{3,2,1,0:T(8,128)S(1)} %get-tuple-element.52.refs_2_, ...), custom_call_target="tpu_custom_call" | custom-call | tf_op jit(solution)/shard_map/pallas_call | solution.py:317
  37.5 2.6 %collective-permute-done.6.refs_1_ = bf16[6,3,16,128]{3,2,1,0:T(8,128)(2,1)S(1)} collective-permute-done((bf16[6,3,16,128]{3,2,1,0:T(8,128)(2,1)S(1)}, bf16[6,3,16,128]{3,2,1,0:T(8,128)(2,1)S(1)}, u32[]{:S(2)}, u32[]{:S(2)}) %collective-permute-start.6) | collective-permute-done | bytes 73760 | tf_op jit(solution)/shard_map/ppermute | solution.py:385
  40.2 2.1 %shard_map.69 = (f32[32,4,128]{2,1,0:T(4,128)S(1)}, f32[32,4,128]{2,1,0:T(4,128)S(1)}, f32[32,4,128]{2,1,0:T(4,128)S(1)}, f32[32,4,128]{2,1,0:T(4,128)S(1)}) custom-call(f32[4,16,128]{2,1,0:T(8,128)S(1)} %get-tuple-element.33.refs_0_, bf16[6,3,16,128]{3,2,1,0:T(8,128)(2,1)S(1)} %collective-permute-done.6.refs_1_, ...), custom_call_target="tpu_custom_call" | custom-call | tf_op jit(solution)/shard_map/pallas_call | solution.py:317
  42.3 0.1 collective-permute-start.8
  42.4 3.5 %collective-permute-start.9 = (f32[32,4,128]{2,1,0:T(4,128)S(1)}, f32[32,4,128]{2,1,0:T(4,128)S(1)}, u32[]{:S(2)}, u32[]{:S(2)}) collective-permute-start(f32[32,4,128]{2,1,0:T(4,128)S(1)} %get-tuple-element.59), channel_id=1, source_target_pairs={{0,128},{64,192},{128,0},{192,64},{1,129},{65,193},{129,1},{193,65... | collective-permute-start | bytes 196616 | tf_op jit(solution)/shard_map/ppermute | solution.py:381
  45.9 1.2 %collective-permute-start.10 = (f32[32,4,128]{2,1,0:T(4,128)S(1)}, f32[32,4,128]{2,1,0:T(4,128)S(1)}, u32[]{:S(2)}, u32[]{:S(2)}) collective-permute-start(f32[32,4,128]{2,1,0:T(4,128)S(1)} %get-tuple-element.60), channel_id=1, source_target_pairs={{0,192},{64,128},{128,64},{192,0},{1,193},{65,129},{129,65},{193,1... | collective-permute-start | bytes 196616 | tf_op jit(solution)/shard_map/ppermute | solution.py:381
  47.1 0.0 collective-permute-done.8.p1
  47.1 1.8 %collective-permute-done.9.p2 = f32[32,4,128]{2,1,0:T(4,128)S(1)} collective-permute-done((f32[32,4,128]{2,1,0:T(4,128)S(1)}, f32[32,4,128]{2,1,0:T(4,128)S(1)}, u32[]{:S(2)}, u32[]{:S(2)}) %collective-permute-start.9) | collective-permute-done | bytes 65568 | tf_op jit(solution)/shard_map/ppermute | solution.py:381
  48.9 2.5 %collective-permute-done.10.p3 = f32[32,4,128]{2,1,0:T(4,128)S(1)} collective-permute-done((f32[32,4,128]{2,1,0:T(4,128)S(1)}, f32[32,4,128]{2,1,0:T(4,128)S(1)}, u32[]{:S(2)}, u32[]{:S(2)}) %collective-permute-start.10) | collective-permute-done | bytes 65568 | tf_op jit(solution)/shard_map/ppermute | solution.py:381
  51.4 0.9 %join.1 = f32[32,4,448]{2,1,0:T(4,128)} custom-call(f32[32,4,128]{2,1,0:T(4,128)S(1)} %get-tuple-element.57.p0, f32[32,4,128]{2,1,0:T(4,128)S(1)} %collective-permute-done.8.p1, f32[32,4,128]{2,1,0:T(4,128)S(1)} %collective-permute-done.9.p2, f32[32,4,128]{2,1,0:T(4,128)S(1)} %collective-permute-done.10.p3), custom_call_target="tpu_custom_call" | custom-call | tf_op jit(solution)/shard_map/join/pallas_call | solution.py:370
Async XLA Ops:
  1.2 15.7 %collective-permute-start.1 = (bf16[4,16,128]{2,1,0:T(8,128)(2,1)S(1)}, bf16[4,16,128]{2,1,0:T(8,128)(2,1)S(1)}, u32[]{:S(2)}, u32[]{:S(2)}) collective-permute-start(bf16[4,16,128]{2,1,0:T(8,128)(2,1)S(1)} %get-tuple-element.35), channel_id=1, source_target_pairs={{0,129},{1,128},{2,131},{3,130},{4,133},{5,132},{6,135},{7,134},{8... | collective-permute-start | bytes 49160 | tf_op jit(solution)/shard_map/ppermute | solution.py:391
  3.8 15.5 %collective-permute-start = (bf16[3,16,128]{2,1,0:T(8,128)(2,1)S(1)}, bf16[3,16,128]{2,1,0:T(8,128)(2,1)S(1)}, u32[]{:S(2)}, u32[]{:S(2)}) collective-permute-start(bf16[3,16,128]{2,1,0:T(8,128)(2,1)S(1)} %get-tuple-element.34), channel_id=1, source_target_pairs={{1,2},{3,4},{5,6},{7,8},{9,10},{11,12},{13,14},{15,16},{17,18},{19... | collective-permute-start | bytes 36872 | tf_op jit(solution)/shard_map/ppermute | solution.py:385
  12.0 4.9 %collective-permute-start.3 = (bf16[16,128]{1,0:T(8,128)(2,1)S(1)}, bf16[16,128]{1,0:T(8,128)(2,1)S(1)}, u32[]{:S(2)}, u32[]{:S(2)}) collective-permute-start(bf16[16,128]{1,0:T(8,128)(2,1)S(1)} %get-tuple-element.36.refs_2_), channel_id=1, source_target_pairs={{0,192},{64,128},{128,64},{192,0},{1,193},{65,129},{129,65},{193,1... | collective-permute-start | bytes 12296 | tf_op jit(solution)/shard_map/ppermute | solution.py:381
  13.2 3.7 %collective-permute-start.2 = (bf16[16,128]{1,0:T(8,128)(2,1)S(1)}, bf16[16,128]{1,0:T(8,128)(2,1)S(1)}, u32[]{:S(2)}, u32[]{:S(2)}) collective-permute-start(bf16[16,128]{1,0:T(8,128)(2,1)S(1)} %get-tuple-element.36.refs_2_), channel_id=1, source_target_pairs={{0,64},{64,0},{128,192},{192,128},{1,65},{65,1},{129,193},{193,129... | collective-permute-start | bytes 12296 | tf_op jit(solution)/shard_map/ppermute | solution.py:381
  21.8 3.1 %collective-permute-start.5 = (bf16[7,3,16,128]{3,2,1,0:T(8,128)(2,1)S(1)}, bf16[7,3,16,128]{3,2,1,0:T(8,128)(2,1)S(1)}, u32[]{:S(2)}, u32[]{:S(2)}) collective-permute-start(bf16[7,3,16,128]{3,2,1,0:T(8,128)(2,1)S(1)} %get-tuple-element.47), channel_id=1, source_target_pairs={{0,1},{2,3},{4,5},{6,7},{8,9},{10,11},{12,13},{14,15},{16,17},{18,... | collective-permute-start | bytes 258056 | tf_op jit(solution)/shard_map/ppermute | solution.py:385
  21.9 7.9 %collective-permute-start.4 = (bf16[7,3,16,128]{3,2,1,0:T(8,128)(2,1)S(1)}, bf16[7,3,16,128]{3,2,1,0:T(8,128)(2,1)S(1)}, u32[]{:S(2)}, u32[]{:S(2)}) collective-permute-start(bf16[7,3,16,128]{3,2,1,0:T(8,128)(2,1)S(1)} %get-tuple-element.45), channel_id=1, source_target_pairs={{1,2},{3,4},{5,6},{7,8},{9,10},{11,12},{13,14},{15,16},{17,18},{19... | collective-permute-start | bytes 258056 | tf_op jit(solution)/shard_map/ppermute | solution.py:385
  32.3 3.3 %collective-permute-start.7 = (bf16[6,3,16,128]{3,2,1,0:T(8,128)(2,1)S(1)}, bf16[6,3,16,128]{3,2,1,0:T(8,128)(2,1)S(1)}, u32[]{:S(2)}, u32[]{:S(2)}) collective-permute-start(bf16[6,3,16,128]{3,2,1,0:T(8,128)(2,1)S(1)} %get-tuple-element.53), channel_id=1, source_target_pairs={{0,1},{2,3},{4,5},{6,7},{8,9},{10,11},{12,13},{14,15},{16,17},{18,... | collective-permute-start | bytes 221192 | tf_op jit(solution)/shard_map/ppermute | solution.py:385
  32.4 7.8 %collective-permute-start.6 = (bf16[6,3,16,128]{3,2,1,0:T(8,128)(2,1)S(1)}, bf16[6,3,16,128]{3,2,1,0:T(8,128)(2,1)S(1)}, u32[]{:S(2)}, u32[]{:S(2)}) collective-permute-start(bf16[6,3,16,128]{3,2,1,0:T(8,128)(2,1)S(1)} %get-tuple-element.51), channel_id=1, source_target_pairs={{1,2},{3,4},{5,6},{7,8},{9,10},{11,12},{13,14},{15,16},{17,18},{19... | collective-permute-start | bytes 221192 | tf_op jit(solution)/shard_map/ppermute | solution.py:385
  42.3 4.8 %collective-permute-start.8 = (f32[32,4,128]{2,1,0:T(4,128)S(1)}, f32[32,4,128]{2,1,0:T(4,128)S(1)}, u32[]{:S(2)}, u32[]{:S(2)}) collective-permute-start(f32[32,4,128]{2,1,0:T(4,128)S(1)} %get-tuple-element.58), channel_id=1, source_target_pairs={{0,64},{64,0},{128,192},{192,128},{1,65},{65,1},{129,193},{193,129... | collective-permute-start | bytes 196616 | tf_op jit(solution)/shard_map/ppermute | solution.py:381
  42.4 6.5 %collective-permute-start.9 = (f32[32,4,128]{2,1,0:T(4,128)S(1)}, f32[32,4,128]{2,1,0:T(4,128)S(1)}, u32[]{:S(2)}, u32[]{:S(2)}) collective-permute-start(f32[32,4,128]{2,1,0:T(4,128)S(1)} %get-tuple-element.59), channel_id=1, source_target_pairs={{0,128},{64,192},{128,0},{192,64},{1,129},{65,193},{129,1},{193,65... | collective-permute-start | bytes 196616 | tf_op jit(solution)/shard_map/ppermute | solution.py:381
  45.9 5.5 %collective-permute-start.10 = (f32[32,4,128]{2,1,0:T(4,128)S(1)}, f32[32,4,128]{2,1,0:T(4,128)S(1)}, u32[]{:S(2)}, u32[]{:S(2)}) collective-permute-start(f32[32,4,128]{2,1,0:T(4,128)S(1)} %get-tuple-element.60), channel_id=1, source_target_pairs={{0,192},{64,128},{128,64},{192,0},{1,193},{65,129},{129,65},{193,1... | collective-permute-start | bytes 196616 | tf_op jit(solution)/shard_map/ppermute | solution.py:381

commit v6 on v5

--- a/solution.py
+++ b/solution.py
@@ -122,8 +122,8 @@
 
 
 def tables(tm, smalls, w_conv, w_in, steps, gathered):
-    for k in range(4):
-        gathered[tm ^ k] = smalls[k].astype(F32)
+    for k, small in smalls:
+        gathered[tm ^ k] = small.astype(F32)
     high, middle, rest = [jnp.concatenate([gathered[t, at:at + 2] for t in range(4)], axis=0) * 0.5 for at in (0, 4, 8)]
     steps[...] = sum(jnp.concatenate([gathered[t, at:at + 2] for t in range(4)], axis=0) for at in (2, 6, 10))
     tail = jnp.concatenate([jnp.zeros((64, F), F32), high, middle, rest, jnp.zeros((40, F), F32)], axis=0)
@@ -226,8 +226,9 @@
 
 def first_part(rounds, *refs):
     if rounds == 0:
-        lat, from_a, own, one, three, w_conv, w_mid, w_out, kept_h, kept_s, done, w_in, steps, *rest = refs
-        smalls = [own[...], one[...], from_a[3], three[...]]
+        lat, from_a, own, mixed, swapped, w_conv, w_mid, w_out, kept_h, kept_s, done, w_in, steps, *rest = refs
+        core = lax.axis_index("pix") % 2
+        smalls = [(0, own[...]), (2, from_a[3]), (1 + 2 * core, mixed[...]), (3 - 2 * core, swapped[...])]
         tables(lax.axis_index("tm"), smalls, w_conv, w_in, steps, rest.pop())
         prior = None
     else:
@@ -385,9 +386,13 @@
     return lax.ppermute(x, "pix", [(a, b) for a, b in pairs] + [(b, a) for a, b in pairs])
 
 
-def partner_of_other_half(x):
+def over_both(x, target):
     pixels = lax.axis_size("pix")
-    pairs = [(t * pixels + p, (t ^ 2) * pixels + (p ^ 1)) for t in range(4) for p in range(pixels)]
+    pairs = []
+    for t in range(4):
+        for p in range(pixels):
+            to_t, to_p = target(t, p)
+            pairs.append((t * pixels + p, to_t * pixels + to_p))
     return lax.ppermute(x, ("tm", "pix"), pairs)
 
 
@@ -397,14 +402,14 @@
 
 def shards(latent, step_size, time_embed, conv_in, conv_mid, conv_out):
     lat, to_a, to_b, small = enter(step_size, latent, time_embed)
-    smalls = [small]
-    for k in (1, 3):
-        smalls.append(across(small, k))
+    mixed = over_both(small, lambda t, p: (t ^ (1 + 2 * (p % 2)), p))
+    swapped = pair_up(mixed, CORES)
+    smalls = [small, mixed, swapped]
     w_conv, w_mid, w_out = prepare(conv_in.transpose(0, 1, 3, 2), conv_mid, conv_out)
     prior = ()
     for rounds in range(3):
         from_b = pair_up(to_b, CHIPS)
-        from_a = pair_up(to_a, CORES) if rounds else partner_of_other_half(to_a)
+        from_a = pair_up(to_a, CORES) if rounds else over_both(to_a, lambda t, p: (t ^ 2, p ^ 1))
         if rounds == 0:
             *kept, w_in, steps = run_first(0, lat, from_a, *smalls, w_conv, w_mid, w_out)
         else:

time: 52.5 us -> 52.1 us (level)
  starting transfers between devices: 23.1 us -> 22.2 us
  waiting for transfers between devices: 11.8 us -> 12.4 us
    ppermute x5 -> x3, waiting for transfers between devices: 6.69 us -> 3.38 us  [across(): return lax.ppermute(x, 'tm', [(t, t ^ k) for t in range(4)])]
    ppermute x1 -> x2, waiting for transfers between devices: 0.01 us -> 3.02 us  [over_both(): return lax.ppermute(x, ('tm', 'pix'), pairs)]
    ppermute x5 -> x3, starting transfers between devices: 6.01 us -> 4.79 us  [across(): return lax.ppermute(x, 'tm', [(t, t ^ k) for t in range(4)])]
    ppermute x5 -> x6, waiting for transfers between devices: 5.1 us -> 6.02 us  [pair_up(): lax.ppermute(x, 'pix', [(a, b) for a, b in pairs] + [(b, a) for a, b in p...]
    ppermute x1 -> x2, starting transfers between devices: 2.55 us -> 3.22 us  [over_both(): return lax.ppermute(x, ('tm', 'pix'), pairs)]
    ppermute x5 -> x6, starting transfers between devices: 14.6 us -> 14.2 us  [pair_up(): lax.ppermute(x, 'pix', [(a, b) for a, b in pairs] + [(b, a) for a, b in p...]
where the time goes in v6:
time: 52.1 us; the launch traced here: 51.9 us
  starting transfers between devices  22.2 us (43%)
  Pallas kernels  17.2 us (33%)
  waiting for transfers between devices  12.4 us (24%)
    ppermute x6, starting transfers between devices, pair_up(): lax.ppermute(x, 'pix', [(a, b) for a, b in pairs] + [(b, a) for a, b in p...  14.2 us
    pallas_call x6, Pallas kernels, call(): pl.pallas_call(functools.partial(body, rounds), out_shape=out_shape, in_s...  13.9 us
    ppermute x6, waiting for transfers between devices, pair_up(): lax.ppermute(x, 'pix', [(a, b) for a, b in pairs] + [(b, a) for a, b in p...  6.02 us
    ppermute x3, starting transfers between devices, across(): return lax.ppermute(x, 'tm', [(t, t ^ k) for t in range(4)])  4.79 us
    ppermute x3, waiting for transfers between devices, across(): return lax.ppermute(x, 'tm', [(t, t ^ k) for t in range(4)])  3.38 us
    ppermute x2, starting transfers between devices, over_both(): return lax.ppermute(x, ('tm', 'pix'), pairs)  3.22 us
    ppermute x2, waiting for transfers between devices, over_both(): return lax.ppermute(x, ('tm', 'pix'), pairs)  3.02 us
    pallas_call x1, Pallas kernels, prepare(): pl.pallas_call(prepare_body, out_shape=tuple((jax.ShapeDtypeStruct(shape,...  1.24 us
  transfers between devices with their start and end apart: 11, of which 5 were waited for; matrix products, arithmetic and copies ran while one was open for 0% of the time, Pallas kernels for 15%

profile of v6, /device:TPU:24, one launch (start us, length us, event | category | flops | bytes accessed | tf_op | source)
XLA Modules:
  0.0 51.9 jit_solution(15708639224480937226)
XLA Ops:
  0.0 1.2 %enter.1 = (f32[4,16,128]{2,1,0:T(8,128)S(1)}, bf16[4,16,128]{2,1,0:T(8,128)(2,1)S(1)}, bf16[3,16,128]{2,1,0:T(8,128)(2,1)S(1)}, bf16[16,128]{1,0:T(8,128)(2,1)S(1)}) custom-call(f32[2]{0:T(128)} %step.1, f32[16,4,448]{2,1,0:T(4,128)} %latent.1, f32[2,128]{1,0:T(2,128)} %embed.1), custom_call_target="tpu_custom_call" | custom-call | tf_op jit(solution)/shard_map/enter/pallas_call | solution.py:64
  1.2 2.5 %collective-permute-start.1 = (bf16[4,16,128]{2,1,0:T(8,128)(2,1)S(1)}, bf16[4,16,128]{2,1,0:T(8,128)(2,1)S(1)}, u32[]{:S(2)}, u32[]{:S(2)}) collective-permute-start(bf16[4,16,128]{2,1,0:T(8,128)(2,1)S(1)} %get-tuple-element.35), channel_id=1, source_target_pairs={{0,129},{1,128},{2,131},{3,130},{4,133},{5,132},{6,135},{7,134},{8... | collective-permute-start | bytes 49160 | tf_op jit(solution)/shard_map/ppermute | solution.py:396
  3.8 8.2 %collective-permute-start = (bf16[3,16,128]{2,1,0:T(8,128)(2,1)S(1)}, bf16[3,16,128]{2,1,0:T(8,128)(2,1)S(1)}, u32[]{:S(2)}, u32[]{:S(2)}) collective-permute-start(bf16[3,16,128]{2,1,0:T(8,128)(2,1)S(1)} %get-tuple-element.34), channel_id=1, source_target_pairs={{1,2},{3,4},{5,6},{7,8},{9,10},{11,12},{13,14},{15,16},{17,18},{19... | collective-permute-start | bytes 36872 | tf_op jit(solution)/shard_map/ppermute | solution.py:386
  12.0 0.7 %collective-permute-start.2 = (bf16[16,128]{1,0:T(8,128)(2,1)S(1)}, bf16[16,128]{1,0:T(8,128)(2,1)S(1)}, u32[]{:S(2)}, u32[]{:S(2)}) collective-permute-start(bf16[16,128]{1,0:T(8,128)(2,1)S(1)} %get-tuple-element.36.refs_2_), channel_id=1, source_target_pairs={{0,64},{1,193},{2,66},{3,195},{4,68},{5,197},{6,70},{7,199},{8,72}... | collective-permute-start | bytes 12296 | tf_op jit(solution)/shard_map/ppermute | solution.py:396
  12.7 3.0 %collective-permute-done.2.refs_3_ = bf16[16,128]{1,0:T(8,128)(2,1)S(1)} collective-permute-done((bf16[16,128]{1,0:T(8,128)(2,1)S(1)}, bf16[16,128]{1,0:T(8,128)(2,1)S(1)}, u32[]{:S(2)}, u32[]{:S(2)}) %collective-permute-start.2) | collective-permute-done | bytes 4128 | tf_op jit(solution)/shard_map/ppermute | solution.py:396
  15.7 0.0 collective-permute-start.3
  15.7 1.2 %prepare.1 = (bf16[384,256]{1,0:T(8,128)(2,1)S(1)}, bf16[896,512]{1,0:T(8,128)(2,1)S(1)}, bf16[96,512]{1,0:T(8,128)(2,1)S(1)}) custom-call(bf16[3,3,16,128]{3,2,1,0:T(8,128)(2,1)} %bitcast.2, bf16[3,3,128,128]{3,2,1,0:T(8,128)(2,1)} %conv_mid.1, bf16[3,3,16,128]{3,2,1,0:T(8,128)(2,1)} %conv_out.1), custom_call_target="tpu_custom_call" | custom-call | tf_op jit(solution)/shard_map/prepare/pallas_call | solution.py:107
  16.9 0.0 collective-permute-done.3.refs_4_
  16.9 0.0 collective-permute-done.1.refs_1_
  17.0 2.4 %shard_map.64 = (bf16[4,256,256]{2,1,0:T(8,128)(2,1)S(1)}, bf16[4,256,256]{2,1,0:T(8,128)(2,1)S(1)}, f32[9,16,128]{2,1,0:T(8,128)S(1)}, bf16[384,256]{1,0:T(8,128)(2,1)S(1)}, f32[8,128]{1,0:T(8,128)S(1)}) custom-call(f32[4,16,128]{2,1,0:T(8,128)S(1)} %get-tuple-element.33.refs_0_, bf16[4,16,128]{2,1,0:T(8,128)(2,1)S(1)} %collective-permute-done.1.refs_1_, ...), custom_call_target="tpu_custom_call" | custom-call | tf_op jit(solution)/shard_map/pallas_call | solution.py:318
  19.4 0.0 collective-permute-done.refs_1_
  19.4 2.5 %shard_map.65 = (f32[9,4,16,128]{3,2,1,0:T(8,128)S(1)}, bf16[7,3,16,128]{3,2,1,0:T(8,128)(2,1)S(1)}, bf16[7,3,16,128]{3,2,1,0:T(8,128)(2,1)S(1)}) custom-call(f32[4,16,128]{2,1,0:T(8,128)S(1)} %get-tuple-element.33.refs_0_, bf16[3,16,128]{2,1,0:T(8,128)(2,1)S(1)} %collective-permute-done.refs_1_, bf16[4,256,256]{2,1,0:T(8,128)(2,1)S(1)} %get-tuple-element.40.refs_2_, ...), custom_call_target="tpu_custom_call" | custom-call | tf_op jit(solution)/shard_map/pallas_call | solution.py:318
  21.9 0.6 %collective-permute-start.5 = (bf16[7,3,16,128]{3,2,1,0:T(8,128)(2,1)S(1)}, bf16[7,3,16,128]{3,2,1,0:T(8,128)(2,1)S(1)}, u32[]{:S(2)}, u32[]{:S(2)}) collective-permute-start(bf16[7,3,16,128]{3,2,1,0:T(8,128)(2,1)S(1)} %get-tuple-element.47), channel_id=1, source_target_pairs={{0,1},{2,3},{4,5},{6,7},{8,9},{10,11},{12,13},{14,15},{16,17},{18,... | collective-permute-start | bytes 258056 | tf_op jit(solution)/shard_map/ppermute | solution.py:386
  22.5 2.5 %collective-permute-start.4 = (bf16[7,3,16,128]{3,2,1,0:T(8,128)(2,1)S(1)}, bf16[7,3,16,128]{3,2,1,0:T(8,128)(2,1)S(1)}, u32[]{:S(2)}, u32[]{:S(2)}) collective-permute-start(bf16[7,3,16,128]{3,2,1,0:T(8,128)(2,1)S(1)} %get-tuple-element.45), channel_id=1, source_target_pairs={{1,2},{3,4},{5,6},{7,8},{9,10},{11,12},{13,14},{15,16},{17,18},{19... | collective-permute-start | bytes 258056 | tf_op jit(solution)/shard_map/ppermute | solution.py:386
  25.0 0.0 collective-permute-done.5.refs_1_
  25.0 2.4 %shard_map.66 = (bf16[4,256,256]{2,1,0:T(8,128)(2,1)S(1)}, bf16[4,256,256]{2,1,0:T(8,128)(2,1)S(1)}, f32[9,16,128]{2,1,0:T(8,128)S(1)}) custom-call(f32[4,16,128]{2,1,0:T(8,128)S(1)} %get-tuple-element.33.refs_0_, bf16[7,3,16,128]{3,2,1,0:T(8,128)(2,1)S(1)} %collective-permute-done.5.refs_1_, f32[9,4,16,128]{3,2,1,0:T(8,128)S(1)} %get-tuple-element.46.refs_2_, ...), custom_call_target="tpu_custom_call" | custom-call | tf_op jit(solution)/shard_map/pallas_call | solution.py:318
  27.5 2.9 %collective-permute-done.4.refs_1_ = bf16[7,3,16,128]{3,2,1,0:T(8,128)(2,1)S(1)} collective-permute-done((bf16[7,3,16,128]{3,2,1,0:T(8,128)(2,1)S(1)}, bf16[7,3,16,128]{3,2,1,0:T(8,128)(2,1)S(1)}, u32[]{:S(2)}, u32[]{:S(2)}) %collective-permute-start.4) | collective-permute-done | bytes 86048 | tf_op jit(solution)/shard_map/ppermute | solution.py:386
  30.4 2.5 %shard_map.67 = (f32[9,4,16,128]{3,2,1,0:T(8,128)S(1)}, bf16[6,3,16,128]{3,2,1,0:T(8,128)(2,1)S(1)}, bf16[6,3,16,128]{3,2,1,0:T(8,128)(2,1)S(1)}) custom-call(f32[4,16,128]{2,1,0:T(8,128)S(1)} %get-tuple-element.33.refs_0_, bf16[7,3,16,128]{3,2,1,0:T(8,128)(2,1)S(1)} %collective-permute-done.4.refs_1_, f32[9,4,16,128]{3,2,1,0:T(8,128)S(1)} %get-tuple-element.46.refs_2_, ...), custom_call_target="tpu_custom_call" | custom-call | tf_op jit(solution)/shard_map/pallas_call | solution.py:318
  32.8 0.1 collective-permute-start.7
  32.9 2.7 %collective-permute-start.6 = (bf16[6,3,16,128]{3,2,1,0:T(8,128)(2,1)S(1)}, bf16[6,3,16,128]{3,2,1,0:T(8,128)(2,1)S(1)}, u32[]{:S(2)}, u32[]{:S(2)}) collective-permute-start(bf16[6,3,16,128]{3,2,1,0:T(8,128)(2,1)S(1)} %get-tuple-element.51), channel_id=1, source_target_pairs={{1,2},{3,4},{5,6},{7,8},{9,10},{11,12},{13,14},{15,16},{17,18},{19... | collective-permute-start | bytes 221192 | tf_op jit(solution)/shard_map/ppermute | solution.py:386
  35.7 0.0 collective-permute-done.7.refs_1_
  35.7 1.9 %shard_map.68 = (bf16[3,256,256]{2,1,0:T(8,128)(2,1)S(1)}, bf16[3,256,256]{2,1,0:T(8,128)(2,1)S(1)}, f32[9,16,128]{2,1,0:T(8,128)S(1)}) custom-call(f32[4,16,128]{2,1,0:T(8,128)S(1)} %get-tuple-element.33.refs_0_, bf16[6,3,16,128]{3,2,1,0:T(8,128)(2,1)S(1)} %collective-permute-done.7.refs_1_, f32[9,4,16,128]{3,2,1,0:T(8,128)S(1)} %get-tuple-element.52.refs_2_, ...), custom_call_target="tpu_custom_call" | custom-call | tf_op jit(solution)/shard_map/pallas_call | solution.py:318
  37.6 3.1 %collective-permute-done.6.refs_1_ = bf16[6,3,16,128]{3,2,1,0:T(8,128)(2,1)S(1)} collective-permute-done((bf16[6,3,16,128]{3,2,1,0:T(8,128)(2,1)S(1)}, bf16[6,3,16,128]{3,2,1,0:T(8,128)(2,1)S(1)}, u32[]{:S(2)}, u32[]{:S(2)}) %collective-permute-start.6) | collective-permute-done | bytes 73760 | tf_op jit(solution)/shard_map/ppermute | solution.py:386
  40.7 2.1 %shard_map.69 = (f32[32,4,128]{2,1,0:T(4,128)S(1)}, f32[32,4,128]{2,1,0:T(4,128)S(1)}, f32[32,4,128]{2,1,0:T(4,128)S(1)}, f32[32,4,128]{2,1,0:T(4,128)S(1)}) custom-call(f32[4,16,128]{2,1,0:T(8,128)S(1)} %get-tuple-element.33.refs_0_, bf16[6,3,16,128]{3,2,1,0:T(8,128)(2,1)S(1)} %collective-permute-done.6.refs_1_, ...), custom_call_target="tpu_custom_call" | custom-call | tf_op jit(solution)/shard_map/pallas_call | solution.py:318
  42.9 0.7 %collective-permute-start.8 = (f32[32,4,128]{2,1,0:T(4,128)S(1)}, f32[32,4,128]{2,1,0:T(4,128)S(1)}, u32[]{:S(2)}, u32[]{:S(2)}) collective-permute-start(f32[32,4,128]{2,1,0:T(4,128)S(1)} %get-tuple-element.58), channel_id=1, source_target_pairs={{0,64},{64,0},{128,192},{192,128},{1,65},{65,1},{129,193},{193,129... | collective-permute-start | bytes 196616 | tf_op jit(solution)/shard_map/ppermute | solution.py:382
  43.5 2.0 %collective-permute-start.9 = (f32[32,4,128]{2,1,0:T(4,128)S(1)}, f32[32,4,128]{2,1,0:T(4,128)S(1)}, u32[]{:S(2)}, u32[]{:S(2)}) collective-permute-start(f32[32,4,128]{2,1,0:T(4,128)S(1)} %get-tuple-element.59), channel_id=1, source_target_pairs={{0,128},{64,192},{128,0},{192,64},{1,129},{65,193},{129,1},{193,65... | collective-permute-start | bytes 196616 | tf_op jit(solution)/shard_map/ppermute | solution.py:382
  45.5 2.1 %collective-permute-start.10 = (f32[32,4,128]{2,1,0:T(4,128)S(1)}, f32[32,4,128]{2,1,0:T(4,128)S(1)}, u32[]{:S(2)}, u32[]{:S(2)}) collective-permute-start(f32[32,4,128]{2,1,0:T(4,128)S(1)} %get-tuple-element.60), channel_id=1, source_target_pairs={{0,192},{64,128},{128,64},{192,0},{1,193},{65,129},{129,65},{193,1... | collective-permute-start | bytes 196616 | tf_op jit(solution)/shard_map/ppermute | solution.py:382
  47.6 0.0 collective-permute-done.8.p1
  47.6 1.7 %collective-permute-done.9.p2 = f32[32,4,128]{2,1,0:T(4,128)S(1)} collective-permute-done((f32[32,4,128]{2,1,0:T(4,128)S(1)}, f32[32,4,128]{2,1,0:T(4,128)S(1)}, u32[]{:S(2)}, u32[]{:S(2)}) %collective-permute-start.9) | collective-permute-done | bytes 65568 | tf_op jit(solution)/shard_map/ppermute | solution.py:382
  49.3 1.7 %collective-permute-done.10.p3 = f32[32,4,128]{2,1,0:T(4,128)S(1)} collective-permute-done((f32[32,4,128]{2,1,0:T(4,128)S(1)}, f32[32,4,128]{2,1,0:T(4,128)S(1)}, u32[]{:S(2)}, u32[]{:S(2)}) %collective-permute-start.10) | collective-permute-done | bytes 65568 | tf_op jit(solution)/shard_map/ppermute | solution.py:382
  51.0 0.9 %join.1 = f32[32,4,448]{2,1,0:T(4,128)} custom-call(f32[32,4,128]{2,1,0:T(4,128)S(1)} %get-tuple-element.57.p0, f32[32,4,128]{2,1,0:T(4,128)S(1)} %collective-permute-done.8.p1, f32[32,4,128]{2,1,0:T(4,128)S(1)} %collective-permute-done.9.p2, f32[32,4,128]{2,1,0:T(4,128)S(1)} %collective-permute-done.10.p3), custom_call_target="tpu_custom_call" | custom-call | tf_op jit(solution)/shard_map/join/pallas_call | solution.py:371
Async XLA Ops:
  1.2 15.7 %collective-permute-start.1 = (bf16[4,16,128]{2,1,0:T(8,128)(2,1)S(1)}, bf16[4,16,128]{2,1,0:T(8,128)(2,1)S(1)}, u32[]{:S(2)}, u32[]{:S(2)}) collective-permute-start(bf16[4,16,128]{2,1,0:T(8,128)(2,1)S(1)} %get-tuple-element.35), channel_id=1, source_target_pairs={{0,129},{1,128},{2,131},{3,130},{4,133},{5,132},{6,135},{7,134},{8... | collective-permute-start | bytes 49160 | tf_op jit(solution)/shard_map/ppermute | solution.py:396
  3.8 15.6 %collective-permute-start = (bf16[3,16,128]{2,1,0:T(8,128)(2,1)S(1)}, bf16[3,16,128]{2,1,0:T(8,128)(2,1)S(1)}, u32[]{:S(2)}, u32[]{:S(2)}) collective-permute-start(bf16[3,16,128]{2,1,0:T(8,128)(2,1)S(1)} %get-tuple-element.34), channel_id=1, source_target_pairs={{1,2},{3,4},{5,6},{7,8},{9,10},{11,12},{13,14},{15,16},{17,18},{19... | collective-permute-start | bytes 36872 | tf_op jit(solution)/shard_map/ppermute | solution.py:386
  12.0 3.7 %collective-permute-start.2 = (bf16[16,128]{1,0:T(8,128)(2,1)S(1)}, bf16[16,128]{1,0:T(8,128)(2,1)S(1)}, u32[]{:S(2)}, u32[]{:S(2)}) collective-permute-start(bf16[16,128]{1,0:T(8,128)(2,1)S(1)} %get-tuple-element.36.refs_2_), channel_id=1, source_target_pairs={{0,64},{1,193},{2,66},{3,195},{4,68},{5,197},{6,70},{7,199},{8,72}... | collective-permute-start | bytes 12296 | tf_op jit(solution)/shard_map/ppermute | solution.py:396
  15.7 1.3 %collective-permute-start.3 = (bf16[16,128]{1,0:T(8,128)(2,1)S(1)}, bf16[16,128]{1,0:T(8,128)(2,1)S(1)}, u32[]{:S(2)}, u32[]{:S(2)}) collective-permute-start(bf16[16,128]{1,0:T(8,128)(2,1)S(1)} %collective-permute-done.2.refs_3_), channel_id=1, source_target_pairs={{0,1},{2,3},{4,5},{6,7},{8,9},{10,11},{12,13},{14,15},{16,17},{18,... | collective-permute-start | bytes 12296 | tf_op jit(solution)/shard_map/ppermute | solution.py:386
  21.9 3.1 %collective-permute-start.5 = (bf16[7,3,16,128]{3,2,1,0:T(8,128)(2,1)S(1)}, bf16[7,3,16,128]{3,2,1,0:T(8,128)(2,1)S(1)}, u32[]{:S(2)}, u32[]{:S(2)}) collective-permute-start(bf16[7,3,16,128]{3,2,1,0:T(8,128)(2,1)S(1)} %get-tuple-element.47), channel_id=1, source_target_pairs={{0,1},{2,3},{4,5},{6,7},{8,9},{10,11},{12,13},{14,15},{16,17},{18,... | collective-permute-start | bytes 258056 | tf_op jit(solution)/shard_map/ppermute | solution.py:386
  22.5 7.9 %collective-permute-start.4 = (bf16[7,3,16,128]{3,2,1,0:T(8,128)(2,1)S(1)}, bf16[7,3,16,128]{3,2,1,0:T(8,128)(2,1)S(1)}, u32[]{:S(2)}, u32[]{:S(2)}) collective-permute-start(bf16[7,3,16,128]{3,2,1,0:T(8,128)(2,1)S(1)} %get-tuple-element.45), channel_id=1, source_target_pairs={{1,2},{3,4},{5,6},{7,8},{9,10},{11,12},{13,14},{15,16},{17,18},{19... | collective-permute-start | bytes 258056 | tf_op jit(solution)/shard_map/ppermute | solution.py:386
  32.8 2.8 %collective-permute-start.7 = (bf16[6,3,16,128]{3,2,1,0:T(8,128)(2,1)S(1)}, bf16[6,3,16,128]{3,2,1,0:T(8,128)(2,1)S(1)}, u32[]{:S(2)}, u32[]{:S(2)}) collective-permute-start(bf16[6,3,16,128]{3,2,1,0:T(8,128)(2,1)S(1)} %get-tuple-element.53), channel_id=1, source_target_pairs={{0,1},{2,3},{4,5},{6,7},{8,9},{10,11},{12,13},{14,15},{16,17},{18,... | collective-permute-start | bytes 221192 | tf_op jit(solution)/shard_map/ppermute | solution.py:386
  32.9 7.8 %collective-permute-start.6 = (bf16[6,3,16,128]{3,2,1,0:T(8,128)(2,1)S(1)}, bf16[6,3,16,128]{3,2,1,0:T(8,128)(2,1)S(1)}, u32[]{:S(2)}, u32[]{:S(2)}) collective-permute-start(bf16[6,3,16,128]{3,2,1,0:T(8,128)(2,1)S(1)} %get-tuple-element.51), channel_id=1, source_target_pairs={{1,2},{3,4},{5,6},{7,8},{9,10},{11,12},{13,14},{15,16},{17,18},{19... | collective-permute-start | bytes 221192 | tf_op jit(solution)/shard_map/ppermute | solution.py:386
  42.9 4.8 %collective-permute-start.8 = (f32[32,4,128]{2,1,0:T(4,128)S(1)}, f32[32,4,128]{2,1,0:T(4,128)S(1)}, u32[]{:S(2)}, u32[]{:S(2)}) collective-permute-start(f32[32,4,128]{2,1,0:T(4,128)S(1)} %get-tuple-element.58), channel_id=1, source_target_pairs={{0,64},{64,0},{128,192},{192,128},{1,65},{65,1},{129,193},{193,129... | collective-permute-start | bytes 196616 | tf_op jit(solution)/shard_map/ppermute | solution.py:382
  43.5 5.8 %collective-permute-start.9 = (f32[32,4,128]{2,1,0:T(4,128)S(1)}, f32[32,4,128]{2,1,0:T(4,128)S(1)}, u32[]{:S(2)}, u32[]{:S(2)}) collective-permute-start(f32[32,4,128]{2,1,0:T(4,128)S(1)} %get-tuple-element.59), channel_id=1, source_target_pairs={{0,128},{64,192},{128,0},{192,64},{1,129},{65,193},{129,1},{193,65... | collective-permute-start | bytes 196616 | tf_op jit(solution)/shard_map/ppermute | solution.py:382
  45.5 5.5 %collective-permute-start.10 = (f32[32,4,128]{2,1,0:T(4,128)S(1)}, f32[32,4,128]{2,1,0:T(4,128)S(1)}, u32[]{:S(2)}, u32[]{:S(2)}) collective-permute-start(f32[32,4,128]{2,1,0:T(4,128)S(1)} %get-tuple-element.60), channel_id=1, source_target_pairs={{0,192},{64,128},{128,64},{192,0},{1,193},{65,129},{129,65},{193,1... | collective-permute-start | bytes 196616 | tf_op jit(solution)/shard_map/ppermute | solution.py:382

commit v7 on v6

--- a/solution.py
+++ b/solution.py
@@ -35,11 +35,14 @@
     return high, middle, rest - middle
 
 
-def enter_body(step, latent, embed, lat, to_a, to_b, small, step_s, latent_v, embed_v, other, sems):
-    copies = [pltpu.make_async_copy(x, y, sems.at[i]) for i, (x, y) in enumerate(((latent, latent_v), (embed, embed_v), (step, step_s)))]
+def enter_body(step, latent, embed, *refs):
+    weights, (lat, to_a, to_b, small), fetched = refs[:3], refs[3:7], refs[7:10]
+    step_s, latent_v, embed_v, other, sems = refs[10:]
+    pairs = ((latent, latent_v), (embed, embed_v), (step, step_s), *zip(weights, fetched))
+    copies = [pltpu.make_async_copy(x, y, sems.at[i]) for i, (x, y) in enumerate(pairs)]
     for copy in copies:
         copy.start()
-    for copy in copies:
+    for copy in copies[:3]:
         copy.wait()
     tm, core = lax.axis_index("tm"), lax.axis_index("pix") % 2
     lane = lax.broadcasted_iota(jnp.int32, (C, L), 1)
@@ -57,37 +60,34 @@
     table = jnp.concatenate([*pieces_of(rows), jnp.zeros((4, F), F32)], axis=0).astype(BF)
     small[...] = table
     to_a[3] = table
-
-
-def enter(step, latent, embed):
-    shapes = ((4, C, L), (3, C, L), (16, F))
+    for copy in copies[3:]:
+        copy.wait()
+
+
+def enter(step, latent, embed, *weights):
+    shapes = ((4, C, L), (3, C, L), (16, F)) + tuple(w.shape for w in weights)
     return pl.pallas_call(
         enter_body,
         out_shape=(jax.ShapeDtypeStruct((ROWS, C, L), F32),) + tuple(jax.ShapeDtypeStruct(shape, BF) for shape in shapes),
-        in_specs=[ANY] * 3,
-        out_specs=(VM,) * 4,
+        in_specs=[ANY] * 6,
+        out_specs=(VM,) * 7,
         scratch_shapes=[
             pltpu.SMEM((2,), F32),
             pltpu.VMEM((C, ROWS, 448), F32),
             pltpu.VMEM((2, F), F32),
             pltpu.VMEM((ROWS, C, L), F32),
-            pltpu.SemaphoreType.DMA((3,)),
+            pltpu.SemaphoreType.DMA((6,)),
         ],
         compiler_params=pltpu.CompilerParams(vmem_limit_bytes=4 << 20),
         name="enter",
-    )(*[pltpu.with_memory_space_constraint(v, pltpu.HBM) for v in (step, latent, embed)])
-
-
-def prepare_body(conv_in, conv_mid, conv_out, w_in, w_mid, w_out, in_v, mid_v, out_v, turned, sems):
-    copies = [pltpu.make_async_copy(x, y, sems.at[i]) for i, (x, y) in enumerate(((conv_in, in_v), (conv_mid, mid_v), (conv_out, out_v)))]
-    for copy in copies:
-        copy.start()
+    )(*[pltpu.with_memory_space_constraint(v, pltpu.HBM) for v in (step, latent, embed, *weights)])
+
+
+def prepare_body(in_v, mid_v, out_v, w_in, w_mid, w_out, turned):
     core = lax.axis_index("pix") % 2
     w_mid[...] = jnp.zeros_like(w_mid)
     w_out[...] = jnp.zeros_like(w_out)
     turned[...] = jnp.zeros_like(turned)
-    for copy in copies:
-        copy.wait()
     for a in range(3):
         row = a + core * (2 - 2 * a)
         for b in range(3):
@@ -107,18 +107,14 @@
     return pl.pallas_call(
         prepare_body,
         out_shape=tuple(jax.ShapeDtypeStruct(shape, BF) for shape in shapes),
-        in_specs=[ANY] * 3,
+        in_specs=[VM] * 3,
         out_specs=(VM,) * 3,
         scratch_shapes=[
-            pltpu.VMEM((3, 3, C, F), BF),
-            pltpu.VMEM((3, 3, F, F), BF),
-            pltpu.VMEM((3, 3, C, F), BF),
             pltpu.VMEM((2 * F, 2 * F), BF),
-            pltpu.SemaphoreType.DMA((3,)),
         ],
         compiler_params=pltpu.CompilerParams(vmem_limit_bytes=8 << 20),
         name="prepare",
-    )(*[pltpu.with_memory_space_constraint(v, pltpu.HBM) for v in (conv_in, conv_mid, conv_out)])
+    )(conv_in, conv_mid, conv_out)
 
 
 def tables(tm, smalls, w_conv, w_in, steps, gathered):
@@ -401,11 +397,11 @@
 
 
 def shards(latent, step_size, time_embed, conv_in, conv_mid, conv_out):
-    lat, to_a, to_b, small = enter(step_size, latent, time_embed)
+    lat, to_a, to_b, small, *weights = enter(step_size, latent, time_embed, conv_in.transpose(0, 1, 3, 2), conv_mid, conv_out)
     mixed = over_both(small, lambda t, p: (t ^ (1 + 2 * (p % 2)), p))
     swapped = pair_up(mixed, CORES)
     smalls = [small, mixed, swapped]
-    w_conv, w_mid, w_out = prepare(conv_in.transpose(0, 1, 3, 2), conv_mid, conv_out)
+    w_conv, w_mid, w_out = prepare(*weights)
     prior = ()
     for rounds in range(3):
         from_b = pair_up(to_b, CHIPS)

time: 52.1 us -> 51.7 us (level)
  Pallas kernels: 17.2 us -> 16.3 us
    pallas_call x1, Pallas kernels: 1.24 us -> 0.28 us  [prepare(): pl.pallas_call(prepare_body, out_shape=tuple((jax.ShapeDtypeStruct(shape,...]
  transfers between devices with their start and end apart: 11 -> 11, of which waited for: 5 -> 6; matrix products, arithmetic and copies ran while one was open for 0% -> 0% of each run, Pallas kernels for 15% -> 14%
where the time goes in v7:
time: 51.7 us; the launch traced here: 51.5 us
  starting transfers between devices  22.5 us (44%)
  Pallas kernels  16.3 us (32%)
  waiting for transfers between devices  12.7 us (25%)
    ppermute x6, starting transfers between devices, pair_up(): lax.ppermute(x, 'pix', [(a, b) for a, b in pairs] + [(b, a) for a, b in p...  14.4 us
    pallas_call x6, Pallas kernels, call(): pl.pallas_call(functools.partial(body, rounds), out_shape=out_shape, in_s...  13.9 us
    ppermute x6, waiting for transfers between devices, pair_up(): lax.ppermute(x, 'pix', [(a, b) for a, b in pairs] + [(b, a) for a, b in p...  6.26 us
    ppermute x3, starting transfers between devices, across(): return lax.ppermute(x, 'tm', [(t, t ^ k) for t in range(4)])  4.79 us
    ppermute x3, waiting for transfers between devices, across(): return lax.ppermute(x, 'tm', [(t, t ^ k) for t in range(4)])  3.38 us
    ppermute x2, starting transfers between devices, over_both(): return lax.ppermute(x, ('tm', 'pix'), pairs)  3.22 us
    ppermute x2, waiting for transfers between devices, over_both(): return lax.ppermute(x, ('tm', 'pix'), pairs)  3.02 us
    pallas_call x1, Pallas kernels, enter(): pl.pallas_call(enter_body, out_shape=(jax.ShapeDtypeStruct((ROWS, C, L),...  1.23 us
  transfers between devices with their start and end apart: 11, of which 6 were waited for; matrix products, arithmetic and copies ran while one was open for 0% of the time, Pallas kernels for 14%

profile of v7, /device:TPU:24, one launch (start us, length us, event | category | flops | bytes accessed | tf_op | source)
XLA Modules:
  0.0 51.5 jit_solution(14694988520591945436)
XLA Ops:
  0.0 1.2 %enter.1 = (f32[4,16,128]{2,1,0:T(8,128)S(1)}, bf16[4,16,128]{2,1,0:T(8,128)(2,1)S(1)}, bf16[3,16,128]{2,1,0:T(8,128)(2,1)S(1)}, bf16[16,128]{1,0:T(8,128)(2,1)S...) custom-call(f32[2]{0:T(128)} %step.1, ...), custom_call_target="tpu_custom_call" | custom-call | tf_op jit(solution)/shard_map/enter/pallas_call | solution.py:69
  1.2 2.5 %collective-permute-start.1 = (bf16[4,16,128]{2,1,0:T(8,128)(2,1)S(1)}, bf16[4,16,128]{2,1,0:T(8,128)(2,1)S(1)}, u32[]{:S(2)}, u32[]{:S(2)}) collective-permute-start(bf16[4,16,128]{2,1,0:T(8,128)(2,1)S(1)} %get-tuple-element.38), channel_id=1, source_target_pairs={{0,129},{1,128},{2,131},{3,130},{4,133},{5,132},{6,135},{7,134},{8... | collective-permute-start | bytes 49160 | tf_op jit(solution)/shard_map/ppermute | solution.py:392
  3.8 8.2 %collective-permute-start = (bf16[3,16,128]{2,1,0:T(8,128)(2,1)S(1)}, bf16[3,16,128]{2,1,0:T(8,128)(2,1)S(1)}, u32[]{:S(2)}, u32[]{:S(2)}) collective-permute-start(bf16[3,16,128]{2,1,0:T(8,128)(2,1)S(1)} %get-tuple-element.37), channel_id=1, source_target_pairs={{1,2},{3,4},{5,6},{7,8},{9,10},{11,12},{13,14},{15,16},{17,18},{19... | collective-permute-start | bytes 36872 | tf_op jit(solution)/shard_map/ppermute | solution.py:382
  12.0 0.7 %collective-permute-start.2 = (bf16[16,128]{1,0:T(8,128)(2,1)S(1)}, bf16[16,128]{1,0:T(8,128)(2,1)S(1)}, u32[]{:S(2)}, u32[]{:S(2)}) collective-permute-start(bf16[16,128]{1,0:T(8,128)(2,1)S(1)} %get-tuple-element.39.refs_2_), channel_id=1, source_target_pairs={{0,64},{1,193},{2,66},{3,195},{4,68},{5,197},{6,70},{7,199},{8,72}... | collective-permute-start | bytes 12296 | tf_op jit(solution)/shard_map/ppermute | solution.py:392
  12.7 3.0 %collective-permute-done.2.refs_3_ = bf16[16,128]{1,0:T(8,128)(2,1)S(1)} collective-permute-done((bf16[16,128]{1,0:T(8,128)(2,1)S(1)}, bf16[16,128]{1,0:T(8,128)(2,1)S(1)}, u32[]{:S(2)}, u32[]{:S(2)}) %collective-permute-start.2) | collective-permute-done | bytes 4128 | tf_op jit(solution)/shard_map/ppermute | solution.py:392
  15.7 0.0 collective-permute-start.3
  15.7 0.3 prepare.1
  16.0 0.9 %collective-permute-done.3.refs_4_ = bf16[16,128]{1,0:T(8,128)(2,1)S(1)} collective-permute-done((bf16[16,128]{1,0:T(8,128)(2,1)S(1)}, bf16[16,128]{1,0:T(8,128)(2,1)S(1)}, u32[]{:S(2)}, u32[]{:S(2)}) %collective-permute-start.3) | collective-permute-done | bytes 4128 | tf_op jit(solution)/shard_map/ppermute | solution.py:382
  16.9 0.0 collective-permute-done.1.refs_1_
  16.9 2.4 %shard_map.64 = (bf16[4,256,256]{2,1,0:T(8,128)(2,1)S(1)}, bf16[4,256,256]{2,1,0:T(8,128)(2,1)S(1)}, f32[9,16,128]{2,1,0:T(8,128)S(1)}, bf16[384,256]{1,0:T(8,128)(2,1)S(1)}, f32[8,128]{1,0:T(8,128)S(1)}) custom-call(f32[4,16,128]{2,1,0:T(8,128)S(1)} %get-tuple-element.36.refs_0_, bf16[4,16,128]{2,1,0:T(8,128)(2,1)S(1)} %collective-permute-done.1.refs_1_, ...), custom_call_target="tpu_custom_call" | custom-call | tf_op jit(solution)/shard_map/pallas_call | solution.py:314
  19.3 0.0 collective-permute-done.refs_1_
  19.3 2.5 %shard_map.65 = (f32[9,4,16,128]{3,2,1,0:T(8,128)S(1)}, bf16[7,3,16,128]{3,2,1,0:T(8,128)(2,1)S(1)}, bf16[7,3,16,128]{3,2,1,0:T(8,128)(2,1)S(1)}) custom-call(f32[4,16,128]{2,1,0:T(8,128)S(1)} %get-tuple-element.36.refs_0_, bf16[3,16,128]{2,1,0:T(8,128)(2,1)S(1)} %collective-permute-done.refs_1_, bf16[4,256,256]{2,1,0:T(8,128)(2,1)S(1)} %get-tuple-element.46.refs_2_, ...), custom_call_target="tpu_custom_call" | custom-call | tf_op jit(solution)/shard_map/pallas_call | solution.py:314
  21.8 0.3 collective-permute-start.5
  22.0 2.9 %collective-permute-start.4 = (bf16[7,3,16,128]{3,2,1,0:T(8,128)(2,1)S(1)}, bf16[7,3,16,128]{3,2,1,0:T(8,128)(2,1)S(1)}, u32[]{:S(2)}, u32[]{:S(2)}) collective-permute-start(bf16[7,3,16,128]{3,2,1,0:T(8,128)(2,1)S(1)} %get-tuple-element.51), channel_id=1, source_target_pairs={{1,2},{3,4},{5,6},{7,8},{9,10},{11,12},{13,14},{15,16},{17,18},{19... | collective-permute-start | bytes 258056 | tf_op jit(solution)/shard_map/ppermute | solution.py:382
  24.9 0.0 collective-permute-done.5.refs_1_
  24.9 2.4 %shard_map.66 = (bf16[4,256,256]{2,1,0:T(8,128)(2,1)S(1)}, bf16[4,256,256]{2,1,0:T(8,128)(2,1)S(1)}, f32[9,16,128]{2,1,0:T(8,128)S(1)}) custom-call(f32[4,16,128]{2,1,0:T(8,128)S(1)} %get-tuple-element.36.refs_0_, bf16[7,3,16,128]{3,2,1,0:T(8,128)(2,1)S(1)} %collective-permute-done.5.refs_1_, f32[9,4,16,128]{3,2,1,0:T(8,128)S(1)} %get-tuple-element.52.refs_2_, ...), custom_call_target="tpu_custom_call" | custom-call | tf_op jit(solution)/shard_map/pallas_call | solution.py:314
  27.4 2.6 %collective-permute-done.4.refs_1_ = bf16[7,3,16,128]{3,2,1,0:T(8,128)(2,1)S(1)} collective-permute-done((bf16[7,3,16,128]{3,2,1,0:T(8,128)(2,1)S(1)}, bf16[7,3,16,128]{3,2,1,0:T(8,128)(2,1)S(1)}, u32[]{:S(2)}, u32[]{:S(2)}) %collective-permute-start.4) | collective-permute-done | bytes 86048 | tf_op jit(solution)/shard_map/ppermute | solution.py:382
  29.9 2.5 %shard_map.67 = (f32[9,4,16,128]{3,2,1,0:T(8,128)S(1)}, bf16[6,3,16,128]{3,2,1,0:T(8,128)(2,1)S(1)}, bf16[6,3,16,128]{3,2,1,0:T(8,128)(2,1)S(1)}) custom-call(f32[4,16,128]{2,1,0:T(8,128)S(1)} %get-tuple-element.36.refs_0_, bf16[7,3,16,128]{3,2,1,0:T(8,128)(2,1)S(1)} %collective-permute-done.4.refs_1_, f32[9,4,16,128]{3,2,1,0:T(8,128)S(1)} %get-tuple-element.52.refs_2_, ...), custom_call_target="tpu_custom_call" | custom-call | tf_op jit(solution)/shard_map/pallas_call | solution.py:314
  32.4 0.1 collective-permute-start.7
  32.5 3.0 %collective-permute-start.6 = (bf16[6,3,16,128]{3,2,1,0:T(8,128)(2,1)S(1)}, bf16[6,3,16,128]{3,2,1,0:T(8,128)(2,1)S(1)}, u32[]{:S(2)}, u32[]{:S(2)}) collective-permute-start(bf16[6,3,16,128]{3,2,1,0:T(8,128)(2,1)S(1)} %get-tuple-element.57), channel_id=1, source_target_pairs={{1,2},{3,4},{5,6},{7,8},{9,10},{11,12},{13,14},{15,16},{17,18},{19... | collective-permute-start | bytes 221192 | tf_op jit(solution)/shard_map/ppermute | solution.py:382
  35.6 0.0 collective-permute-done.7.refs_1_
  35.6 1.9 %shard_map.68 = (bf16[3,256,256]{2,1,0:T(8,128)(2,1)S(1)}, bf16[3,256,256]{2,1,0:T(8,128)(2,1)S(1)}, f32[9,16,128]{2,1,0:T(8,128)S(1)}) custom-call(f32[4,16,128]{2,1,0:T(8,128)S(1)} %get-tuple-element.36.refs_0_, bf16[6,3,16,128]{3,2,1,0:T(8,128)(2,1)S(1)} %collective-permute-done.7.refs_1_, f32[9,4,16,128]{3,2,1,0:T(8,128)S(1)} %get-tuple-element.58.refs_2_, ...), custom_call_target="tpu_custom_call" | custom-call | tf_op jit(solution)/shard_map/pallas_call | solution.py:314
  37.5 2.8 %collective-permute-done.6.refs_1_ = bf16[6,3,16,128]{3,2,1,0:T(8,128)(2,1)S(1)} collective-permute-done((bf16[6,3,16,128]{3,2,1,0:T(8,128)(2,1)S(1)}, bf16[6,3,16,128]{3,2,1,0:T(8,128)(2,1)S(1)}, u32[]{:S(2)}, u32[]{:S(2)}) %collective-permute-start.6) | collective-permute-done | bytes 73760 | tf_op jit(solution)/shard_map/ppermute | solution.py:382
  40.3 2.1 %shard_map.69 = (f32[32,4,128]{2,1,0:T(4,128)S(1)}, f32[32,4,128]{2,1,0:T(4,128)S(1)}, f32[32,4,128]{2,1,0:T(4,128)S(1)}, f32[32,4,128]{2,1,0:T(4,128)S(1)}) custom-call(f32[4,16,128]{2,1,0:T(8,128)S(1)} %get-tuple-element.36.refs_0_, bf16[6,3,16,128]{3,2,1,0:T(8,128)(2,1)S(1)} %collective-permute-done.6.refs_1_, ...), custom_call_target="tpu_custom_call" | custom-call | tf_op jit(solution)/shard_map/pallas_call | solution.py:314
  42.4 0.7 %collective-permute-start.8 = (f32[32,4,128]{2,1,0:T(4,128)S(1)}, f32[32,4,128]{2,1,0:T(4,128)S(1)}, u32[]{:S(2)}, u32[]{:S(2)}) collective-permute-start(f32[32,4,128]{2,1,0:T(4,128)S(1)} %get-tuple-element.64), channel_id=1, source_target_pairs={{0,64},{64,0},{128,192},{192,128},{1,65},{65,1},{129,193},{193,129... | collective-permute-start | bytes 196616 | tf_op jit(solution)/shard_map/ppermute | solution.py:378
  43.1 2.0 %collective-permute-start.9 = (f32[32,4,128]{2,1,0:T(4,128)S(1)}, f32[32,4,128]{2,1,0:T(4,128)S(1)}, u32[]{:S(2)}, u32[]{:S(2)}) collective-permute-start(f32[32,4,128]{2,1,0:T(4,128)S(1)} %get-tuple-element.65), channel_id=1, source_target_pairs={{0,128},{64,192},{128,0},{192,64},{1,129},{65,193},{129,1},{193,65... | collective-permute-start | bytes 196616 | tf_op jit(solution)/shard_map/ppermute | solution.py:378
  45.1 2.1 %collective-permute-start.10 = (f32[32,4,128]{2,1,0:T(4,128)S(1)}, f32[32,4,128]{2,1,0:T(4,128)S(1)}, u32[]{:S(2)}, u32[]{:S(2)}) collective-permute-start(f32[32,4,128]{2,1,0:T(4,128)S(1)} %get-tuple-element.66), channel_id=1, source_target_pairs={{0,192},{64,128},{128,64},{192,0},{1,193},{65,129},{129,65},{193,1... | collective-permute-start | bytes 196616 | tf_op jit(solution)/shard_map/ppermute | solution.py:378
  47.2 0.0 collective-permute-done.8.p1
  47.2 1.7 %collective-permute-done.9.p2 = f32[32,4,128]{2,1,0:T(4,128)S(1)} collective-permute-done((f32[32,4,128]{2,1,0:T(4,128)S(1)}, f32[32,4,128]{2,1,0:T(4,128)S(1)}, u32[]{:S(2)}, u32[]{:S(2)}) %collective-permute-start.9) | collective-permute-done | bytes 65568 | tf_op jit(solution)/shard_map/ppermute | solution.py:378
  48.9 1.7 %collective-permute-done.10.p3 = f32[32,4,128]{2,1,0:T(4,128)S(1)} collective-permute-done((f32[32,4,128]{2,1,0:T(4,128)S(1)}, f32[32,4,128]{2,1,0:T(4,128)S(1)}, u32[]{:S(2)}, u32[]{:S(2)}) %collective-permute-start.10) | collective-permute-done | bytes 65568 | tf_op jit(solution)/shard_map/ppermute | solution.py:378
  50.6 0.9 %join.1 = f32[32,4,448]{2,1,0:T(4,128)} custom-call(f32[32,4,128]{2,1,0:T(4,128)S(1)} %get-tuple-element.63.p0, f32[32,4,128]{2,1,0:T(4,128)S(1)} %collective-permute-done.8.p1, f32[32,4,128]{2,1,0:T(4,128)S(1)} %collective-permute-done.9.p2, f32[32,4,128]{2,1,0:T(4,128)S(1)} %collective-permute-done.10.p3), custom_call_target="tpu_custom_call" | custom-call | tf_op jit(solution)/shard_map/join/pallas_call | solution.py:367
Async XLA Ops:
  1.2 15.6 %collective-permute-start.1 = (bf16[4,16,128]{2,1,0:T(8,128)(2,1)S(1)}, bf16[4,16,128]{2,1,0:T(8,128)(2,1)S(1)}, u32[]{:S(2)}, u32[]{:S(2)}) collective-permute-start(bf16[4,16,128]{2,1,0:T(8,128)(2,1)S(1)} %get-tuple-element.38), channel_id=1, source_target_pairs={{0,129},{1,128},{2,131},{3,130},{4,133},{5,132},{6,135},{7,134},{8... | collective-permute-start | bytes 49160 | tf_op jit(solution)/shard_map/ppermute | solution.py:392
  3.8 15.5 %collective-permute-start = (bf16[3,16,128]{2,1,0:T(8,128)(2,1)S(1)}, bf16[3,16,128]{2,1,0:T(8,128)(2,1)S(1)}, u32[]{:S(2)}, u32[]{:S(2)}) collective-permute-start(bf16[3,16,128]{2,1,0:T(8,128)(2,1)S(1)} %get-tuple-element.37), channel_id=1, source_target_pairs={{1,2},{3,4},{5,6},{7,8},{9,10},{11,12},{13,14},{15,16},{17,18},{19... | collective-permute-start | bytes 36872 | tf_op jit(solution)/shard_map/ppermute | solution.py:382
  12.0 3.7 %collective-permute-start.2 = (bf16[16,128]{1,0:T(8,128)(2,1)S(1)}, bf16[16,128]{1,0:T(8,128)(2,1)S(1)}, u32[]{:S(2)}, u32[]{:S(2)}) collective-permute-start(bf16[16,128]{1,0:T(8,128)(2,1)S(1)} %get-tuple-element.39.refs_2_), channel_id=1, source_target_pairs={{0,64},{1,193},{2,66},{3,195},{4,68},{5,197},{6,70},{7,199},{8,72}... | collective-permute-start | bytes 12296 | tf_op jit(solution)/shard_map/ppermute | solution.py:392
  15.7 1.2 %collective-permute-start.3 = (bf16[16,128]{1,0:T(8,128)(2,1)S(1)}, bf16[16,128]{1,0:T(8,128)(2,1)S(1)}, u32[]{:S(2)}, u32[]{:S(2)}) collective-permute-start(bf16[16,128]{1,0:T(8,128)(2,1)S(1)} %collective-permute-done.2.refs_3_), channel_id=1, source_target_pairs={{0,1},{2,3},{4,5},{6,7},{8,9},{10,11},{12,13},{14,15},{16,17},{18,... | collective-permute-start | bytes 12296 | tf_op jit(solution)/shard_map/ppermute | solution.py:382
  21.8 3.1 %collective-permute-start.5 = (bf16[7,3,16,128]{3,2,1,0:T(8,128)(2,1)S(1)}, bf16[7,3,16,128]{3,2,1,0:T(8,128)(2,1)S(1)}, u32[]{:S(2)}, u32[]{:S(2)}) collective-permute-start(bf16[7,3,16,128]{3,2,1,0:T(8,128)(2,1)S(1)} %get-tuple-element.53), channel_id=1, source_target_pairs={{0,1},{2,3},{4,5},{6,7},{8,9},{10,11},{12,13},{14,15},{16,17},{18,... | collective-permute-start | bytes 258056 | tf_op jit(solution)/shard_map/ppermute | solution.py:382
  22.0 7.9 %collective-permute-start.4 = (bf16[7,3,16,128]{3,2,1,0:T(8,128)(2,1)S(1)}, bf16[7,3,16,128]{3,2,1,0:T(8,128)(2,1)S(1)}, u32[]{:S(2)}, u32[]{:S(2)}) collective-permute-start(bf16[7,3,16,128]{3,2,1,0:T(8,128)(2,1)S(1)} %get-tuple-element.51), channel_id=1, source_target_pairs={{1,2},{3,4},{5,6},{7,8},{9,10},{11,12},{13,14},{15,16},{17,18},{19... | collective-permute-start | bytes 258056 | tf_op jit(solution)/shard_map/ppermute | solution.py:382
  32.4 3.1 %collective-permute-start.7 = (bf16[6,3,16,128]{3,2,1,0:T(8,128)(2,1)S(1)}, bf16[6,3,16,128]{3,2,1,0:T(8,128)(2,1)S(1)}, u32[]{:S(2)}, u32[]{:S(2)}) collective-permute-start(bf16[6,3,16,128]{3,2,1,0:T(8,128)(2,1)S(1)} %get-tuple-element.59), channel_id=1, source_target_pairs={{0,1},{2,3},{4,5},{6,7},{8,9},{10,11},{12,13},{14,15},{16,17},{18,... | collective-permute-start | bytes 221192 | tf_op jit(solution)/shard_map/ppermute | solution.py:382
  32.5 7.8 %collective-permute-start.6 = (bf16[6,3,16,128]{3,2,1,0:T(8,128)(2,1)S(1)}, bf16[6,3,16,128]{3,2,1,0:T(8,128)(2,1)S(1)}, u32[]{:S(2)}, u32[]{:S(2)}) collective-permute-start(bf16[6,3,16,128]{3,2,1,0:T(8,128)(2,1)S(1)} %get-tuple-element.57), channel_id=1, source_target_pairs={{1,2},{3,4},{5,6},{7,8},{9,10},{11,12},{13,14},{15,16},{17,18},{19... | collective-permute-start | bytes 221192 | tf_op jit(solution)/shard_map/ppermute | solution.py:382
  42.4 4.8 %collective-permute-start.8 = (f32[32,4,128]{2,1,0:T(4,128)S(1)}, f32[32,4,128]{2,1,0:T(4,128)S(1)}, u32[]{:S(2)}, u32[]{:S(2)}) collective-permute-start(f32[32,4,128]{2,1,0:T(4,128)S(1)} %get-tuple-element.64), channel_id=1, source_target_pairs={{0,64},{64,0},{128,192},{192,128},{1,65},{65,1},{129,193},{193,129... | collective-permute-start | bytes 196616 | tf_op jit(solution)/shard_map/ppermute | solution.py:378
  43.1 5.8 %collective-permute-start.9 = (f32[32,4,128]{2,1,0:T(4,128)S(1)}, f32[32,4,128]{2,1,0:T(4,128)S(1)}, u32[]{:S(2)}, u32[]{:S(2)}) collective-permute-start(f32[32,4,128]{2,1,0:T(4,128)S(1)} %get-tuple-element.65), channel_id=1, source_target_pairs={{0,128},{64,192},{128,0},{192,64},{1,129},{65,193},{129,1},{193,65... | collective-permute-start | bytes 196616 | tf_op jit(solution)/shard_map/ppermute | solution.py:378
  45.1 5.5 %collective-permute-start.10 = (f32[32,4,128]{2,1,0:T(4,128)S(1)}, f32[32,4,128]{2,1,0:T(4,128)S(1)}, u32[]{:S(2)}, u32[]{:S(2)}) collective-permute-start(f32[32,4,128]{2,1,0:T(4,128)S(1)} %get-tuple-element.66), channel_id=1, source_target_pairs={{0,192},{64,128},{128,64},{192,0},{1,193},{65,129},{129,65},{193,1... | collective-permute-start | bytes 196616 | tf_op jit(solution)/shard_map/ppermute | solution.py:378

commit v8 on v6

--- a/solution.py
+++ b/solution.py
@@ -289,17 +289,17 @@
     units = len(r.groups)
     for g in range(units + 2):
         if g < units:
-            r.fill(g, list(range(6)))
+            r.fill(g, list(range(5)))
             r.hidden(g, 2, [(hid[g], 1), (hid[g], 2)])
             r.hidden(g, 1, [(hid[g], 0)])
         if 0 < g <= units:
             k = g - 1
+            r.second(k, 4, [(hid[k], 2, 1), (kept_h.at[k], 0, 2)], [(sec[k], 2)])
             r.second(k, 2, [(hid[k], 0, 3), (kept_h.at[k], 0, 1)], [(sec[k], 0), (sec[k], 1)])
-            r.second(k, 4, [(hid[k], 2, 1), (kept_h.at[k], 0, 2)], [(sec[k], 2)])
         if g > 1:
             k = g - 2
+            r.output(k, 2, 1, [(sec[k], 2, 1), (kept_s.at[k], 0, 2)], emit)
             r.output(k, 0, 2, [(sec[k], 0, 3), (kept_s.at[k], 0, 1)], emit)
-            r.output(k, 2, 1, [(sec[k], 2, 1), (kept_s.at[k], 0, 2)], emit)
 
     for t in range(rounds, TIMES):
         emit(t, 3, done[t + 1], done[0])
@@ -344,10 +344,10 @@
 
 
 def run_second(rounds, *args):
-    scratch = scratch_of(6, 3)
+    scratch = scratch_of(5, 3)
     if rounds == 2:
         out_shape = (jax.ShapeDtypeStruct((32, ROWS, L), F32),) * 4
-        scratch += [pltpu.VMEM((512, L), F32)]
+        scratch += [pltpu.VMEM((520, L), F32)]
     else:
         sent = jax.ShapeDtypeStruct((TIMES - 1 - rounds, 3, C, L), BF)
         out_shape = (jax.ShapeDtypeStruct((TIMES + 1, ROWS, C, L), F32), sent, sent)

time: 52.1 us -> 52 us (level)
  no operation moved by 1% of the time
where the time goes in v8:
time: 52 us; the launch traced here: 51.8 us
  starting transfers between devices  22.2 us (43%)
  Pallas kernels  17.1 us (33%)
  waiting for transfers between devices  12.4 us (24%)
    ppermute x6, starting transfers between devices, pair_up(): lax.ppermute(x, 'pix', [(a, b) for a, b in pairs] + [(b, a) for a, b in p...  14.2 us
    pallas_call x6, Pallas kernels, call(): pl.pallas_call(functools.partial(body, rounds), out_shape=out_shape, in_s...  13.8 us
    ppermute x6, waiting for transfers between devices, pair_up(): lax.ppermute(x, 'pix', [(a, b) for a, b in pairs] + [(b, a) for a, b in p...  6.02 us
    ppermute x3, starting transfers between devices, across(): return lax.ppermute(x, 'tm', [(t, t ^ k) for t in range(4)])  4.79 us
    ppermute x3, waiting for transfers between devices, across(): return lax.ppermute(x, 'tm', [(t, t ^ k) for t in range(4)])  3.38 us
    ppermute x2, starting transfers between devices, over_both(): return lax.ppermute(x, ('tm', 'pix'), pairs)  3.22 us
    ppermute x2, waiting for transfers between devices, over_both(): return lax.ppermute(x, ('tm', 'pix'), pairs)  3.02 us
    pallas_call x1, Pallas kernels, prepare(): pl.pallas_call(prepare_body, out_shape=tuple((jax.ShapeDtypeStruct(shape,...  1.24 us
  transfers between devices with their start and end apart: 11, of which 5 were waited for; matrix products, arithmetic and copies ran while one was open for 0% of the time, Pallas kernels for 15%

profile of v8, /device:TPU:24, one launch (start us, length us, event | category | flops | bytes accessed | tf_op | source)
XLA Modules:
  0.0 51.8 jit_solution(9732620786557034493)
XLA Ops:
  0.0 1.2 %enter.1 = (f32[4,16,128]{2,1,0:T(8,128)S(1)}, bf16[4,16,128]{2,1,0:T(8,128)(2,1)S(1)}, bf16[3,16,128]{2,1,0:T(8,128)(2,1)S(1)}, bf16[16,128]{1,0:T(8,128)(2,1)S(1)}) custom-call(f32[2]{0:T(128)} %step.1, f32[16,4,448]{2,1,0:T(4,128)} %latent.1, f32[2,128]{1,0:T(2,128)} %embed.1), custom_call_target="tpu_custom_call" | custom-call | tf_op jit(solution)/shard_map/enter/pallas_call | solution.py:64
  1.2 2.5 %collective-permute-start.1 = (bf16[4,16,128]{2,1,0:T(8,128)(2,1)S(1)}, bf16[4,16,128]{2,1,0:T(8,128)(2,1)S(1)}, u32[]{:S(2)}, u32[]{:S(2)}) collective-permute-start(bf16[4,16,128]{2,1,0:T(8,128)(2,1)S(1)} %get-tuple-element.35), channel_id=1, source_target_pairs={{0,129},{1,128},{2,131},{3,130},{4,133},{5,132},{6,135},{7,134},{8... | collective-permute-start | bytes 49160 | tf_op jit(solution)/shard_map/ppermute | solution.py:396
  3.8 8.2 %collective-permute-start = (bf16[3,16,128]{2,1,0:T(8,128)(2,1)S(1)}, bf16[3,16,128]{2,1,0:T(8,128)(2,1)S(1)}, u32[]{:S(2)}, u32[]{:S(2)}) collective-permute-start(bf16[3,16,128]{2,1,0:T(8,128)(2,1)S(1)} %get-tuple-element.34), channel_id=1, source_target_pairs={{1,2},{3,4},{5,6},{7,8},{9,10},{11,12},{13,14},{15,16},{17,18},{19... | collective-permute-start | bytes 36872 | tf_op jit(solution)/shard_map/ppermute | solution.py:386
  12.0 0.7 %collective-permute-start.2 = (bf16[16,128]{1,0:T(8,128)(2,1)S(1)}, bf16[16,128]{1,0:T(8,128)(2,1)S(1)}, u32[]{:S(2)}, u32[]{:S(2)}) collective-permute-start(bf16[16,128]{1,0:T(8,128)(2,1)S(1)} %get-tuple-element.36.refs_2_), channel_id=1, source_target_pairs={{0,64},{1,193},{2,66},{3,195},{4,68},{5,197},{6,70},{7,199},{8,72}... | collective-permute-start | bytes 12296 | tf_op jit(solution)/shard_map/ppermute | solution.py:396
  12.7 3.0 %collective-permute-done.2.refs_3_ = bf16[16,128]{1,0:T(8,128)(2,1)S(1)} collective-permute-done((bf16[16,128]{1,0:T(8,128)(2,1)S(1)}, bf16[16,128]{1,0:T(8,128)(2,1)S(1)}, u32[]{:S(2)}, u32[]{:S(2)}) %collective-permute-start.2) | collective-permute-done | bytes 4128 | tf_op jit(solution)/shard_map/ppermute | solution.py:396
  15.7 0.0 collective-permute-start.3
  15.7 1.2 %prepare.1 = (bf16[384,256]{1,0:T(8,128)(2,1)S(1)}, bf16[896,512]{1,0:T(8,128)(2,1)S(1)}, bf16[96,512]{1,0:T(8,128)(2,1)S(1)}) custom-call(bf16[3,3,16,128]{3,2,1,0:T(8,128)(2,1)} %bitcast.2, bf16[3,3,128,128]{3,2,1,0:T(8,128)(2,1)} %conv_mid.1, bf16[3,3,16,128]{3,2,1,0:T(8,128)(2,1)} %conv_out.1), custom_call_target="tpu_custom_call" | custom-call | tf_op jit(solution)/shard_map/prepare/pallas_call | solution.py:107
  16.9 0.0 collective-permute-done.3.refs_4_
  16.9 0.0 collective-permute-done.1.refs_1_
  17.0 2.4 %shard_map.64 = (bf16[4,256,256]{2,1,0:T(8,128)(2,1)S(1)}, bf16[4,256,256]{2,1,0:T(8,128)(2,1)S(1)}, f32[9,16,128]{2,1,0:T(8,128)S(1)}, bf16[384,256]{1,0:T(8,128)(2,1)S(1)}, f32[8,128]{1,0:T(8,128)S(1)}) custom-call(f32[4,16,128]{2,1,0:T(8,128)S(1)} %get-tuple-element.33.refs_0_, bf16[4,16,128]{2,1,0:T(8,128)(2,1)S(1)} %collective-permute-done.1.refs_1_, ...), custom_call_target="tpu_custom_call" | custom-call | tf_op jit(solution)/shard_map/pallas_call | solution.py:318
  19.4 0.0 collective-permute-done.refs_1_
  19.4 2.4 %shard_map.65 = (f32[9,4,16,128]{3,2,1,0:T(8,128)S(1)}, bf16[7,3,16,128]{3,2,1,0:T(8,128)(2,1)S(1)}, bf16[7,3,16,128]{3,2,1,0:T(8,128)(2,1)S(1)}) custom-call(f32[4,16,128]{2,1,0:T(8,128)S(1)} %get-tuple-element.33.refs_0_, bf16[3,16,128]{2,1,0:T(8,128)(2,1)S(1)} %collective-permute-done.refs_1_, bf16[4,256,256]{2,1,0:T(8,128)(2,1)S(1)} %get-tuple-element.40.refs_2_, ...), custom_call_target="tpu_custom_call" | custom-call | tf_op jit(solution)/shard_map/pallas_call | solution.py:318
  21.8 0.6 %collective-permute-start.5 = (bf16[7,3,16,128]{3,2,1,0:T(8,128)(2,1)S(1)}, bf16[7,3,16,128]{3,2,1,0:T(8,128)(2,1)S(1)}, u32[]{:S(2)}, u32[]{:S(2)}) collective-permute-start(bf16[7,3,16,128]{3,2,1,0:T(8,128)(2,1)S(1)} %get-tuple-element.47), channel_id=1, source_target_pairs={{0,1},{2,3},{4,5},{6,7},{8,9},{10,11},{12,13},{14,15},{16,17},{18,... | collective-permute-start | bytes 258056 | tf_op jit(solution)/shard_map/ppermute | solution.py:386
  22.4 2.5 %collective-permute-start.4 = (bf16[7,3,16,128]{3,2,1,0:T(8,128)(2,1)S(1)}, bf16[7,3,16,128]{3,2,1,0:T(8,128)(2,1)S(1)}, u32[]{:S(2)}, u32[]{:S(2)}) collective-permute-start(bf16[7,3,16,128]{3,2,1,0:T(8,128)(2,1)S(1)} %get-tuple-element.45), channel_id=1, source_target_pairs={{1,2},{3,4},{5,6},{7,8},{9,10},{11,12},{13,14},{15,16},{17,18},{19... | collective-permute-start | bytes 258056 | tf_op jit(solution)/shard_map/ppermute | solution.py:386
  24.9 0.0 collective-permute-done.5.refs_1_
  25.0 2.4 %shard_map.66 = (bf16[4,256,256]{2,1,0:T(8,128)(2,1)S(1)}, bf16[4,256,256]{2,1,0:T(8,128)(2,1)S(1)}, f32[9,16,128]{2,1,0:T(8,128)S(1)}) custom-call(f32[4,16,128]{2,1,0:T(8,128)S(1)} %get-tuple-element.33.refs_0_, bf16[7,3,16,128]{3,2,1,0:T(8,128)(2,1)S(1)} %collective-permute-done.5.refs_1_, f32[9,4,16,128]{3,2,1,0:T(8,128)S(1)} %get-tuple-element.46.refs_2_, ...), custom_call_target="tpu_custom_call" | custom-call | tf_op jit(solution)/shard_map/pallas_call | solution.py:318
  27.4 2.9 %collective-permute-done.4.refs_1_ = bf16[7,3,16,128]{3,2,1,0:T(8,128)(2,1)S(1)} collective-permute-done((bf16[7,3,16,128]{3,2,1,0:T(8,128)(2,1)S(1)}, bf16[7,3,16,128]{3,2,1,0:T(8,128)(2,1)S(1)}, u32[]{:S(2)}, u32[]{:S(2)}) %collective-permute-start.4) | collective-permute-done | bytes 86048 | tf_op jit(solution)/shard_map/ppermute | solution.py:386
  30.3 2.5 %shard_map.67 = (f32[9,4,16,128]{3,2,1,0:T(8,128)S(1)}, bf16[6,3,16,128]{3,2,1,0:T(8,128)(2,1)S(1)}, bf16[6,3,16,128]{3,2,1,0:T(8,128)(2,1)S(1)}) custom-call(f32[4,16,128]{2,1,0:T(8,128)S(1)} %get-tuple-element.33.refs_0_, bf16[7,3,16,128]{3,2,1,0:T(8,128)(2,1)S(1)} %collective-permute-done.4.refs_1_, f32[9,4,16,128]{3,2,1,0:T(8,128)S(1)} %get-tuple-element.46.refs_2_, ...), custom_call_target="tpu_custom_call" | custom-call | tf_op jit(solution)/shard_map/pallas_call | solution.py:318
  32.8 0.1 collective-permute-start.7
  32.9 2.7 %collective-permute-start.6 = (bf16[6,3,16,128]{3,2,1,0:T(8,128)(2,1)S(1)}, bf16[6,3,16,128]{3,2,1,0:T(8,128)(2,1)S(1)}, u32[]{:S(2)}, u32[]{:S(2)}) collective-permute-start(bf16[6,3,16,128]{3,2,1,0:T(8,128)(2,1)S(1)} %get-tuple-element.51), channel_id=1, source_target_pairs={{1,2},{3,4},{5,6},{7,8},{9,10},{11,12},{13,14},{15,16},{17,18},{19... | collective-permute-start | bytes 221192 | tf_op jit(solution)/shard_map/ppermute | solution.py:386
  35.6 0.0 collective-permute-done.7.refs_1_
  35.7 1.9 %shard_map.68 = (bf16[3,256,256]{2,1,0:T(8,128)(2,1)S(1)}, bf16[3,256,256]{2,1,0:T(8,128)(2,1)S(1)}, f32[9,16,128]{2,1,0:T(8,128)S(1)}) custom-call(f32[4,16,128]{2,1,0:T(8,128)S(1)} %get-tuple-element.33.refs_0_, bf16[6,3,16,128]{3,2,1,0:T(8,128)(2,1)S(1)} %collective-permute-done.7.refs_1_, f32[9,4,16,128]{3,2,1,0:T(8,128)S(1)} %get-tuple-element.52.refs_2_, ...), custom_call_target="tpu_custom_call" | custom-call | tf_op jit(solution)/shard_map/pallas_call | solution.py:318
  37.6 3.1 %collective-permute-done.6.refs_1_ = bf16[6,3,16,128]{3,2,1,0:T(8,128)(2,1)S(1)} collective-permute-done((bf16[6,3,16,128]{3,2,1,0:T(8,128)(2,1)S(1)}, bf16[6,3,16,128]{3,2,1,0:T(8,128)(2,1)S(1)}, u32[]{:S(2)}, u32[]{:S(2)}) %collective-permute-start.6) | collective-permute-done | bytes 73760 | tf_op jit(solution)/shard_map/ppermute | solution.py:386
  40.7 2.1 %shard_map.69 = (f32[32,4,128]{2,1,0:T(4,128)S(1)}, f32[32,4,128]{2,1,0:T(4,128)S(1)}, f32[32,4,128]{2,1,0:T(4,128)S(1)}, f32[32,4,128]{2,1,0:T(4,128)S(1)}) custom-call(f32[4,16,128]{2,1,0:T(8,128)S(1)} %get-tuple-element.33.refs_0_, bf16[6,3,16,128]{3,2,1,0:T(8,128)(2,1)S(1)} %collective-permute-done.6.refs_1_, ...), custom_call_target="tpu_custom_call" | custom-call | tf_op jit(solution)/shard_map/pallas_call | solution.py:318
  42.8 0.7 %collective-permute-start.8 = (f32[32,4,128]{2,1,0:T(4,128)S(1)}, f32[32,4,128]{2,1,0:T(4,128)S(1)}, u32[]{:S(2)}, u32[]{:S(2)}) collective-permute-start(f32[32,4,128]{2,1,0:T(4,128)S(1)} %get-tuple-element.58), channel_id=1, source_target_pairs={{0,64},{64,0},{128,192},{192,128},{1,65},{65,1},{129,193},{193,129... | collective-permute-start | bytes 196616 | tf_op jit(solution)/shard_map/ppermute | solution.py:382
  43.4 2.0 %collective-permute-start.9 = (f32[32,4,128]{2,1,0:T(4,128)S(1)}, f32[32,4,128]{2,1,0:T(4,128)S(1)}, u32[]{:S(2)}, u32[]{:S(2)}) collective-permute-start(f32[32,4,128]{2,1,0:T(4,128)S(1)} %get-tuple-element.59), channel_id=1, source_target_pairs={{0,128},{64,192},{128,0},{192,64},{1,129},{65,193},{129,1},{193,65... | collective-permute-start | bytes 196616 | tf_op jit(solution)/shard_map/ppermute | solution.py:382
  45.4 2.1 %collective-permute-start.10 = (f32[32,4,128]{2,1,0:T(4,128)S(1)}, f32[32,4,128]{2,1,0:T(4,128)S(1)}, u32[]{:S(2)}, u32[]{:S(2)}) collective-permute-start(f32[32,4,128]{2,1,0:T(4,128)S(1)} %get-tuple-element.60), channel_id=1, source_target_pairs={{0,192},{64,128},{128,64},{192,0},{1,193},{65,129},{129,65},{193,1... | collective-permute-start | bytes 196616 | tf_op jit(solution)/shard_map/ppermute | solution.py:382
  47.5 0.0 collective-permute-done.8.p1
  47.5 1.7 %collective-permute-done.9.p2 = f32[32,4,128]{2,1,0:T(4,128)S(1)} collective-permute-done((f32[32,4,128]{2,1,0:T(4,128)S(1)}, f32[32,4,128]{2,1,0:T(4,128)S(1)}, u32[]{:S(2)}, u32[]{:S(2)}) %collective-permute-start.9) | collective-permute-done | bytes 65568 | tf_op jit(solution)/shard_map/ppermute | solution.py:382
  49.2 1.7 %collective-permute-done.10.p3 = f32[32,4,128]{2,1,0:T(4,128)S(1)} collective-permute-done((f32[32,4,128]{2,1,0:T(4,128)S(1)}, f32[32,4,128]{2,1,0:T(4,128)S(1)}, u32[]{:S(2)}, u32[]{:S(2)}) %collective-permute-start.10) | collective-permute-done | bytes 65568 | tf_op jit(solution)/shard_map/ppermute | solution.py:382
  50.9 0.9 %join.1 = f32[32,4,448]{2,1,0:T(4,128)} custom-call(f32[32,4,128]{2,1,0:T(4,128)S(1)} %get-tuple-element.57.p0, f32[32,4,128]{2,1,0:T(4,128)S(1)} %collective-permute-done.8.p1, f32[32,4,128]{2,1,0:T(4,128)S(1)} %collective-permute-done.9.p2, f32[32,4,128]{2,1,0:T(4,128)S(1)} %collective-permute-done.10.p3), custom_call_target="tpu_custom_call" | custom-call | tf_op jit(solution)/shard_map/join/pallas_call | solution.py:371
Async XLA Ops:
  1.2 15.7 %collective-permute-start.1 = (bf16[4,16,128]{2,1,0:T(8,128)(2,1)S(1)}, bf16[4,16,128]{2,1,0:T(8,128)(2,1)S(1)}, u32[]{:S(2)}, u32[]{:S(2)}) collective-permute-start(bf16[4,16,128]{2,1,0:T(8,128)(2,1)S(1)} %get-tuple-element.35), channel_id=1, source_target_pairs={{0,129},{1,128},{2,131},{3,130},{4,133},{5,132},{6,135},{7,134},{8... | collective-permute-start | bytes 49160 | tf_op jit(solution)/shard_map/ppermute | solution.py:396
  3.8 15.6 %collective-permute-start = (bf16[3,16,128]{2,1,0:T(8,128)(2,1)S(1)}, bf16[3,16,128]{2,1,0:T(8,128)(2,1)S(1)}, u32[]{:S(2)}, u32[]{:S(2)}) collective-permute-start(bf16[3,16,128]{2,1,0:T(8,128)(2,1)S(1)} %get-tuple-element.34), channel_id=1, source_target_pairs={{1,2},{3,4},{5,6},{7,8},{9,10},{11,12},{13,14},{15,16},{17,18},{19... | collective-permute-start | bytes 36872 | tf_op jit(solution)/shard_map/ppermute | solution.py:386
  12.0 3.7 %collective-permute-start.2 = (bf16[16,128]{1,0:T(8,128)(2,1)S(1)}, bf16[16,128]{1,0:T(8,128)(2,1)S(1)}, u32[]{:S(2)}, u32[]{:S(2)}) collective-permute-start(bf16[16,128]{1,0:T(8,128)(2,1)S(1)} %get-tuple-element.36.refs_2_), channel_id=1, source_target_pairs={{0,64},{1,193},{2,66},{3,195},{4,68},{5,197},{6,70},{7,199},{8,72}... | collective-permute-start | bytes 12296 | tf_op jit(solution)/shard_map/ppermute | solution.py:396
  15.7 1.3 %collective-permute-start.3 = (bf16[16,128]{1,0:T(8,128)(2,1)S(1)}, bf16[16,128]{1,0:T(8,128)(2,1)S(1)}, u32[]{:S(2)}, u32[]{:S(2)}) collective-permute-start(bf16[16,128]{1,0:T(8,128)(2,1)S(1)} %collective-permute-done.2.refs_3_), channel_id=1, source_target_pairs={{0,1},{2,3},{4,5},{6,7},{8,9},{10,11},{12,13},{14,15},{16,17},{18,... | collective-permute-start | bytes 12296 | tf_op jit(solution)/shard_map/ppermute | solution.py:386
  21.8 3.1 %collective-permute-start.5 = (bf16[7,3,16,128]{3,2,1,0:T(8,128)(2,1)S(1)}, bf16[7,3,16,128]{3,2,1,0:T(8,128)(2,1)S(1)}, u32[]{:S(2)}, u32[]{:S(2)}) collective-permute-start(bf16[7,3,16,128]{3,2,1,0:T(8,128)(2,1)S(1)} %get-tuple-element.47), channel_id=1, source_target_pairs={{0,1},{2,3},{4,5},{6,7},{8,9},{10,11},{12,13},{14,15},{16,17},{18,... | collective-permute-start | bytes 258056 | tf_op jit(solution)/shard_map/ppermute | solution.py:386
  22.4 7.9 %collective-permute-start.4 = (bf16[7,3,16,128]{3,2,1,0:T(8,128)(2,1)S(1)}, bf16[7,3,16,128]{3,2,1,0:T(8,128)(2,1)S(1)}, u32[]{:S(2)}, u32[]{:S(2)}) collective-permute-start(bf16[7,3,16,128]{3,2,1,0:T(8,128)(2,1)S(1)} %get-tuple-element.45), channel_id=1, source_target_pairs={{1,2},{3,4},{5,6},{7,8},{9,10},{11,12},{13,14},{15,16},{17,18},{19... | collective-permute-start | bytes 258056 | tf_op jit(solution)/shard_map/ppermute | solution.py:386
  32.8 2.8 %collective-permute-start.7 = (bf16[6,3,16,128]{3,2,1,0:T(8,128)(2,1)S(1)}, bf16[6,3,16,128]{3,2,1,0:T(8,128)(2,1)S(1)}, u32[]{:S(2)}, u32[]{:S(2)}) collective-permute-start(bf16[6,3,16,128]{3,2,1,0:T(8,128)(2,1)S(1)} %get-tuple-element.53), channel_id=1, source_target_pairs={{0,1},{2,3},{4,5},{6,7},{8,9},{10,11},{12,13},{14,15},{16,17},{18,... | collective-permute-start | bytes 221192 | tf_op jit(solution)/shard_map/ppermute | solution.py:386
  32.9 7.8 %collective-permute-start.6 = (bf16[6,3,16,128]{3,2,1,0:T(8,128)(2,1)S(1)}, bf16[6,3,16,128]{3,2,1,0:T(8,128)(2,1)S(1)}, u32[]{:S(2)}, u32[]{:S(2)}) collective-permute-start(bf16[6,3,16,128]{3,2,1,0:T(8,128)(2,1)S(1)} %get-tuple-element.51), channel_id=1, source_target_pairs={{1,2},{3,4},{5,6},{7,8},{9,10},{11,12},{13,14},{15,16},{17,18},{19... | collective-permute-start | bytes 221192 | tf_op jit(solution)/shard_map/ppermute | solution.py:386
  42.8 4.8 %collective-permute-start.8 = (f32[32,4,128]{2,1,0:T(4,128)S(1)}, f32[32,4,128]{2,1,0:T(4,128)S(1)}, u32[]{:S(2)}, u32[]{:S(2)}) collective-permute-start(f32[32,4,128]{2,1,0:T(4,128)S(1)} %get-tuple-element.58), channel_id=1, source_target_pairs={{0,64},{64,0},{128,192},{192,128},{1,65},{65,1},{129,193},{193,129... | collective-permute-start | bytes 196616 | tf_op jit(solution)/shard_map/ppermute | solution.py:382
  43.4 5.8 %collective-permute-start.9 = (f32[32,4,128]{2,1,0:T(4,128)S(1)}, f32[32,4,128]{2,1,0:T(4,128)S(1)}, u32[]{:S(2)}, u32[]{:S(2)}) collective-permute-start(f32[32,4,128]{2,1,0:T(4,128)S(1)} %get-tuple-element.59), channel_id=1, source_target_pairs={{0,128},{64,192},{128,0},{192,64},{1,129},{65,193},{129,1},{193,65... | collective-permute-start | bytes 196616 | tf_op jit(solution)/shard_map/ppermute | solution.py:382
  45.4 5.5 %collective-permute-start.10 = (f32[32,4,128]{2,1,0:T(4,128)S(1)}, f32[32,4,128]{2,1,0:T(4,128)S(1)}, u32[]{:S(2)}, u32[]{:S(2)}) collective-permute-start(f32[32,4,128]{2,1,0:T(4,128)S(1)} %get-tuple-element.60), channel_id=1, source_target_pairs={{0,192},{64,128},{128,64},{192,0},{1,193},{65,129},{129,65},{193,1... | collective-permute-start | bytes 196616 | tf_op jit(solution)/shard_map/ppermute | solution.py:382
